TPU v7x, 128 devices: a whole 4x4x4 slice. The times are simulated.
128 devices in a mesh: site: 8 (over x, z_lo), bond: 16 (over z_hi, y, core).
Axes of the slice: x: 4, y: 4, z: 4 (z_hi: 2, z_lo: 2; z = z_hi * 2 + z_lo), core: 2. Of those that a mesh axis runs over, the one named last changes fastest.
Arguments:
- sites: bfloat16 [16, 1024, 2048], P('site', 'bond'), may hold values from -0.1875 to 0.1875
- proj_left: bfloat16 [8, 1024, 2048], P('site', 'bond'), may hold values from -4.1875 to 4.1875
- proj_right: bfloat16 [8, 1024, 2048], P('site', 'bond'), may hold values from -4.1875 to 4.1875
- edge_right: bfloat16 [1024, 2048], P('bond'), may hold values from -4.1875 to 4.1875
- bulk_first: bfloat16 [1024, 2048], P('bond'), may hold values from -0.1875 to 0.1875
- bulk_second: bfloat16 [1024, 2048], P('bond'), may hold values from -0.1875 to 0.1875
- bulk_left_proj: bfloat16 [1024, 2048], P('bond'), may hold values from -4.1875 to 4.1875
- bulk_right_proj: bfloat16 [1024, 2048], P('bond'), may hold values from -4.1875 to 4.1875
- gate: float32 [4, 4], replicated, may hold values from -3 to 3
- gate_mask: int32 [8], P('site'), may hold values 0 or 1
- bond_dims: int32 [8], P('site'), may hold values from 512 to 1024
Outputs:
- new_sites: bfloat16 [16, 1024, 2048], P('site', 'bond')
- new_bulk_first: bfloat16 [1024, 2048], P('bond')
- new_bulk_second: bfloat16 [1024, 2048], P('bond')
All inputs are finite; a program needn't handle non-finite values. No bound on the sum of `gate_mask` on one device may be relied on, other than what follows from the above.
Results may differ from a plain program's by a relative error of at most 0.0049.
Values may be sent and summed in bfloat16 or wider, within the bound.
No kernel may reach another device: no remote copies, remote signals or barrier semaphores. Data moves between devices by JAX's collectives and lax.ppermute only.
A program may use at most 128 MiB of HBM per device.

v0:
```python
import jax
import jax.numpy as jnp
from jax import lax
from jax.experimental import pallas as pl
from jax.experimental.pallas import tpu as pltpu
from jax.sharding import Mesh
from jax.sharding import PartitionSpec as P


SITE = ("x", "zl")
BOND = ("zh", "y", "c")
VMEM_BYTES = 60 * 1024 * 1024
F32 = jnp.float32
BF16 = jnp.bfloat16


def dot(a, b, dims):
    return lax.dot_general(a, b, (dims, ((), ())), preferred_element_type=F32)


def split_kernel(meta, site, edge, proj, bulk, bulk_proj, bulk_left, out_ref, bulk_ref):
    first, g = meta[3], meta[4]
    quarter, width = 256, 1024
    column = lax.broadcasted_iota(jnp.int32, (width, 128), 1)
    source = (column // 8) * 64 + g * 8 + column % 8
    chosen = jnp.where(lax.broadcasted_iota(jnp.int32, (width, 128), 0) == source, 1.0, 0.0)
    chosen = chosen.astype(BF16)
    for s in range(2):
        part = dot(bulk_left[:, s * width : (s + 1) * width], chosen, ((1,), (0,))).astype(BF16)
        for q in range(4):
            bulk_ref[q, :, width + s * 128 : width + (s + 1) * 128] = part
    for q in range(4):
        for t in range(2):
            cols = slice(t * width + q * quarter, t * width + (q + 1) * quarter)
            low = slice(t * quarter, (t + 1) * quarter)
            high = slice((2 + t) * quarter, (3 + t) * quarter)
            out_ref[q, :, low] = site[0, :, cols]
            bulk_ref[q, :, low] = bulk[:, cols]
            out_ref[q, :, high] = jnp.where(first == 1, edge[:, cols], proj[0, :, cols])
            bulk_ref[q, :, high] = bulk_proj[:, cols]


def split(meta, sites, edge, proj, bulk, bulk_proj, bulk_left):
    smem = pl.BlockSpec(memory_space=pltpu.SMEM)
    one = pl.BlockSpec((1, 64, 2048), lambda i: (0, 0, 0))
    flat = pl.BlockSpec((64, 2048), lambda i: (0, 0))
    return pl.pallas_call(
        split_kernel,
        grid=(1,),
        out_shape=(
            jax.ShapeDtypeStruct((4, 64, 1024), BF16),
            jax.ShapeDtypeStruct((4, 64, 1280), BF16),
        ),
        in_specs=[smem, one, flat, one, flat, flat, flat],
        out_specs=(
            pl.BlockSpec((4, 64, 1024), lambda i: (0, 0, 0)),
            pl.BlockSpec((4, 64, 1280), lambda i: (0, 0, 0)),
        ),
        cost_estimate=pl.CostEstimate(
            flops=40_000_000, bytes_accessed=3_000_000, transcendentals=0
        ),
        name="split",
    )(meta, sites, edge, proj, bulk, bulk_proj, bulk_left)


def theta(h, base, x_of, y_part, raw, out):
    for s0 in range(2):
        raw[s0] = dot(x_of(s0), y_part, ((1,), (0,)))
    step, half = 32, 256

    def chunk(i, _):
        r = pl.ds(pl.multiple_of(i * step, step), step)
        parts = [raw[k // 2, r, (k % 2) * half : (k % 2 + 1) * half] for k in range(4)]
        for s in range(2):
            for t in range(2):
                row = base + 4 * (2 * s + t)
                val = h[row] * parts[0]
                for k in range(1, 4):
                    val = val + h[row + k] * parts[k]
                out[s, r, t * half : (t + 1) * half] = val.astype(out.dtype)
        return 0

    lax.fori_loop(0, 256 // step, chunk, 0)


def row_copies(parts, cols, ys, zh, c, sem):
    copies = []
    for n, part in enumerate(parts):
        z_of = lax.rem(zh + n % 2, 2)
        c_of = lax.rem(c + n // 2, 2)
        for y in range(4):
            at = pl.multiple_of((z_of * 8 + y * 2 + c_of) * 64, 64)
            copies.append(
                pltpu.make_async_copy(
                    part.at[y, :, 0:cols], ys.at[pl.ds(at, 64), :], sem.at[n * 4 + y]
                )
            )
    return copies


def bulk_kernel(
    meta, h, own, prev, after, far_low, far_high, b0, b1, b2, b3,
    left_ref, keep_ref, send_ref, xs, ys, ls, raw, th, tmp, sem, sem_y,
):
    c, zh, me, g = meta[0], meta[1], meta[2], meta[4]
    ny, block, width, cols = 4, 64, 1024, 512
    owner = [lax.rem(me + d, ny) for d in (0, 3, 1, 2)]
    rows = [pl.ds(pl.multiple_of(o * block, block), block) for o in owner]
    copies = row_copies((b0, b1, b2, b3), 2 * cols, ys, zh, c, sem_y)
    for n, part in enumerate((own, prev, after)):
        copies.append(pltpu.make_async_copy(part, xs.at[rows[n], :], sem.at[n]))
    copies.append(pltpu.make_async_copy(far_low, xs.at[rows[3], 0:width], sem.at[3]))
    copies.append(pltpu.make_async_copy(far_high, xs.at[rows[3], width : 2 * width], sem.at[4]))
    copies.append(pltpu.make_async_copy(b0.at[:, :, width : width + 256], ls, sem.at[5]))
    for copy in copies:
        copy.start()
    for copy in copies:
        copy.wait()

    theta(h, 32, lambda s: xs[:, s * width : (s + 1) * width], ys[:, 0:cols], raw, th)
    picked = [
        th[s, pl.ds(pl.multiple_of(y * block + g * 8, 8), 8), :] for s in range(2) for y in range(ny)
    ]
    picked = jnp.concatenate(picked, axis=0).astype(BF16)
    for n in range(4):
        part = dot(picked, ys[n * 256 : (n + 1) * 256, cols : 2 * cols], ((1,), (1,)))
        for s in range(2):
            to = (2 * s + n // 2) * 8
            for y in range(ny):
                left_ref[y, to : to + 8, (n % 2) * 256 : (n % 2 + 1) * 256] = part[
                    s * 32 + y * 8 : s * 32 + (y + 1) * 8
                ]
    part = None
    for s in range(2):
        l_part = ls[:, :, s * 128 : (s + 1) * 128].reshape(ny * block, 128)
        one = dot(l_part, th[s].astype(BF16), ((0,), (0,)))
        part = one if s == 0 else part + one
    tmp[...] = part
    for at in range(2 * ny):
        z_of = lax.rem(at // ny + zh, 2)
        mine = pl.multiple_of(at * 16 + c * 8, 8)
        other = pl.multiple_of(at * 16 + (1 - c) * 8, 8)
        keep_ref[z_of, at % ny] = tmp[pl.ds(mine, 8), :]
        send_ref[z_of, at % ny] = tmp[pl.ds(other, 8), :]


def window_kernel(
    meta, h, a_own, a_prev, a_after, x_far, l_far, p0, p1, p2, p3, own, prev, after, far_low, far_high, b0, b1, b2, b3,
    left_ref, keep_ref, send_ref,
    xs, ls, xb, ys, yb, raw, th, tmp, sem, sem_y, sem_b,
):
    c, zh, me, first = meta[0], meta[1], meta[2], meta[3]
    ny, block, width, cols = 4, 64, 1024, 512
    owner = [lax.rem(me + d, ny) for d in (0, 3, 1, 2)]
    rows = [pl.ds(pl.multiple_of(o * block, block), block) for o in owner]
    main = row_copies((p0, p1, p2, p3), 2 * cols, ys, zh, c, sem_y)
    for n, part in enumerate((a_own.at[0], a_prev.at[0], a_after.at[0], x_far)):
        main.append(pltpu.make_async_copy(part, xs.at[rows[n], :], sem.at[n]))
    for n, part in enumerate((own, prev, after)):
        main.append(pltpu.make_async_copy(part, xb.at[rows[n], :], sem.at[4 + n]))
    main.append(pltpu.make_async_copy(far_low, xb.at[rows[3], 0:width], sem.at[7]))
    main.append(pltpu.make_async_copy(far_high, xb.at[rows[3], width : 2 * width], sem.at[8]))
    main += row_copies((b0, b1, b2, b3), cols, yb, zh, c, sem_b)
    later = [
        pltpu.make_async_copy(part, ls.at[rows[n], :], sem.at[10 + n])
        for n, part in enumerate((a_own.at[1], a_prev.at[1], a_after.at[1], l_far))
    ]
    for copy in main + later:
        copy.start()
    for copy in main:
        copy.wait()

    @pl.when(first == 1)
    def _():
        theta(h, 0, lambda s: xs[:, s * width : (s + 1) * width], yb[...], raw, th)

    @pl.when(first == 0)
    def _():
        theta(h, 0, lambda s: xs[:, s * width : (s + 1) * width], ys[:, 0:cols], raw, th)

    def left_chunk(n, _):
        k_at = pl.multiple_of(n * 256, 256)
        r_part = ys[pl.ds(k_at, 256), cols : 2 * cols]
        for s in range(2):
            part = dot(th[s], r_part, ((1,), (1,))).astype(BF16)
            lanes = pl.ds(pl.multiple_of(s * width + n * 256, 256), 256)
            for y in range(ny):
                left_ref[y, :, lanes] = part[y * block : (y + 1) * block]
        return 0

    lax.fori_loop(0, 4, left_chunk, 0)

    @pl.when(first == 1)
    def _():
        theta(h, 16, lambda s: xb[:, s * width : (s + 1) * width], ys[:, 0:cols], raw, th)

    for copy in later:
        copy.wait()

    def right_chunk(n, _):
        part = None
        for s in range(2):
            l_part = ls[:, pl.ds(pl.multiple_of(s * width + n * 256, 256), 256)]
            one = dot(l_part, th[s], ((0,), (0,)))
            part = one if s == 0 else part + one
        tmp[...] = part
        for j in range(2):
            at = 2 * n + j
            z_of = lax.rem(lax.div(at, ny) + zh, 2)
            y_of = lax.rem(at, ny)
            mine = pl.multiple_of(j * 128 + c * block, block)
            other = pl.multiple_of(j * 128 + (1 - c) * block, block)
            keep_ref[z_of, y_of] = tmp[pl.ds(mine, block), :]
            send_ref[z_of, y_of] = tmp[pl.ds(other, block), :]
        return 0

    lax.fori_loop(0, 4, right_chunk, 0)


def call(kernel, outs, scratch, flops, meta, h, *arrays):
    smem = pl.BlockSpec(memory_space=pltpu.SMEM)
    vmem = pl.BlockSpec(memory_space=pltpu.VMEM)
    anywhere = pl.BlockSpec(memory_space=pltpu.HBM)
    return pl.pallas_call(
        kernel,
        out_shape=outs,
        in_specs=[smem, smem] + [anywhere] * len(arrays),
        out_specs=(vmem,) * len(outs),
        scratch_shapes=scratch,
        compiler_params=pltpu.CompilerParams(vmem_limit_bytes=VMEM_BYTES),
        cost_estimate=pl.CostEstimate(
            flops=flops, bytes_accessed=10_000_000, transcendentals=0
        ),
    )(meta, h, *arrays)


def ends_kernel(got, out):
    low = got[:, 8:40, :].astype(F32)
    low = (low[0] + low[1] + low[2] + low[3]).astype(BF16)
    left = jnp.concatenate([low[8 * k : 8 * (k + 1)] for k in range(4)], axis=1)
    right = [got[k, 0:8, t * 256 : (t + 1) * 256] for t in range(2) for k in range(4)]
    ends = jnp.concatenate([left, jnp.concatenate(right, axis=1)], axis=0)
    for g in range(8):
        out[g] = ends


def bulk_ends(got):
    return pl.pallas_call(
        ends_kernel,
        out_shape=jax.ShapeDtypeStruct((8, 16, 2048), BF16),
        cost_estimate=pl.CostEstimate(flops=1_000_000, bytes_accessed=700_000, transcendentals=0),
        name="finish",
    )(got)


def bulk_bond(meta, h, *arrays):
    sums = jax.ShapeDtypeStruct((2, 4, 8, 512), F32)
    return call(
        bulk_kernel,
        (jax.ShapeDtypeStruct((4, 32, 512), F32), sums, sums),
        [
            pltpu.VMEM((256, 2048), BF16),
            pltpu.VMEM((1024, 1024), BF16),
            pltpu.VMEM((4, 64, 256), BF16),
            pltpu.VMEM((2, 256, 512), F32),
            pltpu.VMEM((2, 256, 512), F32),
            pltpu.VMEM((128, 512), F32),
            pltpu.SemaphoreType.DMA((6,)),
            pltpu.SemaphoreType.DMA((16,)),
        ],
        1_000_000_000,
        meta,
        h,
        *arrays,
    )


def window_bonds(meta, h, *arrays):
    sums = jax.ShapeDtypeStruct((2, 4, 64, 512), F32)
    return call(
        window_kernel,
        (jax.ShapeDtypeStruct((4, 64, 2048), BF16), sums, sums),
        [
            pltpu.VMEM((256, 2048), BF16),
            pltpu.VMEM((256, 2048), BF16),
            pltpu.VMEM((256, 2048), BF16),
            pltpu.VMEM((1024, 1024), BF16),
            pltpu.VMEM((1024, 512), BF16),
            pltpu.VMEM((2, 256, 512), F32),
            pltpu.VMEM((2, 256, 512), BF16),
            pltpu.VMEM((256, 512), F32),
            pltpu.SemaphoreType.DMA((14,)),
            pltpu.SemaphoreType.DMA((16,)),
            pltpu.SemaphoreType.DMA((16,)),
        ],
        3_000_000_000,
        meta,
        h,
        *arrays,
    )


def half_step(
    sites,
    proj_left,
    proj_right,
    edge_right,
    bulk_first,
    bulk_second,
    bulk_left_proj,
    bulk_right_proj,
    gate,
    gate_mask,
    bond_dims,
):
    block = sites.shape[1]
    width = sites.shape[2] // 2
    groups = lax.axis_size(SITE)
    ny = lax.axis_size("y")
    quarter = width // ny
    here = lax.axis_index(SITE)
    zh, y, c = (lax.axis_index(name) for name in BOND)
    first_group = here == 0
    identity = jnp.eye(4, dtype=F32)
    weight = gate_mask[0].astype(F32)
    mixer = weight * gate + (1.0 - weight) * identity
    mixer_left = jnp.where(first_group, gate, mixer)
    positions = jnp.arange(width, dtype=jnp.int32)
    keep = (positions < bond_dims[0]).astype(F32)
    keep_left = jnp.where(first_group, 1.0, keep)
    around = [(g, (g + 1) % groups) for g in range(groups)]

    meta = jnp.stack([c, zh, y, first_group.astype(jnp.int32), here]).astype(jnp.int32)
    h = jnp.concatenate([mixer_left.reshape(16), mixer.reshape(16), gate.reshape(16)])
    up = [(k, (k + 1) % ny) for k in range(ny)]
    down = [(b, a) for a, b in up]
    back = [(b, a) for a, b in around]

    def exchange(v, axis):
        return lax.all_to_all(v, axis, split_axis=0, concat_axis=0, tiled=True)

    pair = [(0, 1), (1, 0)]

    x_own = lax.ppermute(sites[sites.shape[0] - 1], SITE, around)
    b_prev = lax.ppermute(bulk_second, "y", up)
    b_after = lax.ppermute(bulk_second, "y", down)

    quarters, bulk_quarters = split(
        meta, sites, edge_right, proj_right, bulk_first, bulk_right_proj, bulk_left_proj
    )
    q0 = exchange(bulk_quarters, "y")
    q1 = lax.ppermute(q0, "zh", pair)
    q2 = lax.ppermute(q0, "c", pair)
    q3 = lax.ppermute(q1, "c", pair)
    b_low = lax.ppermute(b_prev[:, :width], "y", up)
    b_high = lax.ppermute(b_after[:, width:], "y", down)
    p0 = exchange(quarters, "y")
    p1 = lax.ppermute(p0, "zh", pair)
    p2 = lax.ppermute(p0, "c", pair)
    p3 = lax.ppermute(p1, "c", pair)
    a_own = jnp.stack([x_own, proj_left[0]])
    a_prev = lax.ppermute(a_own, "y", up)
    a_after = lax.ppermute(a_own, "y", down)
    x_cut = a_prev[0]
    l_cut = a_after[1]
    x_far = lax.ppermute(x_cut, "y", up)
    l_far = lax.ppermute(l_cut, "y", down)

    bulk_rows = (bulk_second, b_prev, b_after, b_low, b_high)
    bulk_left, bulk_own, bulk_send = bulk_bond(meta, h, *bulk_rows, q0, q1, q2, q3)
    got = lax.ppermute(bulk_send, "c", pair)
    far = lax.ppermute((bulk_own[1] + got[1]).astype(BF16), "zh", pair)
    bulk_right = (bulk_own[0] + got[0] + far.astype(F32)).astype(BF16)
    got = exchange(jnp.concatenate([bulk_right, bulk_left.astype(BF16)], axis=1), "y")
    ends = bulk_ends(got)
    ends = exchange(ends, SITE)
    new_second = ends[:, :8].reshape(block, 2 * width)
    new_first = ends[:, 8:].reshape(block, 2 * width)

    left, right_own, right_send = window_bonds(
        meta, h, a_own, a_prev, a_after, x_far, l_far, p0, p1, p2, p3, *bulk_rows, q0, q1, q2, q3,
    )
    got = lax.ppermute(right_send, "c", pair)
    left = exchange(left, "y")
    far = (right_own[1] + got[1]).astype(BF16)
    far = lax.ppermute(far, "zh", pair)
    keep_rows = lax.dynamic_index_in_dim(
        keep.reshape(2, ny, 2, block), zh, 0, keepdims=False
    )
    keep_rows = lax.dynamic_index_in_dim(keep_rows, c, 1, keepdims=False)
    right = (right_own[0] + got[0] + far.astype(F32)) * keep_rows[:, :, None]
    got = exchange(right.astype(BF16), "y")
    left = left.astype(F32).sum(0) * jnp.concatenate([keep_left, keep_left])
    returned = lax.ppermute(left.astype(BF16), SITE, back)
    right = jnp.concatenate(
        [got[k, :, t * quarter : (t + 1) * quarter] for t in range(2) for k in range(ny)], axis=1
    )
    return jnp.stack([right, returned]), new_first, new_second


def solution(mesh):
    finer = Mesh(mesh.devices.reshape(4, 2, 2, 4, 2), SITE + BOND)
    rows = P(BOND, None)
    stacked = P(SITE, BOND, None)
    placed = (stacked,) * 3 + (rows,) * 5 + (P(), P(SITE), P(SITE))
    return jax.shard_map(
        half_step,
        mesh=finer,
        in_specs=placed,
        out_specs=(stacked, rows, rows),
        check_vma=False,
    )
```

profile of v0, /device:TPU:44, one launch (start us, length us, event | category | flops | bytes accessed | tf_op | source)
XLA Modules:
  0.0 146.4 jit_solution(9006431976532243518)
XLA Ops:
  1.2 2.6 %split.1 = (bf16[4,64,1024]{2,1,0:T(8,128)(2,1)}, bf16[4,64,1280]{2,1,0:T(8,128)(2,1)}) custom-call(s32[5]{0:T(128)} %stack.42.meta, bf16[2,64,2048]{2,1,0:T(8,128)(2,1)} %site.1, bf16[64,2048]{1,0:T(8,128)(2,1)} %edge.1, bf16[1,64,2048]{2,1,0:T(8,128)(2,1)} %proj.1, bf16[64,2048]{1,0:T(8,128)(2,1)} %bulk.1, bf16[64,2048]{1,0:T(8,128)(2,1)} %bulk_proj.1, ...), custom_call_target="tpu_custom_call" | custom-call | flops 40000000 | bytes 3000000 | tf_op jit(solution)/shard_map/split/pallas_call | solution.py:47
  3.9 5.1 %all-to-all-start.1 = ((bf16[4,64,1280]{2,1,0:T(8,128)(2,1)}), bf16[4,64,1280]{2,1,0:T(8,128)(2,1)S(1)}, u32[]{:S(2)}, u32[]{:S(2)}) async-start(bf16[4,64,1280]{2,1,0:T(8,128)(2,1)} %get-tuple-element.12), calls=%async_computation.1 | async-start | bytes 1310720 | tf_op jit(solution)/shard_map/all_to_all | solution.py:340
  9.7 8.6 %all-to-all-done.1.b0 = bf16[4,64,1280]{2,1,0:T(8,128)(2,1)S(1)} async-done(((bf16[4,64,1280]{2,1,0:T(8,128)(2,1)}), bf16[4,64,1280]{2,1,0:T(8,128)(2,1)S(1)}, u32[]{:S(2)}, u32[]{:S(2)}) %all-to-all-start.1) | async-done | bytes 655392 | tf_op jit(solution)/shard_map/all_to_all | solution.py:340
  18.3 3.0 %collective-permute-start.12 = (bf16[4,64,1280]{2,1,0:T(8,128)(2,1)S(1)}, bf16[4,64,1280]{2,1,0:T(8,128)(2,1)}, u32[]{:S(2)}, u32[]{:S(2)}) collective-permute-start(bf16[4,64,1280]{2,1,0:T(8,128)(2,1)S(1)} %all-to-all-done.1.b0), channel_id=1, source_target_pairs={{0,8},{8,0},{1,9},{9,1},{2,10},{10,2},{3,11},{11,3},{4,12},{12,4},... | collective-permute-start | bytes 1966088 | tf_op jit(solution)/shard_map/ppermute | solution.py:352
  21.4 2.1 %collective-permute-start.1 = (bf16[2,64,2048]{2,1,0:T(8,128)(2,1)S(1)}, bf16[2,64,2048]{2,1,0:T(8,128)(2,1)S(1)}, u32[]{:S(2)}, u32[]{:S(2)}) collective-permute-start(bf16[2,64,2048]{2,1,0:T(8,128)(2,1)S(1)} %pad_maximum_fusion.a_own), channel_id=1, source_target_pairs={{0,2},{2,4},{4,6},{6,0},{1,3},{3,5},{5,7},{7,1},{8,10},{10,12},{12... | collective-permute-start | bytes 1572872 | tf_op jit(solution)/shard_map/ppermute | solution.py:362
  23.5 5.4 %all-to-all-start = ((bf16[4,64,1024]{2,1,0:T(8,128)(2,1)}), bf16[4,64,1024]{2,1,0:T(8,128)(2,1)S(1)}, u32[]{:S(2)}, u32[]{:S(2)}) async-start(bf16[4,64,1024]{2,1,0:T(8,128)(2,1)} %get-tuple-element.11), calls=%async_computation | async-start | bytes 1048576 | tf_op jit(solution)/shard_map/all_to_all | solution.py:340
  31.7 3.6 %collective-permute-done.12.b1 = bf16[4,64,1280]{2,1,0:T(8,128)(2,1)} collective-permute-done((bf16[4,64,1280]{2,1,0:T(8,128)(2,1)S(1)}, bf16[4,64,1280]{2,1,0:T(8,128)(2,1)}, u32[]{:S(2)}, u32[]{:S(2)}) %collective-permute-start.12) | collective-permute-done | bytes 655392 | tf_op jit(solution)/shard_map/ppermute | solution.py:352
  35.5 4.4 %collective-permute-done.9.after = bf16[64,2048]{1,0:T(8,128)(2,1)S(1)} collective-permute-done((bf16[64,2048]{1,0:T(8,128)(2,1)S(1)}, bf16[64,2048]{1,0:T(8,128)(2,1)S(1)}, u32[]{:S(2)}, u32[]{:S(2)}) %collective-permute-start.9) | collective-permute-done | bytes 262176 | tf_op jit(solution)/shard_map/ppermute | solution.py:346
  39.9 4.6 %all-to-all-done.p0 = bf16[4,64,1024]{2,1,0:T(8,128)(2,1)S(1)} async-done(((bf16[4,64,1024]{2,1,0:T(8,128)(2,1)}), bf16[4,64,1024]{2,1,0:T(8,128)(2,1)S(1)}, u32[]{:S(2)}, u32[]{:S(2)}) %all-to-all-start) | async-done | bytes 524320 | tf_op jit(solution)/shard_map/all_to_all | solution.py:340
  45.7 2.1 %collective-permute-done.10.far_low = bf16[64,1024]{1,0:T(8,128)(2,1)} collective-permute-done((bf16[64,1024]{1,0:T(8,128)(2,1)S(1)}, bf16[64,1024]{1,0:T(8,128)(2,1)}, u32[]{:S(2)}, u32[]{:S(2)}) %collective-permute-start.10) | collective-permute-done | bytes 131104 | tf_op jit(solution)/shard_map/ppermute | solution.py:355
  47.8 2.6 %collective-permute-start.2 = (bf16[2,64,2048]{2,1,0:T(8,128)(2,1)S(1)}, bf16[2,64,2048]{2,1,0:T(8,128)(2,1)S(1)}, u32[]{:S(2)}, u32[]{:S(2)}) collective-permute-start(bf16[2,64,2048]{2,1,0:T(8,128)(2,1)S(1)} %pad_maximum_fusion.a_own), channel_id=1, source_target_pairs={{2,0},{4,2},{6,4},{0,6},{3,1},{5,3},{7,5},{1,7},{10,8},{12,10},{14... | collective-permute-start | bytes 1572872 | tf_op jit(solution)/shard_map/ppermute | solution.py:363
  50.5 11.1 %collective-permute-done.11.far_high = bf16[64,1024]{1,0:T(8,128)(2,1)S(1)} collective-permute-done((bf16[64,1024]{1,0:T(8,128)(2,1)S(1)}, bf16[64,1024]{1,0:T(8,128)(2,1)S(1)}, u32[]{:S(2)}, u32[]{:S(2)}) %collective-permute-start.11) | collective-permute-done | bytes 131104 | tf_op jit(solution)/shard_map/ppermute | solution.py:356
  62.3 5.1 %shard_map.131 = (f32[4,32,512]{2,1,0:T(8,128)}, f32[2,4,8,512]{3,2,1,0:T(8,128)}, f32[2,4,8,512]{3,2,1,0:T(8,128)}) custom-call(s32[5]{0:T(128)} %stack.42.meta, f32[48]{0:T(128)} %pad_maximum_fusion.4.h, bf16[64,2048]{1,0:T(8,128)(2,1)} %own.3, bf16[64,2048]{1,0:T(8,128)(2,1)} %copy-done.10, bf16[64,2048]{1,0:T(8,128)(2,1)} %copy-done.11, ...), custom_call_target="tpu_custom_call" | custom-call | flops 1000000000 | bytes 10000000 | tf_op jit(solution)/shard_map/pallas_call | solution.py:224
  72.1 5.3 %collective-permute-done.4.l_far = bf16[64,2048]{1,0:T(8,128)(2,1)S(1)} collective-permute-done((bf16[64,2048]{1,0:T(8,128)(2,1)S(1)}, bf16[64,2048]{1,0:T(8,128)(2,1)S(1)}, u32[]{:S(2)}, u32[]{:S(2)}) %collective-permute-start.4) | collective-permute-done | bytes 262176 | tf_op jit(solution)/shard_map/ppermute | solution.py:367
  78.1 9.5 %shard_map.130 = (bf16[4,64,2048]{2,1,0:T(8,128)(2,1)}, f32[2,4,64,512]{3,2,1,0:T(8,128)}, f32[2,4,64,512]{3,2,1,0:T(8,128)}) custom-call(s32[5]{0:T(128)} %stack.42.meta, f32[48]{0:T(128)} %pad_maximum_fusion.4.h, bf16[2,64,2048]{2,1,0:T(8,128)(2,1)} %copy-done.3, bf16[2,64,2048]{2,1,0:T(8,128)(2,1)} %copy-done.8, bf16[2,64,2048]{2,1,0:T(8,128)(2,1)} %copy-done.9, ...), custom_call_target="tpu_custom_call" | custom-call | flops 3000000000 | bytes 10000000 | tf_op jit(solution)/shard_map/pallas_call | solution.py:224
  87.8 10.4 %all_to_all.30.got = bf16[4,40,512]{2,1,0:T(8,128)(2,1)} all-to-all(bf16[4,40,512]{2,1,0:T(8,128)(2,1)S(1)} %pad_maximum_fusion.2), channel_id=1, replica_groups=mesh['x'=4,'zl'=2,'zh'=2,'y'=4,'c'=2] {'y'}, dimensions={0} | all-to-all | bytes 327680 | tf_op jit(solution)/shard_map/all_to_all | solution.py:340
  100.0 5.7 %all-to-all-start.5 = ((bf16[8,16,2048]{2,1,0:T(8,128)(2,1)}), bf16[8,16,2048]{2,1,0:T(8,128)(2,1)S(1)}, u32[]{:S(2)}, u32[]{:S(2)}) async-start(bf16[8,16,2048]{2,1,0:T(8,128)(2,1)} %finish.1), calls=%async_computation.5 | async-start | bytes 1048576 | tf_op jit(solution)/shard_map/all_to_all | solution.py:340
  106.4 5.0 %all-to-all-done.5 = bf16[8,16,2048]{2,1,0:T(8,128)(2,1)S(1)} async-done(((bf16[8,16,2048]{2,1,0:T(8,128)(2,1)}), bf16[8,16,2048]{2,1,0:T(8,128)(2,1)S(1)}, u32[]{:S(2)}, u32[]{:S(2)}) %all-to-all-start.5) | async-done | bytes 524320 | tf_op jit(solution)/shard_map/all_to_all | solution.py:340
  111.4 5.1 %all-to-all-start.3 = ((bf16[4,64,2048]{2,1,0:T(8,128)(2,1)}), bf16[4,64,2048]{2,1,0:T(8,128)(2,1)S(1)}, u32[]{:S(2)}, u32[]{:S(2)}) async-start(bf16[4,64,2048]{2,1,0:T(8,128)(2,1)} %get-tuple-element.15), calls=%async_computation.3 | async-start | bytes 2097152 | tf_op jit(solution)/shard_map/all_to_all | solution.py:340
  120.1 10.5 %all-to-all-done.3 = bf16[4,64,2048]{2,1,0:T(8,128)(2,1)S(1)} async-done(((bf16[4,64,2048]{2,1,0:T(8,128)(2,1)}), bf16[4,64,2048]{2,1,0:T(8,128)(2,1)S(1)}, u32[]{:S(2)}, u32[]{:S(2)}) %all-to-all-start.3) | async-done | bytes 1048608 | tf_op jit(solution)/shard_map/all_to_all | solution.py:340
  130.8 1.9 %fusion.4 = bf16[4,64,512]{2,1,0:T(8,128)(2,1)} fusion(f32[2,4,64,512]{3,2,1,0:T(8,128)} %collective-permute-done.15, bf16[4,64,512]{2,1,0:T(8,128)(2,1)} %collective-permute-done.16, f32[2,4,64,512]{3,2,1,0:T(8,128)S(1)} %copy-done.1, f32[4,64]{1,0:T(4,128)S(1)} %convert_bitcast_fusion), kind=kLoop, calls=%fused_computation.7 | loop fusion | flops 655360 | bytes 1573888 | tf_op jit(solution)/shard_map/convert_element_type | solution.py:392
  132.7 4.8 %all-to-all-start.2 = ((bf16[4,64,512]{2,1,0:T(8,128)(2,1)}), bf16[4,64,512]{2,1,0:T(8,128)(2,1)S(1)}, u32[]{:S(2)}, u32[]{:S(2)}) async-start(bf16[4,64,512]{2,1,0:T(8,128)(2,1)} %fusion.4), calls=%async_computation.2 | async-start | bytes 524288 | tf_op jit(solution)/shard_map/all_to_all | solution.py:340
  137.6 5.1 %all-to-all-done.2 = bf16[4,64,512]{2,1,0:T(8,128)(2,1)S(1)} async-done(((bf16[4,64,512]{2,1,0:T(8,128)(2,1)}), bf16[4,64,512]{2,1,0:T(8,128)(2,1)S(1)}, u32[]{:S(2)}, u32[]{:S(2)}) %all-to-all-start.2) | async-done | bytes 262176 | tf_op jit(solution)/shard_map/all_to_all | solution.py:340
  142.8 2.8 %collective-permute-done.17 = bf16[64,2048]{1,0:T(8,128)(2,1)S(1)} collective-permute-done((bf16[64,2048]{1,0:T(8,128)(2,1)S(1)}, bf16[64,2048]{1,0:T(8,128)(2,1)S(1)}, u32[]{:S(2)}, u32[]{:S(2)}) %collective-permute-start.17) | collective-permute-done | bytes 262176 | tf_op jit(solution)/shard_map/ppermute | solution.py:394
  (98 shorter events, 17.8 us)
Async XLA Ops:
  3.9 14.5 %all-to-all-start.1 = ((bf16[4,64,1280]{2,1,0:T(8,128)(2,1)}), bf16[4,64,1280]{2,1,0:T(8,128)(2,1)S(1)}, u32[]{:S(2)}, u32[]{:S(2)}) async-start(bf16[4,64,1280]{2,1,0:T(8,128)(2,1)} %get-tuple-element.12), calls=%async_computation.1 | async-start | bytes 1310720 | tf_op jit(solution)/shard_map/all_to_all | solution.py:340
  8.9 12.4 %collective-permute-start = (bf16[64,2048]{1,0:T(8,128)(2,1)S(1)}, bf16[64,2048]{1,0:T(8,128)(2,1)S(1)}, u32[]{:S(2)}, u32[]{:S(2)}) collective-permute-start(bf16[64,2048]{1,0:T(8,128)(2,1)S(1)} %slice_bitcast_fusion.4), channel_id=1, source_target_pairs={{0,16},{16,32},{32,48},{48,64},{64,80},{80,96},{96,112},{112,0},{1... | collective-permute-start | bytes 786440 | tf_op jit(solution)/shard_map/ppermute | solution.py:344
  18.3 16.9 %collective-permute-start.12 = (bf16[4,64,1280]{2,1,0:T(8,128)(2,1)S(1)}, bf16[4,64,1280]{2,1,0:T(8,128)(2,1)}, u32[]{:S(2)}, u32[]{:S(2)}) collective-permute-start(bf16[4,64,1280]{2,1,0:T(8,128)(2,1)S(1)} %all-to-all-done.1.b0), channel_id=1, source_target_pairs={{0,8},{8,0},{1,9},{9,1},{2,10},{10,2},{3,11},{11,3},{4,12},{12,4},... | collective-permute-start | bytes 1966088 | tf_op jit(solution)/shard_map/ppermute | solution.py:352
  21.3 9.2 %collective-permute-start.8 = (bf16[64,2048]{1,0:T(8,128)(2,1)S(1)}, bf16[64,2048]{1,0:T(8,128)(2,1)S(1)}, u32[]{:S(2)}, u32[]{:S(2)}) collective-permute-start(bf16[64,2048]{1,0:T(8,128)(2,1)S(1)} %copy-done.13), channel_id=1, source_target_pairs={{0,2},{2,4},{4,6},{6,0},{1,3},{3,5},{5,7},{7,1},{8,10},{10,12},{12... | collective-permute-start | bytes 786440 | tf_op jit(solution)/shard_map/ppermute | solution.py:345
  21.4 29.0 %collective-permute-start.1 = (bf16[2,64,2048]{2,1,0:T(8,128)(2,1)S(1)}, bf16[2,64,2048]{2,1,0:T(8,128)(2,1)S(1)}, u32[]{:S(2)}, u32[]{:S(2)}) collective-permute-start(bf16[2,64,2048]{2,1,0:T(8,128)(2,1)S(1)} %pad_maximum_fusion.a_own), channel_id=1, source_target_pairs={{0,2},{2,4},{4,6},{6,0},{1,3},{3,5},{5,7},{7,1},{8,10},{10,12},{12... | collective-permute-start | bytes 1572872 | tf_op jit(solution)/shard_map/ppermute | solution.py:362
  23.5 21.1 %all-to-all-start = ((bf16[4,64,1024]{2,1,0:T(8,128)(2,1)}), bf16[4,64,1024]{2,1,0:T(8,128)(2,1)S(1)}, u32[]{:S(2)}, u32[]{:S(2)}) async-start(bf16[4,64,1024]{2,1,0:T(8,128)(2,1)} %get-tuple-element.11), calls=%async_computation | async-start | bytes 1048576 | tf_op jit(solution)/shard_map/all_to_all | solution.py:340
  28.9 11.1 %collective-permute-start.9 = (bf16[64,2048]{1,0:T(8,128)(2,1)S(1)}, bf16[64,2048]{1,0:T(8,128)(2,1)S(1)}, u32[]{:S(2)}, u32[]{:S(2)}) collective-permute-start(bf16[64,2048]{1,0:T(8,128)(2,1)S(1)} %copy-done.13), channel_id=1, source_target_pairs={{2,0},{4,2},{6,4},{0,6},{3,1},{5,3},{7,5},{1,7},{10,8},{12,10},{14... | collective-permute-start | bytes 786440 | tf_op jit(solution)/shard_map/ppermute | solution.py:346
  30.5 17.2 %collective-permute-start.10 = (bf16[64,1024]{1,0:T(8,128)(2,1)S(1)}, bf16[64,1024]{1,0:T(8,128)(2,1)}, u32[]{:S(2)}, u32[]{:S(2)}) collective-permute-start(bf16[64,1024]{1,0:T(8,128)(2,1)S(1)} %slice.94), channel_id=1, source_target_pairs={{0,2},{2,4},{4,6},{6,0},{1,3},{3,5},{5,7},{7,1},{8,10},{10,12},{12... | collective-permute-start | bytes 393224 | tf_op jit(solution)/shard_map/ppermute | solution.py:355
  31.7 30.3 %collective-permute-start.13 = (bf16[4,64,1280]{2,1,0:T(8,128)(2,1)S(1)}, bf16[4,64,1280]{2,1,0:T(8,128)(2,1)}, u32[]{:S(2)}, u32[]{:S(2)}) collective-permute-start(bf16[4,64,1280]{2,1,0:T(8,128)(2,1)S(1)} %all-to-all-done.1.b0), channel_id=1, source_target_pairs={{0,1},{1,0},{2,3},{3,2},{4,5},{5,4},{6,7},{7,6},{8,9},{9,8},{10,11... | collective-permute-start | bytes 1966088 | tf_op jit(solution)/shard_map/ppermute | solution.py:353
  35.3 26.9 %collective-permute-start.14 = (bf16[4,64,1280]{2,1,0:T(8,128)(2,1)}, bf16[4,64,1280]{2,1,0:T(8,128)(2,1)}, u32[]{:S(2)}, u32[]{:S(2)}) collective-permute-start(bf16[4,64,1280]{2,1,0:T(8,128)(2,1)} %collective-permute-done.12.b1), channel_id=1, source_target_pairs={{0,1},{1,0},{2,3},{3,2},{4,5},{5,4},{6,7},{7,6},{8,9},{9,8},{10,11... | collective-permute-start | bytes 1966088 | tf_op jit(solution)/shard_map/ppermute | solution.py:354
  44.5 17.1 %collective-permute-start.5 = (bf16[4,64,1024]{2,1,0:T(8,128)(2,1)S(1)}, bf16[4,64,1024]{2,1,0:T(8,128)(2,1)}, u32[]{:S(2)}, u32[]{:S(2)}) collective-permute-start(bf16[4,64,1024]{2,1,0:T(8,128)(2,1)S(1)} %all-to-all-done.p0), channel_id=1, source_target_pairs={{0,8},{8,0},{1,9},{9,1},{2,10},{10,2},{3,11},{11,3},{4,12},{12,4},... | collective-permute-start | bytes 1572872 | tf_op jit(solution)/shard_map/ppermute | solution.py:358
  47.8 20.0 %collective-permute-start.2 = (bf16[2,64,2048]{2,1,0:T(8,128)(2,1)S(1)}, bf16[2,64,2048]{2,1,0:T(8,128)(2,1)S(1)}, u32[]{:S(2)}, u32[]{:S(2)}) collective-permute-start(bf16[2,64,2048]{2,1,0:T(8,128)(2,1)S(1)} %pad_maximum_fusion.a_own), channel_id=1, source_target_pairs={{2,0},{4,2},{6,4},{0,6},{3,1},{5,3},{7,5},{1,7},{10,8},{12,10},{14... | collective-permute-start | bytes 1572872 | tf_op jit(solution)/shard_map/ppermute | solution.py:363
  50.4 11.2 %collective-permute-start.11 = (bf16[64,1024]{1,0:T(8,128)(2,1)S(1)}, bf16[64,1024]{1,0:T(8,128)(2,1)S(1)}, u32[]{:S(2)}, u32[]{:S(2)}) collective-permute-start(bf16[64,1024]{1,0:T(8,128)(2,1)S(1)} %slice.95), channel_id=1, source_target_pairs={{2,0},{4,2},{6,4},{0,6},{3,1},{5,3},{7,5},{1,7},{10,8},{12,10},{14... | collective-permute-start | bytes 393224 | tf_op jit(solution)/shard_map/ppermute | solution.py:356
  61.6 10.4 %collective-permute-start.6 = (bf16[4,64,1024]{2,1,0:T(8,128)(2,1)S(1)}, bf16[4,64,1024]{2,1,0:T(8,128)(2,1)}, u32[]{:S(2)}, u32[]{:S(2)}) collective-permute-start(bf16[4,64,1024]{2,1,0:T(8,128)(2,1)S(1)} %all-to-all-done.p0), channel_id=1, source_target_pairs={{0,1},{1,0},{2,3},{3,2},{4,5},{5,4},{6,7},{7,6},{8,9},{9,8},{10,11... | collective-permute-start | bytes 1572872 | tf_op jit(solution)/shard_map/ppermute | solution.py:359
  61.6 10.4 %collective-permute-start.3 = (bf16[64,2048]{1,0:T(8,128)(2,1)S(1)}, bf16[64,2048]{1,0:T(8,128)(2,1)S(1)}, u32[]{:S(2)}, u32[]{:S(2)}) collective-permute-start(bf16[64,2048]{1,0:T(8,128)(2,1)S(1)} %slice_bitcast_fusion.3), channel_id=1, source_target_pairs={{0,2},{2,4},{4,6},{6,0},{1,3},{3,5},{5,7},{7,1},{8,10},{10,12},{12... | collective-permute-start | bytes 786440 | tf_op jit(solution)/shard_map/ppermute | solution.py:366
  62.0 15.4 %collective-permute-start.7 = (bf16[4,64,1024]{2,1,0:T(8,128)(2,1)}, bf16[4,64,1024]{2,1,0:T(8,128)(2,1)}, u32[]{:S(2)}, u32[]{:S(2)}) collective-permute-start(bf16[4,64,1024]{2,1,0:T(8,128)(2,1)} %collective-permute-done.5.p1), channel_id=1, source_target_pairs={{0,1},{1,0},{2,3},{3,2},{4,5},{5,4},{6,7},{7,6},{8,9},{9,8},{10,11... | collective-permute-start | bytes 1572872 | tf_op jit(solution)/shard_map/ppermute | solution.py:360
  67.8 9.6 %collective-permute-start.4 = (bf16[64,2048]{1,0:T(8,128)(2,1)S(1)}, bf16[64,2048]{1,0:T(8,128)(2,1)S(1)}, u32[]{:S(2)}, u32[]{:S(2)}) collective-permute-start(bf16[64,2048]{1,0:T(8,128)(2,1)S(1)} %slice_bitcast_fusion.2), channel_id=1, source_target_pairs={{2,0},{4,2},{6,4},{0,6},{3,1},{5,3},{7,5},{1,7},{10,8},{12,10},{14... | collective-permute-start | bytes 786440 | tf_op jit(solution)/shard_map/ppermute | solution.py:367
  70.5 17.3 %collective-permute-start.19 = (bf16[4,8,512]{2,1,0:T(8,128)(2,1)S(1)}, bf16[4,8,512]{2,1,0:T(8,128)(2,1)S(1)}, u32[]{:S(2)}, u32[]{:S(2)}) collective-permute-start(bf16[4,8,512]{2,1,0:T(8,128)(2,1)S(1)} %fusion.10), channel_id=1, source_target_pairs={{0,8},{8,0},{1,9},{9,1},{2,10},{10,2},{3,11},{11,3},{4,12},{12,4},... | collective-permute-start | bytes 98312 | tf_op jit(solution)/shard_map/ppermute | solution.py:372
  87.6 28.9 %collective-permute-start.15 = (f32[2,4,64,512]{3,2,1,0:T(8,128)}, f32[2,4,64,512]{3,2,1,0:T(8,128)}, u32[]{:S(2)}, u32[]{:S(2)}) collective-permute-start(f32[2,4,64,512]{3,2,1,0:T(8,128)} %get-tuple-element.14), channel_id=1, source_target_pairs={{0,1},{1,0},{2,3},{3,2},{4,5},{5,4},{6,7},{7,6},{8,9},{9,8},{10,11... | collective-permute-start | bytes 3145736 | tf_op jit(solution)/shard_map/ppermute | solution.py:383
  100.0 11.4 %all-to-all-start.5 = ((bf16[8,16,2048]{2,1,0:T(8,128)(2,1)}), bf16[8,16,2048]{2,1,0:T(8,128)(2,1)S(1)}, u32[]{:S(2)}, u32[]{:S(2)}) async-start(bf16[8,16,2048]{2,1,0:T(8,128)(2,1)} %finish.1), calls=%async_computation.5 | async-start | bytes 1048576 | tf_op jit(solution)/shard_map/all_to_all | solution.py:340
  111.4 19.2 %all-to-all-start.3 = ((bf16[4,64,2048]{2,1,0:T(8,128)(2,1)}), bf16[4,64,2048]{2,1,0:T(8,128)(2,1)S(1)}, u32[]{:S(2)}, u32[]{:S(2)}) async-start(bf16[4,64,2048]{2,1,0:T(8,128)(2,1)} %get-tuple-element.15), calls=%async_computation.3 | async-start | bytes 2097152 | tf_op jit(solution)/shard_map/all_to_all | solution.py:340
  117.6 13.1 %collective-permute-start.16 = (bf16[4,64,512]{2,1,0:T(8,128)(2,1)S(1)}, bf16[4,64,512]{2,1,0:T(8,128)(2,1)}, u32[]{:S(2)}, u32[]{:S(2)}) collective-permute-start(bf16[4,64,512]{2,1,0:T(8,128)(2,1)S(1)} %fusion.5), channel_id=1, source_target_pairs={{0,8},{8,0},{1,9},{9,1},{2,10},{10,2},{3,11},{11,3},{4,12},{12,4},... | collective-permute-start | bytes 786440 | tf_op jit(solution)/shard_map/ppermute | solution.py:386
  132.7 10.1 %all-to-all-start.2 = ((bf16[4,64,512]{2,1,0:T(8,128)(2,1)}), bf16[4,64,512]{2,1,0:T(8,128)(2,1)S(1)}, u32[]{:S(2)}, u32[]{:S(2)}) async-start(bf16[4,64,512]{2,1,0:T(8,128)(2,1)} %fusion.4), calls=%async_computation.2 | async-start | bytes 524288 | tf_op jit(solution)/shard_map/all_to_all | solution.py:340
  137.5 8.1 %collective-permute-start.17 = (bf16[64,2048]{1,0:T(8,128)(2,1)S(1)}, bf16[64,2048]{1,0:T(8,128)(2,1)S(1)}, u32[]{:S(2)}, u32[]{:S(2)}) collective-permute-start(bf16[64,2048]{1,0:T(8,128)(2,1)S(1)} %multiply_convert_fusion), channel_id=1, source_target_pairs={{16,0},{32,16},{48,32},{64,48},{80,64},{96,80},{112,96},{0,112},{1... | collective-permute-start | bytes 786440 | tf_op jit(solution)/shard_map/ppermute | solution.py:394
  (18 other events, 248.6 us)
where the time goes:
time: 147 us; the launch traced here: 146 us
  waiting for transfers between devices  64.1 us (44%)
  starting transfers between devices  42.5 us (29%)
  Pallas kernels  19 us (13%)
  blocking collectives  10.4 us (7%)
  other arithmetic  5.59 us (4%)
  local copies, waits for them, and re-layouts  2.57 us (2%)
  between operations  2.29 us (2%)
    all_to_all x5, waiting for transfers between devices, exchange(): return lax.all_to_all(v, axis, split_axis=0, concat_axis=0, tiled=True)  33.8 us
    all_to_all x5, starting transfers between devices, exchange(): return lax.all_to_all(v, axis, split_axis=0, concat_axis=0, tiled=True)  26.1 us
    pallas_call x2, Pallas kernels, call(): pl.pallas_call(kernel, out_shape=outs, in_specs=[smem, smem] + [anywhere]...  14.6 us
    ppermute x1, waiting for transfers between devices, half_step(): b_high = lax.ppermute(b_after[:, width:], 'y', down)  11.1 us
    all_to_all x1, blocking collectives, exchange(): return lax.all_to_all(v, axis, split_axis=0, concat_axis=0, tiled=True)  10.4 us
    ppermute x1, waiting for transfers between devices, half_step(): l_far = lax.ppermute(l_cut, 'y', down)  5.35 us
    ppermute x1, waiting for transfers between devices, half_step(): b_after = lax.ppermute(bulk_second, 'y', down)  4.4 us
    ppermute x1, waiting for transfers between devices, half_step(): q1 = lax.ppermute(q0, 'zh', pair)  3.6 us
  transfers between devices with their start and end apart: 25, of which 12 were waited for; matrix products, arithmetic and copies ran while one was open for 3% of the time, Pallas kernels for 11%

commit v1 on v0

--- a/solution.py
+++ b/solution.py
@@ -83,7 +83,7 @@
     lax.fori_loop(0, 256 // step, chunk, 0)
 
 
-def row_copies(parts, cols, ys, zh, c, sem):
+def row_copies(parts, low, high, ys, zh, c, sem):
     copies = []
     for n, part in enumerate(parts):
         z_of = lax.rem(zh + n % 2, 2)
@@ -92,7 +92,7 @@
             at = pl.multiple_of((z_of * 8 + y * 2 + c_of) * 64, 64)
             copies.append(
                 pltpu.make_async_copy(
-                    part.at[y, :, 0:cols], ys.at[pl.ds(at, 64), :], sem.at[n * 4 + y]
+                    part.at[y, :, low:high], ys.at[pl.ds(at, 64), :], sem.at[n * 4 + y]
                 )
             )
     return copies
@@ -100,13 +100,13 @@
 
 def bulk_kernel(
     meta, h, own, prev, after, far_low, far_high, b0, b1, b2, b3,
-    left_ref, keep_ref, send_ref, xs, ys, ls, raw, th, tmp, sem, sem_y,
+    left_ref, keep_ref, send_ref, xs, ys, ls, raw, th, tmp, left_f32, sem, sem_y,
 ):
     c, zh, me, g = meta[0], meta[1], meta[2], meta[4]
     ny, block, width, cols = 4, 64, 1024, 512
     owner = [lax.rem(me + d, ny) for d in (0, 3, 1, 2)]
     rows = [pl.ds(pl.multiple_of(o * block, block), block) for o in owner]
-    copies = row_copies((b0, b1, b2, b3), 2 * cols, ys, zh, c, sem_y)
+    copies = row_copies((b0, b1, b2, b3), 0, 2 * cols, ys, zh, c, sem_y)
     for n, part in enumerate((own, prev, after)):
         copies.append(pltpu.make_async_copy(part, xs.at[rows[n], :], sem.at[n]))
     copies.append(pltpu.make_async_copy(far_low, xs.at[rows[3], 0:width], sem.at[3]))
@@ -119,17 +119,17 @@
 
     theta(h, 32, lambda s: xs[:, s * width : (s + 1) * width], ys[:, 0:cols], raw, th)
     picked = [
-        th[s, pl.ds(pl.multiple_of(y * block + g * 8, 8), 8), :] for s in range(2) for y in range(ny)
+        th[s, pl.ds(pl.multiple_of(o * block + g * 8, 8), 8), :] for s in range(2) for o in owner
     ]
     picked = jnp.concatenate(picked, axis=0).astype(BF16)
     for n in range(4):
         part = dot(picked, ys[n * 256 : (n + 1) * 256, cols : 2 * cols], ((1,), (1,)))
         for s in range(2):
-            to = (2 * s + n // 2) * 8
-            for y in range(ny):
-                left_ref[y, to : to + 8, (n % 2) * 256 : (n % 2 + 1) * 256] = part[
-                    s * 32 + y * 8 : s * 32 + (y + 1) * 8
+            for j in range(ny):
+                left_f32[j, (4 * s + n) * 8 : (4 * s + n + 1) * 8, :] = part[
+                    s * 32 + j * 8 : s * 32 + (j + 1) * 8
                 ]
+    left_ref[...] = left_f32[...].astype(BF16)
     part = None
     for s in range(2):
         l_part = ls[:, :, s * 128 : (s + 1) * 128].reshape(ny * block, 128)
@@ -137,64 +137,102 @@
         part = one if s == 0 else part + one
     tmp[...] = part
     for at in range(2 * ny):
-        z_of = lax.rem(at // ny + zh, 2)
         mine = pl.multiple_of(at * 16 + c * 8, 8)
         other = pl.multiple_of(at * 16 + (1 - c) * 8, 8)
-        keep_ref[z_of, at % ny] = tmp[pl.ds(mine, 8), :]
-        send_ref[z_of, at % ny] = tmp[pl.ds(other, 8), :]
+        keep_ref[at] = tmp[pl.ds(mine, 8), :]
+        send_ref[at] = tmp[pl.ds(other, 8), :]
 
 
 def window_kernel(
-    meta, h, a_own, a_prev, a_after, x_far, l_far, p0, p1, p2, p3, own, prev, after, far_low, far_high, b0, b1, b2, b3,
-    left_ref, keep_ref, send_ref,
-    xs, ls, xb, ys, yb, raw, th, tmp, sem, sem_y, sem_b,
+    meta, h, a_own, a_prev, a_after, x_far, l_far, p0, p1, p2, p3, own, prev, after, far_low, far_high,
+    b0, b1, b2, b3, bulk_left, bulk_keep, bulk_send, left_0, left_1, left_2, left_3, keep_out, send_out,
+    xs, ls, xb, ys, yb, raw, th, tmp, left, keep_rows, send_rows, sem, sem_y, sem_r, sem_b, sem_out,
 ):
-    c, zh, me, first = meta[0], meta[1], meta[2], meta[3]
+    c, zh, first = meta[0], meta[1], meta[3]
     ny, block, width, cols = 4, 64, 1024, 512
-    owner = [lax.rem(me + d, ny) for d in (0, 3, 1, 2)]
-    rows = [pl.ds(pl.multiple_of(o * block, block), block) for o in owner]
-    main = row_copies((p0, p1, p2, p3), 2 * cols, ys, zh, c, sem_y)
-    for n, part in enumerate((a_own.at[0], a_prev.at[0], a_after.at[0], x_far)):
-        main.append(pltpu.make_async_copy(part, xs.at[rows[n], :], sem.at[n]))
-    for n, part in enumerate((own, prev, after)):
-        main.append(pltpu.make_async_copy(part, xb.at[rows[n], :], sem.at[4 + n]))
-    main.append(pltpu.make_async_copy(far_low, xb.at[rows[3], 0:width], sem.at[7]))
-    main.append(pltpu.make_async_copy(far_high, xb.at[rows[3], width : 2 * width], sem.at[8]))
-    main += row_copies((b0, b1, b2, b3), cols, yb, zh, c, sem_b)
-    later = [
-        pltpu.make_async_copy(part, ls.at[rows[n], :], sem.at[10 + n])
+    rows = [slice(n * block, (n + 1) * block) for n in range(ny)]
+    early = [
+        pltpu.make_async_copy(part, xs.at[rows[n], :], sem.at[n])
+        for n, part in enumerate((a_own.at[0], a_prev.at[0], a_after.at[0], x_far))
+    ]
+    early += row_copies((p0, p1, p2, p3), 0, cols, ys.at[:, 0:cols], zh, c, sem_y)
+    edge = row_copies((b0, b1, b2, b3), 0, cols, yb, zh, c, sem_b)
+    proj = row_copies((p0, p1, p2, p3), cols, 2 * cols, ys.at[:, cols : 2 * cols], zh, c, sem_r)
+    bulk = [
+        pltpu.make_async_copy(part, xb.at[rows[n], :], sem.at[4 + n])
+        for n, part in enumerate((own, prev, after))
+    ]
+    bulk.append(pltpu.make_async_copy(far_low, xb.at[rows[3], 0:width], sem.at[7]))
+    bulk.append(pltpu.make_async_copy(far_high, xb.at[rows[3], width : 2 * width], sem.at[8]))
+    late = [
+        pltpu.make_async_copy(part, ls.at[rows[n], :], sem.at[9 + n])
         for n, part in enumerate((a_own.at[1], a_prev.at[1], a_after.at[1], l_far))
     ]
-    for copy in main + later:
-        copy.start()
-    for copy in main:
-        copy.wait()
+    late.append(pltpu.make_async_copy(bulk_keep, keep_rows.at[:, block : block + 8, :], sem.at[13]))
+    late.append(pltpu.make_async_copy(bulk_send, send_rows.at[:, block : block + 8, :], sem.at[14]))
+    for n in range(ny):
+        proj.append(
+            pltpu.make_async_copy(
+                bulk_left.at[n], left.at[rows[n], 2 * width : 2 * width + 256], sem.at[15 + n]
+            )
+        )
+    for copy in early:
+        copy.start()
 
     @pl.when(first == 1)
     def _():
+        for copy in edge:
+            copy.start()
+
+    for copy in proj:
+        copy.start()
+
+    @pl.when(first == 1)
+    def _():
+        for copy in bulk:
+            copy.start()
+
+    for copy in late:
+        copy.start()
+    for copy in early:
+        copy.wait()
+
+    @pl.when(first == 1)
+    def _():
+        for copy in edge:
+            copy.wait()
         theta(h, 0, lambda s: xs[:, s * width : (s + 1) * width], yb[...], raw, th)
 
     @pl.when(first == 0)
     def _():
         theta(h, 0, lambda s: xs[:, s * width : (s + 1) * width], ys[:, 0:cols], raw, th)
+
+    for copy in proj:
+        copy.wait()
 
     def left_chunk(n, _):
         k_at = pl.multiple_of(n * 256, 256)
         r_part = ys[pl.ds(k_at, 256), cols : 2 * cols]
         for s in range(2):
-            part = dot(th[s], r_part, ((1,), (1,))).astype(BF16)
             lanes = pl.ds(pl.multiple_of(s * width + n * 256, 256), 256)
-            for y in range(ny):
-                left_ref[y, :, lanes] = part[y * block : (y + 1) * block]
+            left[:, lanes] = dot(th[s], r_part, ((1,), (1,))).astype(BF16)
         return 0
 
     lax.fori_loop(0, 4, left_chunk, 0)
+    outs = [
+        pltpu.make_async_copy(left.at[rows[n], :], ref, sem_out.at[n])
+        for n, ref in enumerate((left_0, left_1, left_2, left_3))
+    ]
+    for copy in outs:
+        copy.start()
 
     @pl.when(first == 1)
     def _():
+        for copy in bulk:
+            copy.wait()
         theta(h, 16, lambda s: xb[:, s * width : (s + 1) * width], ys[:, 0:cols], raw, th)
 
-    for copy in later:
+    for copy in late:
         copy.wait()
 
     def right_chunk(n, _):
@@ -205,27 +243,29 @@
             part = one if s == 0 else part + one
         tmp[...] = part
         for j in range(2):
-            at = 2 * n + j
-            z_of = lax.rem(lax.div(at, ny) + zh, 2)
-            y_of = lax.rem(at, ny)
             mine = pl.multiple_of(j * 128 + c * block, block)
             other = pl.multiple_of(j * 128 + (1 - c) * block, block)
-            keep_ref[z_of, y_of] = tmp[pl.ds(mine, block), :]
-            send_ref[z_of, y_of] = tmp[pl.ds(other, block), :]
+            keep_rows[2 * n + j, 0:block, :] = tmp[pl.ds(mine, block), :]
+            send_rows[2 * n + j, 0:block, :] = tmp[pl.ds(other, block), :]
         return 0
 
     lax.fori_loop(0, 4, right_chunk, 0)
-
-
-def call(kernel, outs, scratch, flops, meta, h, *arrays):
+    outs.append(pltpu.make_async_copy(send_rows, send_out, sem_out.at[4]))
+    outs.append(pltpu.make_async_copy(keep_rows, keep_out, sem_out.at[5]))
+    for copy in outs[4:]:
+        copy.start()
+    for copy in outs:
+        copy.wait()
+
+
+def call(kernel, outs, out_space, scratch, flops, meta, h, *arrays):
     smem = pl.BlockSpec(memory_space=pltpu.SMEM)
-    vmem = pl.BlockSpec(memory_space=pltpu.VMEM)
     anywhere = pl.BlockSpec(memory_space=pltpu.HBM)
     return pl.pallas_call(
         kernel,
         out_shape=outs,
         in_specs=[smem, smem] + [anywhere] * len(arrays),
-        out_specs=(vmem,) * len(outs),
+        out_specs=(pl.BlockSpec(memory_space=out_space),) * len(outs),
         scratch_shapes=scratch,
         compiler_params=pltpu.CompilerParams(vmem_limit_bytes=VMEM_BYTES),
         cost_estimate=pl.CostEstimate(
@@ -234,30 +274,32 @@
     )(meta, h, *arrays)
 
 
-def ends_kernel(got, out):
-    low = got[:, 8:40, :].astype(F32)
-    low = (low[0] + low[1] + low[2] + low[3]).astype(BF16)
-    left = jnp.concatenate([low[8 * k : 8 * (k + 1)] for k in range(4)], axis=1)
-    right = [got[k, 0:8, t * 256 : (t + 1) * 256] for t in range(2) for k in range(4)]
-    ends = jnp.concatenate([left, jnp.concatenate(right, axis=1)], axis=0)
+def ends_kernel(left, got, out):
+    lows = [left[8 * k : 8 * (k + 1), :] for k in range(8)]
+    rights = [got[q, 64:72].astype(F32) + got[4 + q, 64:72].astype(F32) for q in range(4)]
+    rights = [rights[q][:, t * 256 : (t + 1) * 256] for t in range(2) for q in range(4)]
+    ends = jnp.concatenate(
+        [jnp.concatenate(lows, axis=1), jnp.concatenate(rights, axis=1)], axis=0
+    ).astype(BF16)
     for g in range(8):
         out[g] = ends
 
 
-def bulk_ends(got):
+def bulk_ends(left, got):
     return pl.pallas_call(
         ends_kernel,
         out_shape=jax.ShapeDtypeStruct((8, 16, 2048), BF16),
         cost_estimate=pl.CostEstimate(flops=1_000_000, bytes_accessed=700_000, transcendentals=0),
         name="finish",
-    )(got)
+    )(left, got)
 
 
 def bulk_bond(meta, h, *arrays):
-    sums = jax.ShapeDtypeStruct((2, 4, 8, 512), F32)
+    sums = jax.ShapeDtypeStruct((8, 8, 512), F32)
     return call(
         bulk_kernel,
-        (jax.ShapeDtypeStruct((4, 32, 512), F32), sums, sums),
+        (jax.ShapeDtypeStruct((4, 64, 256), BF16), sums, sums),
+        pltpu.VMEM,
         [
             pltpu.VMEM((256, 2048), BF16),
             pltpu.VMEM((1024, 1024), BF16),
@@ -265,6 +307,7 @@
             pltpu.VMEM((2, 256, 512), F32),
             pltpu.VMEM((2, 256, 512), F32),
             pltpu.VMEM((128, 512), F32),
+            pltpu.VMEM((4, 64, 256), F32),
             pltpu.SemaphoreType.DMA((6,)),
             pltpu.SemaphoreType.DMA((16,)),
         ],
@@ -276,10 +319,12 @@
 
 
 def window_bonds(meta, h, *arrays):
-    sums = jax.ShapeDtypeStruct((2, 4, 64, 512), F32)
+    rows = jax.ShapeDtypeStruct((64, 2304), BF16)
+    sums = jax.ShapeDtypeStruct((8, 72, 512), F32)
     return call(
         window_kernel,
-        (jax.ShapeDtypeStruct((4, 64, 2048), BF16), sums, sums),
+        (rows, rows, rows, rows, sums, sums),
+        pltpu.HBM,
         [
             pltpu.VMEM((256, 2048), BF16),
             pltpu.VMEM((256, 2048), BF16),
@@ -289,15 +334,43 @@
             pltpu.VMEM((2, 256, 512), F32),
             pltpu.VMEM((2, 256, 512), BF16),
             pltpu.VMEM((256, 512), F32),
-            pltpu.SemaphoreType.DMA((14,)),
+            pltpu.VMEM((256, 2304), BF16),
+            pltpu.VMEM((8, 72, 512), F32),
+            pltpu.VMEM((8, 72, 512), F32),
+            pltpu.SemaphoreType.DMA((19,)),
             pltpu.SemaphoreType.DMA((16,)),
             pltpu.SemaphoreType.DMA((16,)),
+            pltpu.SemaphoreType.DMA((16,)),
+            pltpu.SemaphoreType.DMA((6,)),
         ],
         3_000_000_000,
         meta,
         h,
         *arrays,
     )
+
+
+def join_kernel(meta, got, returned, out):
+    row = lax.broadcasted_iota(jnp.int32, (64, 1), 0) + meta[5] * 64
+    keep = jnp.where(row < meta[6], 1.0, 0.0).astype(F32)
+    for q in range(4):
+        part = (got[q, 0:64].astype(F32) + got[4 + q, 0:64].astype(F32)) * keep
+        for t in range(2):
+            at = t * 1024 + q * 256
+            out[0, :, at : at + 256] = part[:, t * 256 : (t + 1) * 256].astype(BF16)
+    out[1] = returned[...]
+
+
+def join(meta, got, returned):
+    vmem = pl.BlockSpec(memory_space=pltpu.VMEM)
+    return pl.pallas_call(
+        join_kernel,
+        out_shape=jax.ShapeDtypeStruct((2, 64, 2048), BF16),
+        in_specs=[pl.BlockSpec(memory_space=pltpu.SMEM), vmem, vmem],
+        out_specs=vmem,
+        cost_estimate=pl.CostEstimate(flops=1_000_000, bytes_accessed=1_300_000, transcendentals=0),
+        name="join",
+    )(meta, got, returned)
 
 
 def half_step(
@@ -317,7 +390,6 @@
     width = sites.shape[2] // 2
     groups = lax.axis_size(SITE)
     ny = lax.axis_size("y")
-    quarter = width // ny
     here = lax.axis_index(SITE)
     zh, y, c = (lax.axis_index(name) for name in BOND)
     first_group = here == 0
@@ -330,7 +402,9 @@
     keep_left = jnp.where(first_group, 1.0, keep)
     around = [(g, (g + 1) % groups) for g in range(groups)]
 
-    meta = jnp.stack([c, zh, y, first_group.astype(jnp.int32), here]).astype(jnp.int32)
+    meta = jnp.stack(
+        [c, zh, y, first_group.astype(jnp.int32), here, lax.axis_index(BOND), bond_dims[0]]
+    ).astype(jnp.int32)
     h = jnp.concatenate([mixer_left.reshape(16), mixer.reshape(16), gate.reshape(16)])
     up = [(k, (k + 1) % ny) for k in range(ny)]
     down = [(b, a) for a, b in up]
@@ -367,35 +441,28 @@
     l_far = lax.ppermute(l_cut, "y", down)
 
     bulk_rows = (bulk_second, b_prev, b_after, b_low, b_high)
-    bulk_left, bulk_own, bulk_send = bulk_bond(meta, h, *bulk_rows, q0, q1, q2, q3)
-    got = lax.ppermute(bulk_send, "c", pair)
-    far = lax.ppermute((bulk_own[1] + got[1]).astype(BF16), "zh", pair)
-    bulk_right = (bulk_own[0] + got[0] + far.astype(F32)).astype(BF16)
-    got = exchange(jnp.concatenate([bulk_right, bulk_left.astype(BF16)], axis=1), "y")
-    ends = bulk_ends(got)
+    bulk_parts = bulk_bond(meta, h, *bulk_rows, q0, q1, q2, q3)
+    left, left_down, left_up, left_far, right_own, right_send = window_bonds(
+        meta, h, a_own, a_prev, a_after, x_far, l_far, p0, p1, p2, p3, *bulk_rows, q0, q1, q2, q3,
+        *bulk_parts,
+    )
+    got = lax.ppermute(right_send, "c", pair)
+    left_down = lax.ppermute(left_down, "y", down)
+    left_up = lax.ppermute(left_up, "y", up)
+    left_far = lax.ppermute(left_far, "y", [(k, (k + 2) % ny) for k in range(ny)])
+    right = (right_own + got).astype(BF16)
+    got = exchange(right, ("zh", "y"))
+    left = sum(v.astype(F32) for v in (left, left_down, left_up, left_far))
+    bulk_left = left[:, 2 * width :]
+    left = left[:, : 2 * width] * jnp.concatenate([keep_left, keep_left])
+    left = left.astype(BF16)
+    returned = lax.ppermute(left, SITE, back)
+    ends = bulk_ends(bulk_left, got)
     ends = exchange(ends, SITE)
+    new_sites = join(meta, got, returned)
     new_second = ends[:, :8].reshape(block, 2 * width)
     new_first = ends[:, 8:].reshape(block, 2 * width)
-
-    left, right_own, right_send = window_bonds(
-        meta, h, a_own, a_prev, a_after, x_far, l_far, p0, p1, p2, p3, *bulk_rows, q0, q1, q2, q3,
-    )
-    got = lax.ppermute(right_send, "c", pair)
-    left = exchange(left, "y")
-    far = (right_own[1] + got[1]).astype(BF16)
-    far = lax.ppermute(far, "zh", pair)
-    keep_rows = lax.dynamic_index_in_dim(
-        keep.reshape(2, ny, 2, block), zh, 0, keepdims=False
-    )
-    keep_rows = lax.dynamic_index_in_dim(keep_rows, c, 1, keepdims=False)
-    right = (right_own[0] + got[0] + far.astype(F32)) * keep_rows[:, :, None]
-    got = exchange(right.astype(BF16), "y")
-    left = left.astype(F32).sum(0) * jnp.concatenate([keep_left, keep_left])
-    returned = lax.ppermute(left.astype(BF16), SITE, back)
-    right = jnp.concatenate(
-        [got[k, :, t * quarter : (t + 1) * quarter] for t in range(2) for k in range(ny)], axis=1
-    )
-    return jnp.stack([right, returned]), new_first, new_second
+    return new_sites, new_first, new_second
 
 
 def solution(mesh):

time: 147 us -> 133 us (0.905)
  the two profiles are of different devices: /device:TPU:44 before, /device:TPU:0 now
where the time goes in v1:
time: 133 us; the launch traced here: 132 us
  waiting for transfers between devices  51.4 us (39%)
  starting transfers between devices  46.8 us (35%)
  Pallas kernels  22.3 us (17%)
  local copies, waits for them, and re-layouts  6.25 us (5%)
  other arithmetic  3.17 us (2%)
  between operations  2.24 us (2%)
    all_to_all x4, starting transfers between devices, exchange(): return lax.all_to_all(v, axis, split_axis=0, concat_axis=0, tiled=True)  18.2 us
    pallas_call x2, Pallas kernels, call(): pl.pallas_call(kernel, out_shape=outs, in_specs=[smem, smem] + [anywhere]...  15.7 us
    all_to_all x4, waiting for transfers between devices, exchange(): return lax.all_to_all(v, axis, split_axis=0, concat_axis=0, tiled=True)  14.4 us
    ppermute x1, waiting for transfers between devices, half_step(): returned = lax.ppermute(left, SITE, back)  8.73 us
    ppermute x1, waiting for transfers between devices, half_step(): b_prev = lax.ppermute(bulk_second, 'y', up)  8.05 us
    ppermute x1, waiting for transfers between devices, half_step(): left_up = lax.ppermute(left_up, 'y', up)  6.89 us
    ppermute x1, waiting for transfers between devices, half_step(): b_low = lax.ppermute(b_prev[:, :width], 'y', up)  5.52 us
    ppermute x1, starting transfers between devices, half_step(): returned = lax.ppermute(left, SITE, back)  4.13 us
  transfers between devices with their start and end apart: 24, of which 10 were waited for; matrix products, arithmetic and copies ran while one was open for 4% of the time, Pallas kernels for 7%

profile of v1, /device:TPU:0, one launch (start us, length us, event | category | flops | bytes accessed | tf_op | source)
XLA Modules:
  0.0 132.2 jit_solution(13065966904205587016)
XLA Ops:
  1.6 2.1 %collective-permute-start = (bf16[64,2048]{1,0:T(8,128)(2,1)S(1)}, bf16[64,2048]{1,0:T(8,128)(2,1)S(1)}, u32[]{:S(2)}, u32[]{:S(2)}) collective-permute-start(bf16[64,2048]{1,0:T(8,128)(2,1)S(1)} %slice_bitcast_fusion.4), channel_id=1, source_target_pairs={{0,16},{16,32},{32,48},{48,64},{64,80},{80,96},{96,112},{112,0},{1... | collective-permute-start | bytes 786440 | tf_op jit(solution)/shard_map/ppermute | solution.py:418
  5.0 2.6 %split.1 = (bf16[4,64,1024]{2,1,0:T(8,128)(2,1)}, bf16[4,64,1280]{2,1,0:T(8,128)(2,1)}) custom-call(s32[7]{0:T(128)} %stack.37.meta, bf16[2,64,2048]{2,1,0:T(8,128)(2,1)} %site.1, bf16[64,2048]{1,0:T(8,128)(2,1)} %edge.1, bf16[1,64,2048]{2,1,0:T(8,128)(2,1)} %proj.1, bf16[64,2048]{1,0:T(8,128)(2,1)} %bulk.1, bf16[64,2048]{1,0:T(8,128)(2,1)} %bulk_proj.1, ...), custom_call_target="tpu_custom_call" | custom-call | flops 40000000 | bytes 3000000 | tf_op jit(solution)/shard_map/split/pallas_call | solution.py:47
  7.6 4.5 %all-to-all-start.1 = ((bf16[4,64,1280]{2,1,0:T(8,128)(2,1)}), bf16[4,64,1280]{2,1,0:T(8,128)(2,1)S(1)}, u32[]{:S(2)}, u32[]{:S(2)}) async-start(bf16[4,64,1280]{2,1,0:T(8,128)(2,1)} %get-tuple-element.15), calls=%async_computation.1 | async-start | bytes 1310720 | tf_op jit(solution)/shard_map/all_to_all | solution.py:414
  14.2 10.1 %all-to-all-done.1.b0 = bf16[4,64,1280]{2,1,0:T(8,128)(2,1)S(1)} async-done(((bf16[4,64,1280]{2,1,0:T(8,128)(2,1)}), bf16[4,64,1280]{2,1,0:T(8,128)(2,1)S(1)}, u32[]{:S(2)}, u32[]{:S(2)}) %all-to-all-start.1) | async-done | bytes 655392 | tf_op jit(solution)/shard_map/all_to_all | solution.py:414
  24.4 3.6 %all-to-all-start = ((bf16[4,64,1024]{2,1,0:T(8,128)(2,1)}), bf16[4,64,1024]{2,1,0:T(8,128)(2,1)S(1)}, u32[]{:S(2)}, u32[]{:S(2)}) async-start(bf16[4,64,1024]{2,1,0:T(8,128)(2,1)} %get-tuple-element.14), calls=%async_computation | async-start | bytes 1048576 | tf_op jit(solution)/shard_map/all_to_all | solution.py:414
  28.0 2.0 %collective-permute-start.8 = (bf16[64,2048]{1,0:T(8,128)(2,1)}, bf16[64,2048]{1,0:T(8,128)(2,1)S(1)}, u32[]{:S(2)}, u32[]{:S(2)}) collective-permute-start(bf16[64,2048]{1,0:T(8,128)(2,1)} %own.3), channel_id=1, source_target_pairs={{0,2},{2,4},{4,6},{6,0},{1,3},{3,5},{5,7},{7,1},{8,10},{10,12},{12... | collective-permute-start | bytes 786440 | tf_op jit(solution)/shard_map/ppermute | solution.py:419
  31.3 3.6 %collective-permute-start.12 = (bf16[4,64,1280]{2,1,0:T(8,128)(2,1)S(1)}, bf16[4,64,1280]{2,1,0:T(8,128)(2,1)}, u32[]{:S(2)}, u32[]{:S(2)}) collective-permute-start(bf16[4,64,1280]{2,1,0:T(8,128)(2,1)S(1)} %all-to-all-done.1.b0), channel_id=1, source_target_pairs={{0,8},{8,0},{1,9},{9,1},{2,10},{10,2},{3,11},{11,3},{4,12},{12,4},... | collective-permute-start | bytes 1966088 | tf_op jit(solution)/shard_map/ppermute | solution.py:426
  36.8 8.1 %collective-permute-done.8.prev = bf16[64,2048]{1,0:T(8,128)(2,1)S(1)} collective-permute-done((bf16[64,2048]{1,0:T(8,128)(2,1)}, bf16[64,2048]{1,0:T(8,128)(2,1)S(1)}, u32[]{:S(2)}, u32[]{:S(2)}) %collective-permute-start.8) | collective-permute-done | bytes 262176 | tf_op jit(solution)/shard_map/ppermute | solution.py:419
  44.9 3.7 %collective-permute-start.5 = (bf16[4,64,1024]{2,1,0:T(8,128)(2,1)S(1)}, bf16[4,64,1024]{2,1,0:T(8,128)(2,1)}, u32[]{:S(2)}, u32[]{:S(2)}) collective-permute-start(bf16[4,64,1024]{2,1,0:T(8,128)(2,1)S(1)} %all-to-all-done.p0), channel_id=1, source_target_pairs={{0,8},{8,0},{1,9},{9,1},{2,10},{10,2},{3,11},{11,3},{4,12},{12,4},... | collective-permute-start | bytes 1572872 | tf_op jit(solution)/shard_map/ppermute | solution.py:432
  49.9 5.5 %collective-permute-done.10.far_low = bf16[64,1024]{1,0:T(8,128)(2,1)S(1)} collective-permute-done((bf16[64,1024]{1,0:T(8,128)(2,1)S(1)}, bf16[64,1024]{1,0:T(8,128)(2,1)S(1)}, u32[]{:S(2)}, u32[]{:S(2)}) %collective-permute-start.10) | collective-permute-done | bytes 131104 | tf_op jit(solution)/shard_map/ppermute | solution.py:429
  55.6 3.6 %collective-permute-done.5.p1 = bf16[4,64,1024]{2,1,0:T(8,128)(2,1)} collective-permute-done((bf16[4,64,1024]{2,1,0:T(8,128)(2,1)S(1)}, bf16[4,64,1024]{2,1,0:T(8,128)(2,1)}, u32[]{:S(2)}, u32[]{:S(2)}) %collective-permute-start.5) | collective-permute-done | bytes 524320 | tf_op jit(solution)/shard_map/ppermute | solution.py:432
  60.5 3.2 %collective-permute-start.4 = (bf16[64,2048]{1,0:T(8,128)(2,1)S(1)}, bf16[64,2048]{1,0:T(8,128)(2,1)S(1)}, u32[]{:S(2)}, u32[]{:S(2)}) collective-permute-start(bf16[64,2048]{1,0:T(8,128)(2,1)S(1)} %slice_bitcast_fusion.2), channel_id=1, source_target_pairs={{2,0},{4,2},{6,4},{0,6},{3,1},{5,3},{7,5},{1,7},{10,8},{12,10},{14... | collective-permute-start | bytes 786440 | tf_op jit(solution)/shard_map/ppermute | solution.py:441
  64.6 5.1 %shard_map.130 = (bf16[4,64,256]{2,1,0:T(8,128)(2,1)}, f32[8,8,512]{2,1,0:T(8,128)}, f32[8,8,512]{2,1,0:T(8,128)}) custom-call(s32[7]{0:T(128)} %stack.37.meta, f32[48]{0:T(128)} %pad_maximum_fusion.2.h, bf16[64,2048]{1,0:T(8,128)(2,1)} %own.3, bf16[64,2048]{1,0:T(8,128)(2,1)} %copy-done.9, bf16[64,2048]{1,0:T(8,128)(2,1)} %copy-done.10, ...), custom_call_target="tpu_custom_call" | custom-call | flops 1000000000 | bytes 10000000 | tf_op jit(solution)/shard_map/pallas_call | solution.py:264
  70.6 10.6 %shard_map.131 = (bf16[64,2304]{1,0:T(8,128)(2,1)}, bf16[64,2304]{1,0:T(8,128)(2,1)}, bf16[64,2304]{1,0:T(8,128)(2,1)}, bf16[64,2304]{1,0:T(8,128)(2,1)}, f32[8,72,512]{2,1,0:T(8,128)}, /*index=5*/f32[8,72,512]{2,1,0:T(8,128)}) custom-call(s32[7]{0:T(128)} %stack.37.meta, f32[48]{0:T(128)} %pad_maximum_fusion.2.h, bf16[2,64,2048]{2,1,0:T(8,128)(2,1)} %copy-done.2, ...), custom_call_target="tpu_custom_call" | custom-call | flops 3000000000 | bytes 10000000 | tf_op jit(solution)/shard_map/pallas_call | solution.py:264
  81.3 2.4 %collective-permute-start.16 = (bf16[64,2304]{1,0:T(8,128)(2,1)}, bf16[64,2304]{1,0:T(8,128)(2,1)S(1)}, u32[]{:S(2)}, u32[]{:S(2)}) collective-permute-start(bf16[64,2304]{1,0:T(8,128)(2,1)} %get-tuple-element.22), channel_id=1, source_target_pairs={{2,0},{4,2},{6,4},{0,6},{3,1},{5,3},{7,5},{1,7},{10,8},{12,10},{14... | collective-permute-start | bytes 884744 | tf_op jit(solution)/shard_map/ppermute | solution.py:450
  85.3 2.3 %add_convert_fusion = bf16[8,72,512]{2,1,0:T(8,128)(2,1)} fusion(f32[8,72,512]{2,1,0:T(8,128)} %get-tuple-element.19, f32[8,72,512]{2,1,0:T(8,128)S(1)} %collective-permute-done.15), kind=kLoop, calls=%fused_computation | loop fusion | flops 589824 | bytes 2949120 | tf_op jit(solution)/shard_map/convert_element_type | solution.py:453
  87.6 6.6 %all-to-all-start.2 = ((bf16[8,72,512]{2,1,0:T(8,128)(2,1)}), bf16[8,72,512]{2,1,0:T(8,128)(2,1)S(1)}, u32[]{:S(2)}, u32[]{:S(2)}) async-start(bf16[8,72,512]{2,1,0:T(8,128)(2,1)} %add_convert_fusion), calls=%async_computation.2 | async-start | bytes 1179648 | tf_op jit(solution)/shard_map/all_to_all | solution.py:414
  94.2 3.4 %collective-permute-done.16 = bf16[64,2304]{1,0:T(8,128)(2,1)S(1)} collective-permute-done((bf16[64,2304]{1,0:T(8,128)(2,1)}, bf16[64,2304]{1,0:T(8,128)(2,1)S(1)}, u32[]{:S(2)}, u32[]{:S(2)}) %collective-permute-start.16) | collective-permute-done | bytes 294944 | tf_op jit(solution)/shard_map/ppermute | solution.py:450
  97.6 6.9 %collective-permute-done.17 = bf16[64,2304]{1,0:T(8,128)(2,1)S(1)} collective-permute-done((bf16[64,2304]{1,0:T(8,128)(2,1)}, bf16[64,2304]{1,0:T(8,128)(2,1)S(1)}, u32[]{:S(2)}, u32[]{:S(2)}) %collective-permute-start.17) | collective-permute-done | bytes 294944 | tf_op jit(solution)/shard_map/ppermute | solution.py:451
  105.3 4.2 %all-to-all-done.2.got = bf16[8,72,512]{2,1,0:T(8,128)(2,1)S(1)} async-done(((bf16[8,72,512]{2,1,0:T(8,128)(2,1)}), bf16[8,72,512]{2,1,0:T(8,128)(2,1)S(1)}, u32[]{:S(2)}, u32[]{:S(2)}) %all-to-all-start.2) | async-done | bytes 589856 | tf_op jit(solution)/shard_map/all_to_all | solution.py:414
  112.2 3.5 %all-to-all-start.3 = ((bf16[8,16,2048]{2,1,0:T(8,128)(2,1)}), bf16[8,16,2048]{2,1,0:T(8,128)(2,1)S(1)}, u32[]{:S(2)}, u32[]{:S(2)}) async-start(bf16[8,16,2048]{2,1,0:T(8,128)(2,1)} %finish.1), calls=%async_computation.3 | async-start | bytes 1048576 | tf_op jit(solution)/shard_map/all_to_all | solution.py:414
  115.8 4.1 %collective-permute-start.19 = (bf16[64,2048]{1,0:T(8,128)(2,1)S(1)}, bf16[64,2048]{1,0:T(8,128)(2,1)S(1)}, u32[]{:S(2)}, u32[]{:S(2)}) collective-permute-start(bf16[64,2048]{1,0:T(8,128)(2,1)S(1)} %fusion), channel_id=1, source_target_pairs={{16,0},{32,16},{48,32},{64,48},{80,64},{96,80},{112,96},{0,112},{1... | collective-permute-start | bytes 786440 | tf_op jit(solution)/shard_map/ppermute | solution.py:459
  119.9 8.7 %collective-permute-done.19.returned = bf16[64,2048]{1,0:T(8,128)(2,1)S(1)} collective-permute-done((bf16[64,2048]{1,0:T(8,128)(2,1)S(1)}, bf16[64,2048]{1,0:T(8,128)(2,1)S(1)}, u32[]{:S(2)}, u32[]{:S(2)}) %collective-permute-start.19) | collective-permute-done | bytes 262176 | tf_op jit(solution)/shard_map/ppermute | solution.py:459
  129.4 2.0 %join.1 = bf16[2,64,2048]{2,1,0:T(8,128)(2,1)} custom-call(s32[7]{0:T(128)} %stack.37.meta, bf16[8,72,512]{2,1,0:T(8,128)(2,1)} %copy-done, bf16[64,2048]{1,0:T(8,128)(2,1)} %copy-done.5), custom_call_target="tpu_custom_call" | custom-call | flops 1000000 | bytes 1300000 | tf_op jit(solution)/shard_map/join/pallas_call | solution.py:366
  (82 shorter events, 17.5 us)
Async XLA Ops:
  1.6 10.6 %collective-permute-start = (bf16[64,2048]{1,0:T(8,128)(2,1)S(1)}, bf16[64,2048]{1,0:T(8,128)(2,1)S(1)}, u32[]{:S(2)}, u32[]{:S(2)}) collective-permute-start(bf16[64,2048]{1,0:T(8,128)(2,1)S(1)} %slice_bitcast_fusion.4), channel_id=1, source_target_pairs={{0,16},{16,32},{32,48},{48,64},{64,80},{80,96},{96,112},{112,0},{1... | collective-permute-start | bytes 786440 | tf_op jit(solution)/shard_map/ppermute | solution.py:418
  7.6 16.8 %all-to-all-start.1 = ((bf16[4,64,1280]{2,1,0:T(8,128)(2,1)}), bf16[4,64,1280]{2,1,0:T(8,128)(2,1)S(1)}, u32[]{:S(2)}, u32[]{:S(2)}) async-start(bf16[4,64,1280]{2,1,0:T(8,128)(2,1)} %get-tuple-element.15), calls=%async_computation.1 | async-start | bytes 1310720 | tf_op jit(solution)/shard_map/all_to_all | solution.py:414
  12.3 37.0 %collective-permute-start.1 = (bf16[2,64,2048]{2,1,0:T(8,128)(2,1)S(1)}, bf16[2,64,2048]{2,1,0:T(8,128)(2,1)S(1)}, u32[]{:S(2)}, u32[]{:S(2)}) collective-permute-start(bf16[2,64,2048]{2,1,0:T(8,128)(2,1)S(1)} %pad_maximum_fusion.a_own), channel_id=1, source_target_pairs={{0,2},{2,4},{4,6},{6,0},{1,3},{3,5},{5,7},{7,1},{8,10},{10,12},{12... | collective-permute-start | bytes 1572872 | tf_op jit(solution)/shard_map/ppermute | solution.py:436
  24.4 20.5 %all-to-all-start = ((bf16[4,64,1024]{2,1,0:T(8,128)(2,1)}), bf16[4,64,1024]{2,1,0:T(8,128)(2,1)S(1)}, u32[]{:S(2)}, u32[]{:S(2)}) async-start(bf16[4,64,1024]{2,1,0:T(8,128)(2,1)} %get-tuple-element.14), calls=%async_computation | async-start | bytes 1048576 | tf_op jit(solution)/shard_map/all_to_all | solution.py:414
  28.0 16.9 %collective-permute-start.8 = (bf16[64,2048]{1,0:T(8,128)(2,1)}, bf16[64,2048]{1,0:T(8,128)(2,1)S(1)}, u32[]{:S(2)}, u32[]{:S(2)}) collective-permute-start(bf16[64,2048]{1,0:T(8,128)(2,1)} %own.3), channel_id=1, source_target_pairs={{0,2},{2,4},{4,6},{6,0},{1,3},{3,5},{5,7},{7,1},{8,10},{10,12},{12... | collective-permute-start | bytes 786440 | tf_op jit(solution)/shard_map/ppermute | solution.py:419
  30.0 19.2 %collective-permute-start.9 = (bf16[64,2048]{1,0:T(8,128)(2,1)}, bf16[64,2048]{1,0:T(8,128)(2,1)S(1)}, u32[]{:S(2)}, u32[]{:S(2)}) collective-permute-start(bf16[64,2048]{1,0:T(8,128)(2,1)} %own.3), channel_id=1, source_target_pairs={{2,0},{4,2},{6,4},{0,6},{3,1},{5,3},{7,5},{1,7},{10,8},{12,10},{14... | collective-permute-start | bytes 786440 | tf_op jit(solution)/shard_map/ppermute | solution.py:420
  31.3 27.8 %collective-permute-start.12 = (bf16[4,64,1280]{2,1,0:T(8,128)(2,1)S(1)}, bf16[4,64,1280]{2,1,0:T(8,128)(2,1)}, u32[]{:S(2)}, u32[]{:S(2)}) collective-permute-start(bf16[4,64,1280]{2,1,0:T(8,128)(2,1)S(1)} %all-to-all-done.1.b0), channel_id=1, source_target_pairs={{0,8},{8,0},{1,9},{9,1},{2,10},{10,2},{3,11},{11,3},{4,12},{12,4},... | collective-permute-start | bytes 1966088 | tf_op jit(solution)/shard_map/ppermute | solution.py:426
  34.9 20.6 %collective-permute-start.2 = (bf16[2,64,2048]{2,1,0:T(8,128)(2,1)S(1)}, bf16[2,64,2048]{2,1,0:T(8,128)(2,1)S(1)}, u32[]{:S(2)}, u32[]{:S(2)}) collective-permute-start(bf16[2,64,2048]{2,1,0:T(8,128)(2,1)S(1)} %pad_maximum_fusion.a_own), channel_id=1, source_target_pairs={{2,0},{4,2},{6,4},{0,6},{3,1},{5,3},{7,5},{1,7},{10,8},{12,10},{14... | collective-permute-start | bytes 1572872 | tf_op jit(solution)/shard_map/ppermute | solution.py:437
  44.9 14.3 %collective-permute-start.5 = (bf16[4,64,1024]{2,1,0:T(8,128)(2,1)S(1)}, bf16[4,64,1024]{2,1,0:T(8,128)(2,1)}, u32[]{:S(2)}, u32[]{:S(2)}) collective-permute-start(bf16[4,64,1024]{2,1,0:T(8,128)(2,1)S(1)} %all-to-all-done.p0), channel_id=1, source_target_pairs={{0,8},{8,0},{1,9},{9,1},{2,10},{10,2},{3,11},{11,3},{4,12},{12,4},... | collective-permute-start | bytes 1572872 | tf_op jit(solution)/shard_map/ppermute | solution.py:432
  49.2 6.2 %collective-permute-start.10 = (bf16[64,1024]{1,0:T(8,128)(2,1)S(1)}, bf16[64,1024]{1,0:T(8,128)(2,1)S(1)}, u32[]{:S(2)}, u32[]{:S(2)}) collective-permute-start(bf16[64,1024]{1,0:T(8,128)(2,1)S(1)} %slice.38), channel_id=1, source_target_pairs={{0,2},{2,4},{4,6},{6,0},{1,3},{3,5},{5,7},{7,1},{8,10},{10,12},{12... | collective-permute-start | bytes 393224 | tf_op jit(solution)/shard_map/ppermute | solution.py:429
  49.9 10.5 %collective-permute-start.13 = (bf16[4,64,1280]{2,1,0:T(8,128)(2,1)S(1)}, bf16[4,64,1280]{2,1,0:T(8,128)(2,1)S(1)}, u32[]{:S(2)}, u32[]{:S(2)}) collective-permute-start(bf16[4,64,1280]{2,1,0:T(8,128)(2,1)S(1)} %all-to-all-done.1.b0), channel_id=1, source_target_pairs={{0,1},{1,0},{2,3},{3,2},{4,5},{5,4},{6,7},{7,6},{8,9},{9,8},{10,11... | collective-permute-start | bytes 1966088 | tf_op jit(solution)/shard_map/ppermute | solution.py:427
  55.5 5.0 %collective-permute-start.11 = (bf16[64,1024]{1,0:T(8,128)(2,1)S(1)}, bf16[64,1024]{1,0:T(8,128)(2,1)S(1)}, u32[]{:S(2)}, u32[]{:S(2)}) collective-permute-start(bf16[64,1024]{1,0:T(8,128)(2,1)S(1)} %slice.39), channel_id=1, source_target_pairs={{2,0},{4,2},{6,4},{0,6},{3,1},{5,3},{7,5},{1,7},{10,8},{12,10},{14... | collective-permute-start | bytes 393224 | tf_op jit(solution)/shard_map/ppermute | solution.py:430
  55.5 14.3 %collective-permute-start.6 = (bf16[4,64,1024]{2,1,0:T(8,128)(2,1)S(1)}, bf16[4,64,1024]{2,1,0:T(8,128)(2,1)}, u32[]{:S(2)}, u32[]{:S(2)}) collective-permute-start(bf16[4,64,1024]{2,1,0:T(8,128)(2,1)S(1)} %all-to-all-done.p0), channel_id=1, source_target_pairs={{0,1},{1,0},{2,3},{3,2},{4,5},{5,4},{6,7},{7,6},{8,9},{9,8},{10,11... | collective-permute-start | bytes 1572872 | tf_op jit(solution)/shard_map/ppermute | solution.py:433
  59.1 10.7 %collective-permute-start.7 = (bf16[4,64,1024]{2,1,0:T(8,128)(2,1)}, bf16[4,64,1024]{2,1,0:T(8,128)(2,1)}, u32[]{:S(2)}, u32[]{:S(2)}) collective-permute-start(bf16[4,64,1024]{2,1,0:T(8,128)(2,1)} %collective-permute-done.5.p1), channel_id=1, source_target_pairs={{0,1},{1,0},{2,3},{3,2},{4,5},{5,4},{6,7},{7,6},{8,9},{9,8},{10,11... | collective-permute-start | bytes 1572872 | tf_op jit(solution)/shard_map/ppermute | solution.py:434
  59.1 5.5 %collective-permute-start.14 = (bf16[4,64,1280]{2,1,0:T(8,128)(2,1)}, bf16[4,64,1280]{2,1,0:T(8,128)(2,1)}, u32[]{:S(2)}, u32[]{:S(2)}) collective-permute-start(bf16[4,64,1280]{2,1,0:T(8,128)(2,1)} %collective-permute-done.12.b1), channel_id=1, source_target_pairs={{0,1},{1,0},{2,3},{3,2},{4,5},{5,4},{6,7},{7,6},{8,9},{9,8},{10,11... | collective-permute-start | bytes 1966088 | tf_op jit(solution)/shard_map/ppermute | solution.py:428
  60.4 9.3 %collective-permute-start.3 = (bf16[64,2048]{1,0:T(8,128)(2,1)S(1)}, bf16[64,2048]{1,0:T(8,128)(2,1)S(1)}, u32[]{:S(2)}, u32[]{:S(2)}) collective-permute-start(bf16[64,2048]{1,0:T(8,128)(2,1)S(1)} %slice_bitcast_fusion.3), channel_id=1, source_target_pairs={{0,2},{2,4},{4,6},{6,0},{1,3},{3,5},{5,7},{7,1},{8,10},{10,12},{12... | collective-permute-start | bytes 786440 | tf_op jit(solution)/shard_map/ppermute | solution.py:440
  60.5 9.3 %collective-permute-start.4 = (bf16[64,2048]{1,0:T(8,128)(2,1)S(1)}, bf16[64,2048]{1,0:T(8,128)(2,1)S(1)}, u32[]{:S(2)}, u32[]{:S(2)}) collective-permute-start(bf16[64,2048]{1,0:T(8,128)(2,1)S(1)} %slice_bitcast_fusion.2), channel_id=1, source_target_pairs={{2,0},{4,2},{6,4},{0,6},{3,1},{5,3},{7,5},{1,7},{10,8},{12,10},{14... | collective-permute-start | bytes 786440 | tf_op jit(solution)/shard_map/ppermute | solution.py:441
  81.2 4.1 %collective-permute-start.15 = (f32[8,72,512]{2,1,0:T(8,128)}, f32[8,72,512]{2,1,0:T(8,128)S(1)}, u32[]{:S(2)}, u32[]{:S(2)}) collective-permute-start(f32[8,72,512]{2,1,0:T(8,128)} %get-tuple-element.20), channel_id=1, source_target_pairs={{0,1},{1,0},{2,3},{3,2},{4,5},{5,4},{6,7},{7,6},{8,9},{9,8},{10,11... | collective-permute-start | bytes 3538952 | tf_op jit(solution)/shard_map/ppermute | solution.py:449
  81.3 16.3 %collective-permute-start.16 = (bf16[64,2304]{1,0:T(8,128)(2,1)}, bf16[64,2304]{1,0:T(8,128)(2,1)S(1)}, u32[]{:S(2)}, u32[]{:S(2)}) collective-permute-start(bf16[64,2304]{1,0:T(8,128)(2,1)} %get-tuple-element.22), channel_id=1, source_target_pairs={{2,0},{4,2},{6,4},{0,6},{3,1},{5,3},{7,5},{1,7},{10,8},{12,10},{14... | collective-permute-start | bytes 884744 | tf_op jit(solution)/shard_map/ppermute | solution.py:450
  83.7 20.8 %collective-permute-start.17 = (bf16[64,2304]{1,0:T(8,128)(2,1)}, bf16[64,2304]{1,0:T(8,128)(2,1)S(1)}, u32[]{:S(2)}, u32[]{:S(2)}) collective-permute-start(bf16[64,2304]{1,0:T(8,128)(2,1)} %get-tuple-element.23), channel_id=1, source_target_pairs={{0,2},{2,4},{4,6},{6,0},{1,3},{3,5},{5,7},{7,1},{8,10},{10,12},{12... | collective-permute-start | bytes 884744 | tf_op jit(solution)/shard_map/ppermute | solution.py:451
  83.7 20.8 %collective-permute-start.18 = (bf16[64,2304]{1,0:T(8,128)(2,1)}, bf16[64,2304]{1,0:T(8,128)(2,1)S(1)}, u32[]{:S(2)}, u32[]{:S(2)}) collective-permute-start(bf16[64,2304]{1,0:T(8,128)(2,1)} %get-tuple-element.24), channel_id=1, source_target_pairs={{0,4},{2,6},{4,0},{6,2},{1,5},{3,7},{5,1},{7,3},{8,12},{10,14},{12... | collective-permute-start | bytes 884744 | tf_op jit(solution)/shard_map/ppermute | solution.py:452
  87.6 21.9 %all-to-all-start.2 = ((bf16[8,72,512]{2,1,0:T(8,128)(2,1)}), bf16[8,72,512]{2,1,0:T(8,128)(2,1)S(1)}, u32[]{:S(2)}, u32[]{:S(2)}) async-start(bf16[8,72,512]{2,1,0:T(8,128)(2,1)} %add_convert_fusion), calls=%async_computation.2 | async-start | bytes 1179648 | tf_op jit(solution)/shard_map/all_to_all | solution.py:414
  112.2 19.1 %all-to-all-start.3 = ((bf16[8,16,2048]{2,1,0:T(8,128)(2,1)}), bf16[8,16,2048]{2,1,0:T(8,128)(2,1)S(1)}, u32[]{:S(2)}, u32[]{:S(2)}) async-start(bf16[8,16,2048]{2,1,0:T(8,128)(2,1)} %finish.1), calls=%async_computation.3 | async-start | bytes 1048576 | tf_op jit(solution)/shard_map/all_to_all | solution.py:414
  115.8 12.9 %collective-permute-start.19 = (bf16[64,2048]{1,0:T(8,128)(2,1)S(1)}, bf16[64,2048]{1,0:T(8,128)(2,1)S(1)}, u32[]{:S(2)}, u32[]{:S(2)}) collective-permute-start(bf16[64,2048]{1,0:T(8,128)(2,1)S(1)} %fusion), channel_id=1, source_target_pairs={{16,0},{32,16},{48,32},{64,48},{80,64},{96,80},{112,96},{0,112},{1... | collective-permute-start | bytes 786440 | tf_op jit(solution)/shard_map/ppermute | solution.py:459
  (17 other events, 238.8 us)

commit v2 on v1

--- a/solution.py
+++ b/solution.py
@@ -80,7 +80,7 @@
                 out[s, r, t * half : (t + 1) * half] = val.astype(out.dtype)
         return 0
 
-    lax.fori_loop(0, 256 // step, chunk, 0)
+    lax.fori_loop(0, 256 // step, chunk, 0, unroll=True)
 
 
 def row_copies(parts, low, high, ys, zh, c, sem):
@@ -99,42 +99,39 @@
 
 
 def bulk_kernel(
-    meta, h, own, prev, after, far_low, far_high, b0, b1, b2, b3,
-    left_ref, keep_ref, send_ref, xs, ys, ls, raw, th, tmp, left_f32, sem, sem_y,
+    meta, h, own, prev, after, far_low, far_high, l_parts, b0, b1, b2, b3,
+    left_ref, keep_ref, send_ref, xs, ys, rs, ls, raw, th, tmp, sem, sem_y,
 ):
     c, zh, me, g = meta[0], meta[1], meta[2], meta[4]
     ny, block, width, cols = 4, 64, 1024, 512
     owner = [lax.rem(me + d, ny) for d in (0, 3, 1, 2)]
-    rows = [pl.ds(pl.multiple_of(o * block, block), block) for o in owner]
-    copies = row_copies((b0, b1, b2, b3), 0, 2 * cols, ys, zh, c, sem_y)
+    copies = row_copies((b0, b1, b2, b3), 0, cols, ys, zh, c, sem_y)
+    for n, part in enumerate((b0, b1, b2, b3)):
+        to = rs.at[n % 2, pl.ds(pl.multiple_of(lax.rem(c + n // 2, 2) * block, block), block), :]
+        copies.append(pltpu.make_async_copy(part.at[ny], to, sem.at[6 + n]))
     for n, part in enumerate((own, prev, after)):
-        copies.append(pltpu.make_async_copy(part, xs.at[rows[n], :], sem.at[n]))
-    copies.append(pltpu.make_async_copy(far_low, xs.at[rows[3], 0:width], sem.at[3]))
-    copies.append(pltpu.make_async_copy(far_high, xs.at[rows[3], width : 2 * width], sem.at[4]))
-    copies.append(pltpu.make_async_copy(b0.at[:, :, width : width + 256], ls, sem.at[5]))
+        copies.append(pltpu.make_async_copy(part, xs.at[n * block : (n + 1) * block, :], sem.at[n]))
+    last = slice(3 * block, 4 * block)
+    copies.append(pltpu.make_async_copy(far_low, xs.at[last, 0:width], sem.at[3]))
+    copies.append(pltpu.make_async_copy(far_high, xs.at[last, width : 2 * width], sem.at[4]))
+    copies.append(pltpu.make_async_copy(l_parts.at[:, :, width : width + 256], ls, sem.at[5]))
     for copy in copies:
         copy.start()
     for copy in copies:
         copy.wait()
 
-    theta(h, 32, lambda s: xs[:, s * width : (s + 1) * width], ys[:, 0:cols], raw, th)
-    picked = [
-        th[s, pl.ds(pl.multiple_of(o * block + g * 8, 8), 8), :] for s in range(2) for o in owner
-    ]
-    picked = jnp.concatenate(picked, axis=0).astype(BF16)
-    for n in range(4):
-        part = dot(picked, ys[n * 256 : (n + 1) * 256, cols : 2 * cols], ((1,), (1,)))
-        for s in range(2):
-            for j in range(ny):
-                left_f32[j, (4 * s + n) * 8 : (4 * s + n + 1) * 8, :] = part[
-                    s * 32 + j * 8 : s * 32 + (j + 1) * 8
-                ]
-    left_ref[...] = left_f32[...].astype(BF16)
+    theta(h, 32, lambda s: xs[:, s * width : (s + 1) * width], ys[...], raw, th)
+    far = lax.rem(lax.div(g, ny) + zh, 2)
     part = None
     for s in range(2):
-        l_part = ls[:, :, s * 128 : (s + 1) * 128].reshape(ny * block, 128)
-        one = dot(l_part, th[s].astype(BF16), ((0,), (0,)))
-        part = one if s == 0 else part + one
+        here = th[s].astype(BF16)
+        left = dot(here, rs[far], ((1,), (1,))).astype(BF16)
+        for j in range(ny):
+            left_ref[j, :, s * 128 : (s + 1) * 128] = left[j * block : (j + 1) * block]
+        for j in range(ny):
+            l_part = ls[owner[j], :, s * 128 : (s + 1) * 128]
+            one = dot(l_part, here[j * block : (j + 1) * block], ((0,), (0,)))
+            part = one if part is None else part + one
     tmp[...] = part
     for at in range(2 * ny):
         mine = pl.multiple_of(at * 16 + c * 8, 8)
@@ -218,7 +215,7 @@
             left[:, lanes] = dot(th[s], r_part, ((1,), (1,))).astype(BF16)
         return 0
 
-    lax.fori_loop(0, 4, left_chunk, 0)
+    lax.fori_loop(0, 4, left_chunk, 0, unroll=True)
     outs = [
         pltpu.make_async_copy(left.at[rows[n], :], ref, sem_out.at[n])
         for n, ref in enumerate((left_0, left_1, left_2, left_3))
@@ -249,7 +246,7 @@
             send_rows[2 * n + j, 0:block, :] = tmp[pl.ds(other, block), :]
         return 0
 
-    lax.fori_loop(0, 4, right_chunk, 0)
+    lax.fori_loop(0, 4, right_chunk, 0, unroll=True)
     outs.append(pltpu.make_async_copy(send_rows, send_out, sem_out.at[4]))
     outs.append(pltpu.make_async_copy(keep_rows, keep_out, sem_out.at[5]))
     for copy in outs[4:]:
@@ -275,23 +272,52 @@
 
 
 def ends_kernel(left, got, out):
-    lows = [left[8 * k : 8 * (k + 1), :] for k in range(8)]
-    rights = [got[q, 64:72].astype(F32) + got[4 + q, 64:72].astype(F32) for q in range(4)]
+    rights = [got[q].astype(F32) + got[4 + q].astype(F32) for q in range(4)]
     rights = [rights[q][:, t * 256 : (t + 1) * 256] for t in range(2) for q in range(4)]
-    ends = jnp.concatenate(
-        [jnp.concatenate(lows, axis=1), jnp.concatenate(rights, axis=1)], axis=0
-    ).astype(BF16)
+    rights = jnp.concatenate(rights, axis=0).astype(BF16)
+    lefts = left[...].astype(BF16)
     for g in range(8):
-        out[g] = ends
+        out[g, :, 0:256] = lefts
+        out[g, :, 256:512] = rights
 
 
 def bulk_ends(left, got):
     return pl.pallas_call(
         ends_kernel,
-        out_shape=jax.ShapeDtypeStruct((8, 16, 2048), BF16),
+        grid=(1,),
+        in_specs=[
+            pl.BlockSpec((64, 256), lambda i: (0, 0)),
+            pl.BlockSpec((8, 8, 512), lambda i: (0, 8, 0)),
+        ],
+        out_specs=pl.BlockSpec((8, 64, 512), lambda i: (0, 0, 0)),
+        out_shape=jax.ShapeDtypeStruct((8, 64, 512), BF16),
         cost_estimate=pl.CostEstimate(flops=1_000_000, bytes_accessed=700_000, transcendentals=0),
         name="finish",
     )(left, got)
+
+
+def spread_kernel(ends, first, second):
+    for g in range(8):
+        for s in range(2):
+            second[:, s * 1024 + g * 128 : s * 1024 + (g + 1) * 128] = ends[
+                g, :, s * 128 : (s + 1) * 128
+            ]
+    for pair in range(4):
+        rows = []
+        for g in (2 * pair, 2 * pair + 1):
+            right = ends[g, :, 256:512].astype(F32)
+            rows.append(jnp.concatenate([right[8 * k : 8 * (k + 1)] for k in range(8)], axis=1))
+        first[16 * pair : 16 * (pair + 1), :] = jnp.concatenate(rows, axis=0).astype(BF16)
+
+
+def spread(ends):
+    rows = jax.ShapeDtypeStruct((64, 2048), BF16)
+    return pl.pallas_call(
+        spread_kernel,
+        out_shape=(rows, rows),
+        cost_estimate=pl.CostEstimate(flops=1_000_000, bytes_accessed=1_000_000, transcendentals=0),
+        name="spread",
+    )(ends)
 
 
 def bulk_bond(meta, h, *arrays):
@@ -302,13 +328,13 @@
         pltpu.VMEM,
         [
             pltpu.VMEM((256, 2048), BF16),
-            pltpu.VMEM((1024, 1024), BF16),
+            pltpu.VMEM((1024, 512), BF16),
+            pltpu.VMEM((2, 128, 512), BF16),
             pltpu.VMEM((4, 64, 256), BF16),
             pltpu.VMEM((2, 256, 512), F32),
             pltpu.VMEM((2, 256, 512), F32),
             pltpu.VMEM((128, 512), F32),
-            pltpu.VMEM((4, 64, 256), F32),
-            pltpu.SemaphoreType.DMA((6,)),
+            pltpu.SemaphoreType.DMA((10,)),
             pltpu.SemaphoreType.DMA((16,)),
         ],
         1_000_000_000,
@@ -386,7 +412,6 @@
     gate_mask,
     bond_dims,
 ):
-    block = sites.shape[1]
     width = sites.shape[2] // 2
     groups = lax.axis_size(SITE)
     ny = lax.axis_size("y")
@@ -423,11 +448,15 @@
         meta, sites, edge_right, proj_right, bulk_first, bulk_right_proj, bulk_left_proj
     )
     q0 = exchange(bulk_quarters, "y")
-    q1 = lax.ppermute(q0, "zh", pair)
-    q2 = lax.ppermute(q0, "c", pair)
+    chosen = lax.dynamic_index_in_dim(q0, lax.rem(here, ny), 0)[:, :, width // 2 : width]
+    b_own = jnp.concatenate([q0[:, :, : width // 2], chosen], axis=0)
+    q1 = lax.ppermute(b_own, "zh", pair)
+    q2 = lax.ppermute(b_own, "c", pair)
     q3 = lax.ppermute(q1, "c", pair)
-    b_low = lax.ppermute(b_prev[:, :width], "y", up)
-    b_high = lax.ppermute(b_after[:, width:], "y", down)
+    b_low = b_prev[:, :width]
+    b_high = b_after[:, width:]
+    b_low = lax.ppermute(b_low, "y", up)
+    b_high = lax.ppermute(b_high, "y", down)
     p0 = exchange(quarters, "y")
     p1 = lax.ppermute(p0, "zh", pair)
     p2 = lax.ppermute(p0, "c", pair)
@@ -441,9 +470,9 @@
     l_far = lax.ppermute(l_cut, "y", down)
 
     bulk_rows = (bulk_second, b_prev, b_after, b_low, b_high)
-    bulk_parts = bulk_bond(meta, h, *bulk_rows, q0, q1, q2, q3)
+    bulk_parts = bulk_bond(meta, h, *bulk_rows, q0, b_own, q1, q2, q3)
     left, left_down, left_up, left_far, right_own, right_send = window_bonds(
-        meta, h, a_own, a_prev, a_after, x_far, l_far, p0, p1, p2, p3, *bulk_rows, q0, q1, q2, q3,
+        meta, h, a_own, a_prev, a_after, x_far, l_far, p0, p1, p2, p3, *bulk_rows, b_own, q1, q2, q3,
         *bulk_parts,
     )
     got = lax.ppermute(right_send, "c", pair)
@@ -460,8 +489,7 @@
     ends = bulk_ends(bulk_left, got)
     ends = exchange(ends, SITE)
     new_sites = join(meta, got, returned)
-    new_second = ends[:, :8].reshape(block, 2 * width)
-    new_first = ends[:, 8:].reshape(block, 2 * width)
+    new_first, new_second = spread(ends)
     return new_sites, new_first, new_second
 
 

time: 133 us -> 144 us (1.083)
  the two profiles are of different devices: /device:TPU:0 before, /device:TPU:1 now
where the time goes in v2:
time: 144 us; the launch traced here: 143 us
  starting transfers between devices  55 us (38%)
  waiting for transfers between devices  54.5 us (38%)
  Pallas kernels  22.3 us (15%)
  local copies, waits for them, and re-layouts  6.08 us (4%)
  other arithmetic  3.22 us (2%)
  between operations  2.29 us (2%)
    ppermute x1, waiting for transfers between devices, half_step(): b_prev = lax.ppermute(bulk_second, 'y', up)  20.8 us
    all_to_all x4, starting transfers between devices, exchange(): return lax.all_to_all(v, axis, split_axis=0, concat_axis=0, tiled=True)  18.1 us
    all_to_all x4, waiting for transfers between devices, exchange(): return lax.all_to_all(v, axis, split_axis=0, concat_axis=0, tiled=True)  15.8 us
    pallas_call x2, Pallas kernels, call(): pl.pallas_call(kernel, out_shape=outs, in_specs=[smem, smem] + [anywhere]...  14 us
    ppermute x1, waiting for transfers between devices, half_step(): returned = lax.ppermute(left, SITE, back)  9.52 us
    ppermute x1, starting transfers between devices, half_step(): p3 = lax.ppermute(p1, 'c', pair)  6.96 us
    ppermute x1, waiting for transfers between devices, half_step(): lax.ppermute(left_far, 'y', [(k, (k + 2) % ny) for k in range(ny)])  5.02 us
    unnamed x36, local copies, waits for them, and re-layouts  3.78 us
  transfers between devices with their start and end apart: 24, of which 7 were waited for; matrix products, arithmetic and copies ran while one was open for 3% of the time, Pallas kernels for 5%

profile of v2, /device:TPU:1, one launch (start us, length us, event | category | flops | bytes accessed | tf_op | source)
XLA Modules:
  0.0 143.4 jit_solution(4673725758891422156)
XLA Ops:
  1.9 2.7 %split.1 = (bf16[4,64,1024]{2,1,0:T(8,128)(2,1)}, bf16[4,64,1280]{2,1,0:T(8,128)(2,1)}) custom-call(s32[7]{0:T(128)} %stack.37.meta, bf16[2,64,2048]{2,1,0:T(8,128)(2,1)} %site.1, bf16[64,2048]{1,0:T(8,128)(2,1)} %edge.1, bf16[1,64,2048]{2,1,0:T(8,128)(2,1)} %proj.1, bf16[64,2048]{1,0:T(8,128)(2,1)} %bulk.1, bf16[64,2048]{1,0:T(8,128)(2,1)} %bulk_proj.1, ...), custom_call_target="tpu_custom_call" | custom-call | flops 40000000 | bytes 3000000 | tf_op jit(solution)/shard_map/split/pallas_call | solution.py:47
  4.6 5.0 %all-to-all-start = ((bf16[4,64,1024]{2,1,0:T(8,128)(2,1)}), bf16[4,64,1024]{2,1,0:T(8,128)(2,1)S(1)}, u32[]{:S(2)}, u32[]{:S(2)}) async-start(bf16[4,64,1024]{2,1,0:T(8,128)(2,1)} %get-tuple-element.16), calls=%async_computation | async-start | bytes 1048576 | tf_op jit(solution)/shard_map/all_to_all | solution.py:439
  11.3 6.9 %all-to-all-done.p0 = bf16[4,64,1024]{2,1,0:T(8,128)(2,1)S(1)} async-done(((bf16[4,64,1024]{2,1,0:T(8,128)(2,1)}), bf16[4,64,1024]{2,1,0:T(8,128)(2,1)S(1)}, u32[]{:S(2)}, u32[]{:S(2)}) %all-to-all-start) | async-done | bytes 524320 | tf_op jit(solution)/shard_map/all_to_all | solution.py:439
  18.2 3.5 %all-to-all-start.1 = ((bf16[4,64,1280]{2,1,0:T(8,128)(2,1)}), bf16[4,64,1280]{2,1,0:T(8,128)(2,1)S(1)}, u32[]{:S(2)}, u32[]{:S(2)}) async-start(bf16[4,64,1280]{2,1,0:T(8,128)(2,1)} %get-tuple-element.17), calls=%async_computation.1 | async-start | bytes 1310720 | tf_op jit(solution)/shard_map/all_to_all | solution.py:439
  26.7 20.8 %collective-permute-done.8.prev = bf16[64,2048]{1,0:T(8,128)(2,1)S(1)} collective-permute-done((bf16[64,2048]{1,0:T(8,128)(2,1)}, bf16[64,2048]{1,0:T(8,128)(2,1)S(1)}, u32[]{:S(2)}, u32[]{:S(2)}) %collective-permute-start.8) | collective-permute-done | bytes 262176 | tf_op jit(solution)/shard_map/ppermute | solution.py:444
  48.3 2.7 %collective-permute-start.11 = (bf16[64,1024]{1,0:T(8,128)(2,1)S(1)}, bf16[64,1024]{1,0:T(8,128)(2,1)}, u32[]{:S(2)}, u32[]{:S(2)}) collective-permute-start(bf16[64,1024]{1,0:T(8,128)(2,1)S(1)} %slice.39), channel_id=1, source_target_pairs={{2,0},{4,2},{6,4},{0,6},{3,1},{5,3},{7,5},{1,7},{10,8},{12,10},{14... | collective-permute-start | bytes 393224 | tf_op jit(solution)/shard_map/ppermute | solution.py:459
  51.0 3.6 %collective-permute-start.5 = (bf16[4,64,1024]{2,1,0:T(8,128)(2,1)S(1)}, bf16[4,64,1024]{2,1,0:T(8,128)(2,1)}, u32[]{:S(2)}, u32[]{:S(2)}) collective-permute-start(bf16[4,64,1024]{2,1,0:T(8,128)(2,1)S(1)} %all-to-all-done.p0), channel_id=1, source_target_pairs={{0,8},{8,0},{1,9},{9,1},{2,10},{10,2},{3,11},{11,3},{4,12},{12,4},... | collective-permute-start | bytes 1572872 | tf_op jit(solution)/shard_map/ppermute | solution.py:461
  54.8 3.5 %collective-permute-start.6 = (bf16[4,64,1024]{2,1,0:T(8,128)(2,1)S(1)}, bf16[4,64,1024]{2,1,0:T(8,128)(2,1)}, u32[]{:S(2)}, u32[]{:S(2)}) collective-permute-start(bf16[4,64,1024]{2,1,0:T(8,128)(2,1)S(1)} %all-to-all-done.p0), channel_id=1, source_target_pairs={{0,1},{1,0},{2,3},{3,2},{4,5},{5,4},{6,7},{7,6},{8,9},{9,8},{10,11... | collective-permute-start | bytes 1572872 | tf_op jit(solution)/shard_map/ppermute | solution.py:462
  58.4 2.8 %collective-permute-start.13 = (bf16[5,64,512]{2,1,0:T(8,128)(2,1)S(1)}, bf16[5,64,512]{2,1,0:T(8,128)(2,1)S(1)}, u32[]{:S(2)}, u32[]{:S(2)}) collective-permute-start(bf16[5,64,512]{2,1,0:T(8,128)(2,1)S(1)} %pad_maximum_fusion.1.b0), channel_id=1, source_target_pairs={{0,1},{1,0},{2,3},{3,2},{4,5},{5,4},{6,7},{7,6},{8,9},{9,8},{10,11... | collective-permute-start | bytes 983048 | tf_op jit(solution)/shard_map/ppermute | solution.py:454
  61.2 2.8 %collective-permute-done.5.p1 = bf16[4,64,1024]{2,1,0:T(8,128)(2,1)} collective-permute-done((bf16[4,64,1024]{2,1,0:T(8,128)(2,1)S(1)}, bf16[4,64,1024]{2,1,0:T(8,128)(2,1)}, u32[]{:S(2)}, u32[]{:S(2)}) %collective-permute-start.5) | collective-permute-done | bytes 524320 | tf_op jit(solution)/shard_map/ppermute | solution.py:461
  63.9 7.0 %collective-permute-start.7 = (bf16[4,64,1024]{2,1,0:T(8,128)(2,1)}, bf16[4,64,1024]{2,1,0:T(8,128)(2,1)}, u32[]{:S(2)}, u32[]{:S(2)}) collective-permute-start(bf16[4,64,1024]{2,1,0:T(8,128)(2,1)} %collective-permute-done.5.p1), channel_id=1, source_target_pairs={{0,1},{1,0},{2,3},{3,2},{4,5},{5,4},{6,7},{7,6},{8,9},{9,8},{10,11... | collective-permute-start | bytes 1572872 | tf_op jit(solution)/shard_map/ppermute | solution.py:463
  71.0 2.7 %collective-permute-start.4 = (bf16[64,2048]{1,0:T(8,128)(2,1)S(1)}, bf16[64,2048]{1,0:T(8,128)(2,1)}, u32[]{:S(2)}, u32[]{:S(2)}) collective-permute-start(bf16[64,2048]{1,0:T(8,128)(2,1)S(1)} %slice_bitcast_fusion), channel_id=1, source_target_pairs={{2,0},{4,2},{6,4},{0,6},{3,1},{5,3},{7,5},{1,7},{10,8},{12,10},{14... | collective-permute-start | bytes 786440 | tf_op jit(solution)/shard_map/ppermute | solution.py:470
  77.2 5.0 %shard_map.130 = (bf16[4,64,256]{2,1,0:T(8,128)(2,1)}, f32[8,8,512]{2,1,0:T(8,128)}, f32[8,8,512]{2,1,0:T(8,128)}) custom-call(s32[7]{0:T(128)} %stack.37.meta, f32[48]{0:T(128)} %pad_maximum_fusion.3.h, bf16[64,2048]{1,0:T(8,128)(2,1)} %own.3, bf16[64,2048]{1,0:T(8,128)(2,1)} %copy-done.12, bf16[64,2048]{1,0:T(8,128)(2,1)} %copy-done.13, ...), custom_call_target="tpu_custom_call" | custom-call | flops 1000000000 | bytes 10000000 | tf_op jit(solution)/shard_map/pallas_call | solution.py:261
  82.9 9.0 %shard_map.131 = (bf16[64,2304]{1,0:T(8,128)(2,1)}, bf16[64,2304]{1,0:T(8,128)(2,1)}, bf16[64,2304]{1,0:T(8,128)(2,1)}, bf16[64,2304]{1,0:T(8,128)(2,1)}, f32[8,72,512]{2,1,0:T(8,128)}, /*index=5*/f32[8,72,512]{2,1,0:T(8,128)}) custom-call(s32[7]{0:T(128)} %stack.37.meta, f32[48]{0:T(128)} %pad_maximum_fusion.3.h, bf16[2,64,2048]{2,1,0:T(8,128)(2,1)} %copy-done.5, ...), custom_call_target="tpu_custom_call" | custom-call | flops 3000000000 | bytes 10000000 | tf_op jit(solution)/shard_map/pallas_call | solution.py:261
  95.6 2.3 %add_convert_fusion = bf16[8,72,512]{2,1,0:T(8,128)(2,1)} fusion(f32[8,72,512]{2,1,0:T(8,128)} %get-tuple-element.21, f32[8,72,512]{2,1,0:T(8,128)S(1)} %collective-permute-done.15), kind=kLoop, calls=%fused_computation | loop fusion | flops 589824 | bytes 2949120 | tf_op jit(solution)/shard_map/convert_element_type | solution.py:482
  97.9 6.2 %all-to-all-start.2 = ((bf16[8,72,512]{2,1,0:T(8,128)(2,1)}), bf16[8,72,512]{2,1,0:T(8,128)(2,1)S(1)}, u32[]{:S(2)}, u32[]{:S(2)}) async-start(bf16[8,72,512]{2,1,0:T(8,128)(2,1)} %add_convert_fusion), calls=%async_computation.2 | async-start | bytes 1179648 | tf_op jit(solution)/shard_map/all_to_all | solution.py:439
  104.1 5.0 %collective-permute-done.18 = bf16[64,2304]{1,0:T(8,128)(2,1)S(1)} collective-permute-done((bf16[64,2304]{1,0:T(8,128)(2,1)}, bf16[64,2304]{1,0:T(8,128)(2,1)S(1)}, u32[]{:S(2)}, u32[]{:S(2)}) %collective-permute-start.18) | collective-permute-done | bytes 294944 | tf_op jit(solution)/shard_map/ppermute | solution.py:481
  109.9 8.9 %all-to-all-done.2.got = bf16[8,72,512]{2,1,0:T(8,128)(2,1)S(1)} async-done(((bf16[8,72,512]{2,1,0:T(8,128)(2,1)}), bf16[8,72,512]{2,1,0:T(8,128)(2,1)S(1)}, u32[]{:S(2)}, u32[]{:S(2)}) %all-to-all-start.2) | async-done | bytes 589856 | tf_op jit(solution)/shard_map/all_to_all | solution.py:439
  119.6 1.7 %finish.1 = bf16[8,64,512]{2,1,0:T(8,128)(2,1)} custom-call(f32[64,256]{1,0:T(8,128)} %slice.42.left, bf16[8,72,512]{2,1,0:T(8,128)(2,1)} %copy-done), custom_call_target="tpu_custom_call" | custom-call | flops 1000000 | bytes 700000 | tf_op jit(solution)/shard_map/finish/pallas_call | solution.py:285
  121.3 3.5 %all-to-all-start.3 = ((bf16[8,64,512]{2,1,0:T(8,128)(2,1)}), bf16[8,64,512]{2,1,0:T(8,128)(2,1)S(1)}, u32[]{:S(2)}, u32[]{:S(2)}) async-start(bf16[8,64,512]{2,1,0:T(8,128)(2,1)} %finish.1), calls=%async_computation.3 | async-start | bytes 1048576 | tf_op jit(solution)/shard_map/all_to_all | solution.py:439
  124.9 3.6 %collective-permute-start.19 = (bf16[64,2048]{1,0:T(8,128)(2,1)S(1)}, bf16[64,2048]{1,0:T(8,128)(2,1)S(1)}, u32[]{:S(2)}, u32[]{:S(2)}) collective-permute-start(bf16[64,2048]{1,0:T(8,128)(2,1)S(1)} %fusion), channel_id=1, source_target_pairs={{16,0},{32,16},{48,32},{64,48},{80,64},{96,80},{112,96},{0,112},{1... | collective-permute-start | bytes 786440 | tf_op jit(solution)/shard_map/ppermute | solution.py:488
  128.4 9.5 %collective-permute-done.19.returned = bf16[64,2048]{1,0:T(8,128)(2,1)S(1)} collective-permute-done((bf16[64,2048]{1,0:T(8,128)(2,1)S(1)}, bf16[64,2048]{1,0:T(8,128)(2,1)S(1)}, u32[]{:S(2)}, u32[]{:S(2)}) %collective-permute-start.19) | collective-permute-done | bytes 262176 | tf_op jit(solution)/shard_map/ppermute | solution.py:488
  138.7 2.0 %join.1 = bf16[2,64,2048]{2,1,0:T(8,128)(2,1)} custom-call(s32[7]{0:T(128)} %stack.37.meta, bf16[8,72,512]{2,1,0:T(8,128)(2,1)} %copy-done, bf16[64,2048]{1,0:T(8,128)(2,1)} %copy-done.8), custom_call_target="tpu_custom_call" | custom-call | flops 1000000 | bytes 1300000 | tf_op jit(solution)/shard_map/join/pallas_call | solution.py:392
  141.5 1.9 %spread.1 = (bf16[64,2048]{1,0:T(8,128)(2,1)}, bf16[64,2048]{1,0:T(8,128)(2,1)}) custom-call(bf16[8,64,512]{2,1,0:T(8,128)(2,1)} %copy-done.1), custom_call_target="tpu_custom_call" | custom-call | flops 1000000 | bytes 1000000 | tf_op jit(solution)/shard_map/spread/pallas_call | solution.py:315
  (87 shorter events, 18.7 us)
Async XLA Ops:
  4.6 13.6 %all-to-all-start = ((bf16[4,64,1024]{2,1,0:T(8,128)(2,1)}), bf16[4,64,1024]{2,1,0:T(8,128)(2,1)S(1)}, u32[]{:S(2)}, u32[]{:S(2)}) async-start(bf16[4,64,1024]{2,1,0:T(8,128)(2,1)} %get-tuple-element.16), calls=%async_computation | async-start | bytes 1048576 | tf_op jit(solution)/shard_map/all_to_all | solution.py:439
  9.6 12.1 %collective-permute-start = (bf16[64,2048]{1,0:T(8,128)(2,1)S(1)}, bf16[64,2048]{1,0:T(8,128)(2,1)S(1)}, u32[]{:S(2)}, u32[]{:S(2)}) collective-permute-start(bf16[64,2048]{1,0:T(8,128)(2,1)S(1)} %slice_bitcast_fusion.2), channel_id=1, source_target_pairs={{0,16},{16,32},{32,48},{48,64},{64,80},{80,96},{96,112},{112,0},{1... | collective-permute-start | bytes 786440 | tf_op jit(solution)/shard_map/ppermute | solution.py:443
  18.2 36.4 %all-to-all-start.1 = ((bf16[4,64,1280]{2,1,0:T(8,128)(2,1)}), bf16[4,64,1280]{2,1,0:T(8,128)(2,1)S(1)}, u32[]{:S(2)}, u32[]{:S(2)}) async-start(bf16[4,64,1280]{2,1,0:T(8,128)(2,1)} %get-tuple-element.17), calls=%async_computation.1 | async-start | bytes 1310720 | tf_op jit(solution)/shard_map/all_to_all | solution.py:439
  21.8 32.9 %collective-permute-start.1 = (bf16[2,64,2048]{2,1,0:T(8,128)(2,1)S(1)}, bf16[2,64,2048]{2,1,0:T(8,128)(2,1)S(1)}, u32[]{:S(2)}, u32[]{:S(2)}) collective-permute-start(bf16[2,64,2048]{2,1,0:T(8,128)(2,1)S(1)} %pad_maximum_fusion.a_own), channel_id=1, source_target_pairs={{0,2},{2,4},{4,6},{6,0},{1,3},{3,5},{5,7},{7,1},{8,10},{10,12},{12... | collective-permute-start | bytes 1572872 | tf_op jit(solution)/shard_map/ppermute | solution.py:465
  23.3 24.3 %collective-permute-start.8 = (bf16[64,2048]{1,0:T(8,128)(2,1)}, bf16[64,2048]{1,0:T(8,128)(2,1)S(1)}, u32[]{:S(2)}, u32[]{:S(2)}) collective-permute-start(bf16[64,2048]{1,0:T(8,128)(2,1)} %own.3), channel_id=1, source_target_pairs={{0,2},{2,4},{4,6},{6,0},{1,3},{3,5},{5,7},{7,1},{8,10},{10,12},{12... | collective-permute-start | bytes 786440 | tf_op jit(solution)/shard_map/ppermute | solution.py:444
  24.4 23.8 %collective-permute-start.9 = (bf16[64,2048]{1,0:T(8,128)(2,1)}, bf16[64,2048]{1,0:T(8,128)(2,1)S(1)}, u32[]{:S(2)}, u32[]{:S(2)}) collective-permute-start(bf16[64,2048]{1,0:T(8,128)(2,1)} %own.3), channel_id=1, source_target_pairs={{2,0},{4,2},{6,4},{0,6},{3,1},{5,3},{7,5},{1,7},{10,8},{12,10},{14... | collective-permute-start | bytes 786440 | tf_op jit(solution)/shard_map/ppermute | solution.py:445
  26.6 31.8 %collective-permute-start.2 = (bf16[2,64,2048]{2,1,0:T(8,128)(2,1)S(1)}, bf16[2,64,2048]{2,1,0:T(8,128)(2,1)S(1)}, u32[]{:S(2)}, u32[]{:S(2)}) collective-permute-start(bf16[2,64,2048]{2,1,0:T(8,128)(2,1)S(1)} %pad_maximum_fusion.a_own), channel_id=1, source_target_pairs={{2,0},{4,2},{6,4},{0,6},{3,1},{5,3},{7,5},{1,7},{10,8},{12,10},{14... | collective-permute-start | bytes 1572872 | tf_op jit(solution)/shard_map/ppermute | solution.py:466
  48.2 10.0 %collective-permute-start.10 = (bf16[64,1024]{1,0:T(8,128)(2,1)}, bf16[64,1024]{1,0:T(8,128)(2,1)}, u32[]{:S(2)}, u32[]{:S(2)}) collective-permute-start(bf16[64,1024]{1,0:T(8,128)(2,1)} %slice.38), channel_id=1, source_target_pairs={{0,2},{2,4},{4,6},{6,0},{1,3},{3,5},{5,7},{7,1},{8,10},{10,12},{12... | collective-permute-start | bytes 393224 | tf_op jit(solution)/shard_map/ppermute | solution.py:458
  48.3 22.6 %collective-permute-start.11 = (bf16[64,1024]{1,0:T(8,128)(2,1)S(1)}, bf16[64,1024]{1,0:T(8,128)(2,1)}, u32[]{:S(2)}, u32[]{:S(2)}) collective-permute-start(bf16[64,1024]{1,0:T(8,128)(2,1)S(1)} %slice.39), channel_id=1, source_target_pairs={{2,0},{4,2},{6,4},{0,6},{3,1},{5,3},{7,5},{1,7},{10,8},{12,10},{14... | collective-permute-start | bytes 393224 | tf_op jit(solution)/shard_map/ppermute | solution.py:459
  51.0 12.9 %collective-permute-start.5 = (bf16[4,64,1024]{2,1,0:T(8,128)(2,1)S(1)}, bf16[4,64,1024]{2,1,0:T(8,128)(2,1)}, u32[]{:S(2)}, u32[]{:S(2)}) collective-permute-start(bf16[4,64,1024]{2,1,0:T(8,128)(2,1)S(1)} %all-to-all-done.p0), channel_id=1, source_target_pairs={{0,8},{8,0},{1,9},{9,1},{2,10},{10,2},{3,11},{11,3},{4,12},{12,4},... | collective-permute-start | bytes 1572872 | tf_op jit(solution)/shard_map/ppermute | solution.py:461
  54.8 27.4 %collective-permute-start.6 = (bf16[4,64,1024]{2,1,0:T(8,128)(2,1)S(1)}, bf16[4,64,1024]{2,1,0:T(8,128)(2,1)}, u32[]{:S(2)}, u32[]{:S(2)}) collective-permute-start(bf16[4,64,1024]{2,1,0:T(8,128)(2,1)S(1)} %all-to-all-done.p0), channel_id=1, source_target_pairs={{0,1},{1,0},{2,3},{3,2},{4,5},{5,4},{6,7},{7,6},{8,9},{9,8},{10,11... | collective-permute-start | bytes 1572872 | tf_op jit(solution)/shard_map/ppermute | solution.py:462
  58.3 12.7 %collective-permute-start.12 = (bf16[5,64,512]{2,1,0:T(8,128)(2,1)S(1)}, bf16[5,64,512]{2,1,0:T(8,128)(2,1)}, u32[]{:S(2)}, u32[]{:S(2)}) collective-permute-start(bf16[5,64,512]{2,1,0:T(8,128)(2,1)S(1)} %pad_maximum_fusion.1.b0), channel_id=1, source_target_pairs={{0,8},{8,0},{1,9},{9,1},{2,10},{10,2},{3,11},{11,3},{4,12},{12,4},... | collective-permute-start | bytes 983048 | tf_op jit(solution)/shard_map/ppermute | solution.py:453
  58.4 15.3 %collective-permute-start.13 = (bf16[5,64,512]{2,1,0:T(8,128)(2,1)S(1)}, bf16[5,64,512]{2,1,0:T(8,128)(2,1)S(1)}, u32[]{:S(2)}, u32[]{:S(2)}) collective-permute-start(bf16[5,64,512]{2,1,0:T(8,128)(2,1)S(1)} %pad_maximum_fusion.1.b0), channel_id=1, source_target_pairs={{0,1},{1,0},{2,3},{3,2},{4,5},{5,4},{6,7},{7,6},{8,9},{9,8},{10,11... | collective-permute-start | bytes 983048 | tf_op jit(solution)/shard_map/ppermute | solution.py:454
  63.9 18.3 %collective-permute-start.7 = (bf16[4,64,1024]{2,1,0:T(8,128)(2,1)}, bf16[4,64,1024]{2,1,0:T(8,128)(2,1)}, u32[]{:S(2)}, u32[]{:S(2)}) collective-permute-start(bf16[4,64,1024]{2,1,0:T(8,128)(2,1)} %collective-permute-done.5.p1), channel_id=1, source_target_pairs={{0,1},{1,0},{2,3},{3,2},{4,5},{5,4},{6,7},{7,6},{8,9},{9,8},{10,11... | collective-permute-start | bytes 1572872 | tf_op jit(solution)/shard_map/ppermute | solution.py:463
  70.9 11.3 %collective-permute-start.3 = (bf16[64,2048]{1,0:T(8,128)(2,1)S(1)}, bf16[64,2048]{1,0:T(8,128)(2,1)S(1)}, u32[]{:S(2)}, u32[]{:S(2)}) collective-permute-start(bf16[64,2048]{1,0:T(8,128)(2,1)S(1)} %slice_bitcast_fusion.1), channel_id=1, source_target_pairs={{0,2},{2,4},{4,6},{6,0},{1,3},{3,5},{5,7},{7,1},{8,10},{10,12},{12... | collective-permute-start | bytes 786440 | tf_op jit(solution)/shard_map/ppermute | solution.py:469
  71.0 11.2 %collective-permute-start.4 = (bf16[64,2048]{1,0:T(8,128)(2,1)S(1)}, bf16[64,2048]{1,0:T(8,128)(2,1)}, u32[]{:S(2)}, u32[]{:S(2)}) collective-permute-start(bf16[64,2048]{1,0:T(8,128)(2,1)S(1)} %slice_bitcast_fusion), channel_id=1, source_target_pairs={{2,0},{4,2},{6,4},{0,6},{3,1},{5,3},{7,5},{1,7},{10,8},{12,10},{14... | collective-permute-start | bytes 786440 | tf_op jit(solution)/shard_map/ppermute | solution.py:470
  73.7 2.8 %collective-permute-start.14 = (bf16[5,64,512]{2,1,0:T(8,128)(2,1)}, bf16[5,64,512]{2,1,0:T(8,128)(2,1)S(1)}, u32[]{:S(2)}, u32[]{:S(2)}) collective-permute-start(bf16[5,64,512]{2,1,0:T(8,128)(2,1)} %collective-permute-done.12.b1), channel_id=1, source_target_pairs={{0,1},{1,0},{2,3},{3,2},{4,5},{5,4},{6,7},{7,6},{8,9},{9,8},{10,11... | collective-permute-start | bytes 983048 | tf_op jit(solution)/shard_map/ppermute | solution.py:455
  92.0 3.6 %collective-permute-start.15 = (f32[8,72,512]{2,1,0:T(8,128)}, f32[8,72,512]{2,1,0:T(8,128)S(1)}, u32[]{:S(2)}, u32[]{:S(2)}) collective-permute-start(f32[8,72,512]{2,1,0:T(8,128)} %get-tuple-element.22), channel_id=1, source_target_pairs={{0,1},{1,0},{2,3},{3,2},{4,5},{5,4},{6,7},{7,6},{8,9},{9,8},{10,11... | collective-permute-start | bytes 3538952 | tf_op jit(solution)/shard_map/ppermute | solution.py:478
  92.4 11.6 %collective-permute-start.16 = (bf16[64,2304]{1,0:T(8,128)(2,1)}, bf16[64,2304]{1,0:T(8,128)(2,1)S(1)}, u32[]{:S(2)}, u32[]{:S(2)}) collective-permute-start(bf16[64,2304]{1,0:T(8,128)(2,1)} %get-tuple-element.24), channel_id=1, source_target_pairs={{2,0},{4,2},{6,4},{0,6},{3,1},{5,3},{7,5},{1,7},{10,8},{12,10},{14... | collective-permute-start | bytes 884744 | tf_op jit(solution)/shard_map/ppermute | solution.py:479
  92.8 11.2 %collective-permute-start.17 = (bf16[64,2304]{1,0:T(8,128)(2,1)}, bf16[64,2304]{1,0:T(8,128)(2,1)S(1)}, u32[]{:S(2)}, u32[]{:S(2)}) collective-permute-start(bf16[64,2304]{1,0:T(8,128)(2,1)} %get-tuple-element.25), channel_id=1, source_target_pairs={{0,2},{2,4},{4,6},{6,0},{1,3},{3,5},{5,7},{7,1},{8,10},{10,12},{12... | collective-permute-start | bytes 884744 | tf_op jit(solution)/shard_map/ppermute | solution.py:480
  93.9 15.2 %collective-permute-start.18 = (bf16[64,2304]{1,0:T(8,128)(2,1)}, bf16[64,2304]{1,0:T(8,128)(2,1)S(1)}, u32[]{:S(2)}, u32[]{:S(2)}) collective-permute-start(bf16[64,2304]{1,0:T(8,128)(2,1)} %get-tuple-element.26), channel_id=1, source_target_pairs={{0,4},{2,6},{4,0},{6,2},{1,5},{3,7},{5,1},{7,3},{8,12},{10,14},{12... | collective-permute-start | bytes 884744 | tf_op jit(solution)/shard_map/ppermute | solution.py:481
  97.9 20.9 %all-to-all-start.2 = ((bf16[8,72,512]{2,1,0:T(8,128)(2,1)}), bf16[8,72,512]{2,1,0:T(8,128)(2,1)S(1)}, u32[]{:S(2)}, u32[]{:S(2)}) async-start(bf16[8,72,512]{2,1,0:T(8,128)(2,1)} %add_convert_fusion), calls=%async_computation.2 | async-start | bytes 1179648 | tf_op jit(solution)/shard_map/all_to_all | solution.py:439
  121.3 19.4 %all-to-all-start.3 = ((bf16[8,64,512]{2,1,0:T(8,128)(2,1)}), bf16[8,64,512]{2,1,0:T(8,128)(2,1)S(1)}, u32[]{:S(2)}, u32[]{:S(2)}) async-start(bf16[8,64,512]{2,1,0:T(8,128)(2,1)} %finish.1), calls=%async_computation.3 | async-start | bytes 1048576 | tf_op jit(solution)/shard_map/all_to_all | solution.py:439
  124.9 13.1 %collective-permute-start.19 = (bf16[64,2048]{1,0:T(8,128)(2,1)S(1)}, bf16[64,2048]{1,0:T(8,128)(2,1)S(1)}, u32[]{:S(2)}, u32[]{:S(2)}) collective-permute-start(bf16[64,2048]{1,0:T(8,128)(2,1)S(1)} %fusion), channel_id=1, source_target_pairs={{16,0},{32,16},{48,32},{64,48},{80,64},{96,80},{112,96},{0,112},{1... | collective-permute-start | bytes 786440 | tf_op jit(solution)/shard_map/ppermute | solution.py:488
  (18 other events, 238.7 us)

commit v3 on v2

--- a/solution.py
+++ b/solution.py
@@ -18,8 +18,10 @@
     return lax.dot_general(a, b, (dims, ((), ())), preferred_element_type=F32)
 
 
-def split_kernel(meta, site, edge, proj, bulk, bulk_proj, bulk_left, out_ref, bulk_ref):
-    first, g = meta[3], meta[4]
+def split_kernel(
+    meta, site, edge, proj, bulk, bulk_proj, bulk_left, w_0, w_1, w_2, w_3, b_0, b_1, b_2, b_3
+):
+    me, first, g = meta[2], meta[3], meta[4]
     quarter, width = 256, 1024
     column = lax.broadcasted_iota(jnp.int32, (width, 128), 1)
     source = (column // 8) * 64 + g * 8 + column % 8
@@ -27,17 +29,18 @@
     chosen = chosen.astype(BF16)
     for s in range(2):
         part = dot(bulk_left[:, s * width : (s + 1) * width], chosen, ((1,), (0,))).astype(BF16)
-        for q in range(4):
-            bulk_ref[q, :, width + s * 128 : width + (s + 1) * 128] = part
-    for q in range(4):
+        for ref in (b_0, b_1, b_2, b_3):
+            ref[:, width + s * 128 : width + (s + 1) * 128] = part
+    for step, w_ref, b_ref in ((0, w_0, b_0), (1, w_1, b_1), (3, w_2, b_2), (2, w_3, b_3)):
+        q = lax.rem(me + step, 4)
         for t in range(2):
-            cols = slice(t * width + q * quarter, t * width + (q + 1) * quarter)
+            cols = pl.ds(pl.multiple_of(t * width + q * quarter, quarter), quarter)
             low = slice(t * quarter, (t + 1) * quarter)
             high = slice((2 + t) * quarter, (3 + t) * quarter)
-            out_ref[q, :, low] = site[0, :, cols]
-            bulk_ref[q, :, low] = bulk[:, cols]
-            out_ref[q, :, high] = jnp.where(first == 1, edge[:, cols], proj[0, :, cols])
-            bulk_ref[q, :, high] = bulk_proj[:, cols]
+            w_ref[:, low] = site[0, :, cols]
+            b_ref[:, low] = bulk[:, cols]
+            w_ref[:, high] = jnp.where(first == 1, edge[:, cols], proj[0, :, cols])
+            b_ref[:, high] = bulk_proj[:, cols]
 
 
 def split(meta, sites, edge, proj, bulk, bulk_proj, bulk_left):
@@ -47,15 +50,11 @@
     return pl.pallas_call(
         split_kernel,
         grid=(1,),
-        out_shape=(
-            jax.ShapeDtypeStruct((4, 64, 1024), BF16),
-            jax.ShapeDtypeStruct((4, 64, 1280), BF16),
-        ),
+        out_shape=(jax.ShapeDtypeStruct((64, 1024), BF16),) * 4
+        + (jax.ShapeDtypeStruct((64, 1280), BF16),) * 4,
         in_specs=[smem, one, flat, one, flat, flat, flat],
-        out_specs=(
-            pl.BlockSpec((4, 64, 1024), lambda i: (0, 0, 0)),
-            pl.BlockSpec((4, 64, 1280), lambda i: (0, 0, 0)),
-        ),
+        out_specs=(pl.BlockSpec((64, 1024), lambda i: (0, 0)),) * 4
+        + (pl.BlockSpec((64, 1280), lambda i: (0, 0)),) * 4,
         cost_estimate=pl.CostEstimate(
             flops=40_000_000, bytes_accessed=3_000_000, transcendentals=0
         ),
@@ -83,13 +82,13 @@
     lax.fori_loop(0, 256 // step, chunk, 0, unroll=True)
 
 
-def row_copies(parts, low, high, ys, zh, c, sem):
+def row_copies(parts, low, high, ys, zh, c, me, sem):
     copies = []
     for n, part in enumerate(parts):
         z_of = lax.rem(zh + n % 2, 2)
         c_of = lax.rem(c + n // 2, 2)
-        for y in range(4):
-            at = pl.multiple_of((z_of * 8 + y * 2 + c_of) * 64, 64)
+        for y, step in enumerate((0, 3, 1, 2)):
+            at = pl.multiple_of((z_of * 8 + lax.rem(me + step, 4) * 2 + c_of) * 64, 64)
             copies.append(
                 pltpu.make_async_copy(
                     part.at[y, :, low:high], ys.at[pl.ds(at, 64), :], sem.at[n * 4 + y]
@@ -104,8 +103,7 @@
 ):
     c, zh, me, g = meta[0], meta[1], meta[2], meta[4]
     ny, block, width, cols = 4, 64, 1024, 512
-    owner = [lax.rem(me + d, ny) for d in (0, 3, 1, 2)]
-    copies = row_copies((b0, b1, b2, b3), 0, cols, ys, zh, c, sem_y)
+    copies = row_copies((b0, b1, b2, b3), 0, cols, ys, zh, c, me, sem_y)
     for n, part in enumerate((b0, b1, b2, b3)):
         to = rs.at[n % 2, pl.ds(pl.multiple_of(lax.rem(c + n // 2, 2) * block, block), block), :]
         copies.append(pltpu.make_async_copy(part.at[ny], to, sem.at[6 + n]))
@@ -129,7 +127,7 @@
         for j in range(ny):
             left_ref[j, :, s * 128 : (s + 1) * 128] = left[j * block : (j + 1) * block]
         for j in range(ny):
-            l_part = ls[owner[j], :, s * 128 : (s + 1) * 128]
+            l_part = ls[j, :, s * 128 : (s + 1) * 128]
             one = dot(l_part, here[j * block : (j + 1) * block], ((0,), (0,)))
             part = one if part is None else part + one
     tmp[...] = part
@@ -145,16 +143,16 @@
     b0, b1, b2, b3, bulk_left, bulk_keep, bulk_send, left_0, left_1, left_2, left_3, keep_out, send_out,
     xs, ls, xb, ys, yb, raw, th, tmp, left, keep_rows, send_rows, sem, sem_y, sem_r, sem_b, sem_out,
 ):
-    c, zh, first = meta[0], meta[1], meta[3]
+    c, zh, me, first = meta[0], meta[1], meta[2], meta[3]
     ny, block, width, cols = 4, 64, 1024, 512
     rows = [slice(n * block, (n + 1) * block) for n in range(ny)]
     early = [
         pltpu.make_async_copy(part, xs.at[rows[n], :], sem.at[n])
         for n, part in enumerate((a_own.at[0], a_prev.at[0], a_after.at[0], x_far))
     ]
-    early += row_copies((p0, p1, p2, p3), 0, cols, ys.at[:, 0:cols], zh, c, sem_y)
-    edge = row_copies((b0, b1, b2, b3), 0, cols, yb, zh, c, sem_b)
-    proj = row_copies((p0, p1, p2, p3), cols, 2 * cols, ys.at[:, cols : 2 * cols], zh, c, sem_r)
+    early += row_copies((p0, p1, p2, p3), 0, cols, ys.at[:, 0:cols], zh, c, me, sem_y)
+    edge = row_copies((b0, b1, b2, b3), 0, cols, yb, zh, c, me, sem_b)
+    proj = row_copies((p0, p1, p2, p3), cols, 2 * cols, ys.at[:, cols : 2 * cols], zh, c, me, sem_r)
     bulk = [
         pltpu.make_async_copy(part, xb.at[rows[n], :], sem.at[4 + n])
         for n, part in enumerate((own, prev, after))
@@ -444,11 +442,20 @@
     b_prev = lax.ppermute(bulk_second, "y", up)
     b_after = lax.ppermute(bulk_second, "y", down)
 
-    quarters, bulk_quarters = split(
+    across = [(k, (k + 2) % ny) for k in range(ny)]
+    w_0, w_1, w_2, w_3, b_0, b_1, b_2, b_3 = split(
         meta, sites, edge_right, proj_right, bulk_first, bulk_right_proj, bulk_left_proj
     )
-    q0 = exchange(bulk_quarters, "y")
-    chosen = lax.dynamic_index_in_dim(q0, lax.rem(here, ny), 0)[:, :, width // 2 : width]
+    b_1 = lax.ppermute(b_1, "y", up)
+    b_2 = lax.ppermute(b_2, "y", down)
+    b_3 = lax.ppermute(b_3, "y", across)
+    w_1 = lax.ppermute(w_1, "y", up)
+    w_2 = lax.ppermute(w_2, "y", down)
+    w_3 = lax.ppermute(w_3, "y", across)
+    q0 = jnp.stack([b_0, b_1, b_2, b_3])
+    step = lax.rem(here + 2 * ny - y, ny)
+    place = jnp.where(step == 0, 0, jnp.where(step == 3, 1, step + 1))
+    chosen = lax.dynamic_index_in_dim(q0, place, 0)[:, :, width // 2 : width]
     b_own = jnp.concatenate([q0[:, :, : width // 2], chosen], axis=0)
     q1 = lax.ppermute(b_own, "zh", pair)
     q2 = lax.ppermute(b_own, "c", pair)
@@ -457,7 +464,7 @@
     b_high = b_after[:, width:]
     b_low = lax.ppermute(b_low, "y", up)
     b_high = lax.ppermute(b_high, "y", down)
-    p0 = exchange(quarters, "y")
+    p0 = jnp.stack([w_0, w_1, w_2, w_3])
     p1 = lax.ppermute(p0, "zh", pair)
     p2 = lax.ppermute(p0, "c", pair)
     p3 = lax.ppermute(p1, "c", pair)
@@ -478,7 +485,7 @@
     got = lax.ppermute(right_send, "c", pair)
     left_down = lax.ppermute(left_down, "y", down)
     left_up = lax.ppermute(left_up, "y", up)
-    left_far = lax.ppermute(left_far, "y", [(k, (k + 2) % ny) for k in range(ny)])
+    left_far = lax.ppermute(left_far, "y", across)
     right = (right_own + got).astype(BF16)
     got = exchange(right, ("zh", "y"))
     left = sum(v.astype(F32) for v in (left, left_down, left_up, left_far))

time: 144 us -> 128 us (0.89)
  the two profiles are of different devices: /device:TPU:1 before, /device:TPU:0 now
where the time goes in v3:
time: 128 us
  starting transfers between devices  47.5 us (37%)
  waiting for transfers between devices  45.9 us (36%)
  Pallas kernels  22.4 us (18%)
  local copies, waits for them, and re-layouts  6.43 us (5%)
  other arithmetic  3.33 us (3%)
  between operations  2.28 us (2%)
    pallas_call x2, Pallas kernels, call(): pl.pallas_call(kernel, out_shape=outs, in_specs=[smem, smem] + [anywhere]...  14.2 us
    all_to_all x2, starting transfers between devices, exchange(): return lax.all_to_all(v, axis, split_axis=0, concat_axis=0, tiled=True)  10.5 us
    ppermute x1, waiting for transfers between devices, half_step(): returned = lax.ppermute(left, SITE, back)  8.73 us
    ppermute x1, waiting for transfers between devices, half_step(): left_up = lax.ppermute(left_up, 'y', up)  6.89 us
    ppermute x1, waiting for transfers between devices, half_step(): w_2 = lax.ppermute(w_2, 'y', down)  6.62 us
    ppermute x1, waiting for transfers between devices, half_step(): b_low = lax.ppermute(b_low, 'y', up)  6.14 us
    all_to_all x2, waiting for transfers between devices, exchange(): return lax.all_to_all(v, axis, split_axis=0, concat_axis=0, tiled=True)  4.58 us
    ppermute x1, starting transfers between devices, half_step(): returned = lax.ppermute(left, SITE, back)  4.13 us
  transfers between devices with their start and end apart: 28, of which 11 were waited for; matrix products, arithmetic and copies ran while one was open for 4% of the time, Pallas kernels for 7%

profile of v3, /device:TPU:0, one launch (start us, length us, event | category | flops | bytes accessed | tf_op | source)
XLA Modules:
  0.0 127.9 jit_solution(4994014266103341911)
XLA Ops:
  1.7 2.1 %collective-permute-start = (bf16[64,2048]{1,0:T(8,128)(2,1)S(1)}, bf16[64,2048]{1,0:T(8,128)(2,1)S(1)}, u32[]{:S(2)}, u32[]{:S(2)}) collective-permute-start(bf16[64,2048]{1,0:T(8,128)(2,1)S(1)} %slice_bitcast_fusion.2), channel_id=1, source_target_pairs={{0,16},{16,32},{32,48},{48,64},{64,80},{80,96},{96,112},{112,0},{1... | collective-permute-start | bytes 786440 | tf_op jit(solution)/shard_map/ppermute | solution.py:441
  5.0 2.5 %split.1 = (bf16[64,1024]{1,0:T(8,128)(2,1)}, bf16[64,1024]{1,0:T(8,128)(2,1)}, bf16[64,1024]{1,0:T(8,128)(2,1)}, bf16[64,1024]{1,0:T(8,128)(2,1)}, bf16[64,1280...) custom-call(s32[7]{0:T(128)} %stack.67.meta, ...), custom_call_target="tpu_custom_call" | custom-call | flops 40000000 | bytes 3000000 | tf_op jit(solution)/shard_map/split/pallas_call | solution.py:50
  17.9 6.6 %collective-permute-done.6 = bf16[64,1024]{1,0:T(8,128)(2,1)S(1)} collective-permute-done((bf16[64,1024]{1,0:T(8,128)(2,1)}, bf16[64,1024]{1,0:T(8,128)(2,1)S(1)}, u32[]{:S(2)}, u32[]{:S(2)}) %collective-permute-start.6) | collective-permute-done | bytes 131104 | tf_op jit(solution)/shard_map/ppermute | solution.py:453
  24.5 2.2 %collective-permute-start.11 = (bf16[64,2048]{1,0:T(8,128)(2,1)}, bf16[64,2048]{1,0:T(8,128)(2,1)S(1)}, u32[]{:S(2)}, u32[]{:S(2)}) collective-permute-start(bf16[64,2048]{1,0:T(8,128)(2,1)} %own.3), channel_id=1, source_target_pairs={{0,2},{2,4},{4,6},{6,0},{1,3},{3,5},{5,7},{7,1},{8,10},{10,12},{12... | collective-permute-start | bytes 786440 | tf_op jit(solution)/shard_map/ppermute | solution.py:442
  26.8 3.3 %collective-permute-start.12 = (bf16[64,2048]{1,0:T(8,128)(2,1)}, bf16[64,2048]{1,0:T(8,128)(2,1)S(1)}, u32[]{:S(2)}, u32[]{:S(2)}) collective-permute-start(bf16[64,2048]{1,0:T(8,128)(2,1)} %own.3), channel_id=1, source_target_pairs={{2,0},{4,2},{6,4},{0,6},{3,1},{5,3},{7,5},{1,7},{10,8},{12,10},{14... | collective-permute-start | bytes 786440 | tf_op jit(solution)/shard_map/ppermute | solution.py:443
  30.1 3.6 %collective-permute-start.8 = (bf16[4,64,1024]{2,1,0:T(8,128)(2,1)S(1)}, bf16[4,64,1024]{2,1,0:T(8,128)(2,1)}, u32[]{:S(2)}, u32[]{:S(2)}) collective-permute-start(bf16[4,64,1024]{2,1,0:T(8,128)(2,1)S(1)} %pad_maximum_fusion.2.p0), channel_id=1, source_target_pairs={{0,8},{8,0},{1,9},{9,1},{2,10},{10,2},{3,11},{11,3},{4,12},{12,4},... | collective-permute-start | bytes 1572872 | tf_op jit(solution)/shard_map/ppermute | solution.py:468
  37.1 3.6 %collective-permute-start.18 = (bf16[5,64,512]{2,1,0:T(8,128)(2,1)S(1)}, bf16[5,64,512]{2,1,0:T(8,128)(2,1)}, u32[]{:S(2)}, u32[]{:S(2)}) collective-permute-start(bf16[5,64,512]{2,1,0:T(8,128)(2,1)S(1)} %pad_maximum_fusion.3.b0), channel_id=1, source_target_pairs={{0,8},{8,0},{1,9},{9,1},{2,10},{10,2},{3,11},{11,3},{4,12},{12,4},... | collective-permute-start | bytes 983048 | tf_op jit(solution)/shard_map/ppermute | solution.py:460
  40.7 2.3 %collective-permute-done.1.a_prev = bf16[2,64,2048]{2,1,0:T(8,128)(2,1)S(1)} collective-permute-done((bf16[2,64,2048]{2,1,0:T(8,128)(2,1)S(1)}, bf16[2,64,2048]{2,1,0:T(8,128)(2,1)S(1)}, u32[]{:S(2)}, u32[]{:S(2)}) %collective-permute-start.1) | collective-permute-done | bytes 524320 | tf_op jit(solution)/shard_map/ppermute | solution.py:472
  43.0 6.1 %collective-permute-done.13.far_low = bf16[64,1024]{1,0:T(8,128)(2,1)S(1)} collective-permute-done((bf16[64,1024]{1,0:T(8,128)(2,1)S(1)}, bf16[64,1024]{1,0:T(8,128)(2,1)S(1)}, u32[]{:S(2)}, u32[]{:S(2)}) %collective-permute-start.13) | collective-permute-done | bytes 131104 | tf_op jit(solution)/shard_map/ppermute | solution.py:465
  51.0 4.0 %collective-permute-done.14.far_high = bf16[64,1024]{1,0:T(8,128)(2,1)S(1)} collective-permute-done((bf16[64,1024]{1,0:T(8,128)(2,1)S(1)}, bf16[64,1024]{1,0:T(8,128)(2,1)S(1)}, u32[]{:S(2)}, u32[]{:S(2)}) %collective-permute-start.14) | collective-permute-done | bytes 131104 | tf_op jit(solution)/shard_map/ppermute | solution.py:466
  55.1 3.2 %collective-permute-start.4 = (bf16[64,2048]{1,0:T(8,128)(2,1)S(1)}, bf16[64,2048]{1,0:T(8,128)(2,1)}, u32[]{:S(2)}, u32[]{:S(2)}) collective-permute-start(bf16[64,2048]{1,0:T(8,128)(2,1)S(1)} %slice_bitcast_fusion), channel_id=1, source_target_pairs={{2,0},{4,2},{6,4},{0,6},{3,1},{5,3},{7,5},{1,7},{10,8},{12,10},{14... | collective-permute-start | bytes 786440 | tf_op jit(solution)/shard_map/ppermute | solution.py:477
  60.0 5.0 %shard_map.130 = (bf16[4,64,256]{2,1,0:T(8,128)(2,1)}, f32[8,8,512]{2,1,0:T(8,128)}, f32[8,8,512]{2,1,0:T(8,128)}) custom-call(s32[7]{0:T(128)} %stack.67.meta, f32[48]{0:T(128)} %pad_maximum_fusion.5.h, bf16[64,2048]{1,0:T(8,128)(2,1)} %own.3, bf16[64,2048]{1,0:T(8,128)(2,1)} %copy-done.13, bf16[64,2048]{1,0:T(8,128)(2,1)} %copy-done.14, ...), custom_call_target="tpu_custom_call" | custom-call | flops 1000000000 | bytes 10000000 | tf_op jit(solution)/shard_map/pallas_call | solution.py:259
  65.8 9.2 %shard_map.131 = (bf16[64,2304]{1,0:T(8,128)(2,1)}, bf16[64,2304]{1,0:T(8,128)(2,1)}, bf16[64,2304]{1,0:T(8,128)(2,1)}, bf16[64,2304]{1,0:T(8,128)(2,1)}, f32[8,72,512]{2,1,0:T(8,128)}, /*index=5*/f32[8,72,512]{2,1,0:T(8,128)}) custom-call(s32[7]{0:T(128)} %stack.67.meta, f32[48]{0:T(128)} %pad_maximum_fusion.5.h, bf16[2,64,2048]{2,1,0:T(8,128)(2,1)} %copy-done.3, ...), custom_call_target="tpu_custom_call" | custom-call | flops 3000000000 | bytes 10000000 | tf_op jit(solution)/shard_map/pallas_call | solution.py:259
  75.2 2.2 %collective-permute-start.22 = (bf16[64,2304]{1,0:T(8,128)(2,1)}, bf16[64,2304]{1,0:T(8,128)(2,1)S(1)}, u32[]{:S(2)}, u32[]{:S(2)}) collective-permute-start(bf16[64,2304]{1,0:T(8,128)(2,1)} %get-tuple-element.36), channel_id=1, source_target_pairs={{2,0},{4,2},{6,4},{0,6},{3,1},{5,3},{7,5},{1,7},{10,8},{12,10},{14... | collective-permute-start | bytes 884744 | tf_op jit(solution)/shard_map/ppermute | solution.py:486
  78.9 2.3 %add_convert_fusion = bf16[8,72,512]{2,1,0:T(8,128)(2,1)} fusion(f32[8,72,512]{2,1,0:T(8,128)} %get-tuple-element.33, f32[8,72,512]{2,1,0:T(8,128)S(1)} %collective-permute-done.21), kind=kLoop, calls=%fused_computation | loop fusion | flops 589824 | bytes 2949120 | tf_op jit(solution)/shard_map/convert_element_type | solution.py:489
  81.2 7.0 %all-to-all-start = ((bf16[8,72,512]{2,1,0:T(8,128)(2,1)}), bf16[8,72,512]{2,1,0:T(8,128)(2,1)S(1)}, u32[]{:S(2)}, u32[]{:S(2)}) async-start(bf16[8,72,512]{2,1,0:T(8,128)(2,1)} %add_convert_fusion), calls=%async_computation | async-start | bytes 1179648 | tf_op jit(solution)/shard_map/all_to_all | solution.py:437
  88.2 3.1 %collective-permute-done.22 = bf16[64,2304]{1,0:T(8,128)(2,1)S(1)} collective-permute-done((bf16[64,2304]{1,0:T(8,128)(2,1)}, bf16[64,2304]{1,0:T(8,128)(2,1)S(1)}, u32[]{:S(2)}, u32[]{:S(2)}) %collective-permute-start.22) | collective-permute-done | bytes 294944 | tf_op jit(solution)/shard_map/ppermute | solution.py:486
  91.3 6.9 %collective-permute-done.23 = bf16[64,2304]{1,0:T(8,128)(2,1)S(1)} collective-permute-done((bf16[64,2304]{1,0:T(8,128)(2,1)}, bf16[64,2304]{1,0:T(8,128)(2,1)S(1)}, u32[]{:S(2)}, u32[]{:S(2)}) %collective-permute-start.23) | collective-permute-done | bytes 294944 | tf_op jit(solution)/shard_map/ppermute | solution.py:487
  98.9 4.6 %all-to-all-done.got = bf16[8,72,512]{2,1,0:T(8,128)(2,1)S(1)} async-done(((bf16[8,72,512]{2,1,0:T(8,128)(2,1)}), bf16[8,72,512]{2,1,0:T(8,128)(2,1)S(1)}, u32[]{:S(2)}, u32[]{:S(2)}) %all-to-all-start) | async-done | bytes 589856 | tf_op jit(solution)/shard_map/all_to_all | solution.py:437
  106.1 3.5 %all-to-all-start.1 = ((bf16[8,64,512]{2,1,0:T(8,128)(2,1)}), bf16[8,64,512]{2,1,0:T(8,128)(2,1)S(1)}, u32[]{:S(2)}, u32[]{:S(2)}) async-start(bf16[8,64,512]{2,1,0:T(8,128)(2,1)} %finish.1), calls=%async_computation.1 | async-start | bytes 1048576 | tf_op jit(solution)/shard_map/all_to_all | solution.py:437
  109.6 4.1 %collective-permute-start.25 = (bf16[64,2048]{1,0:T(8,128)(2,1)S(1)}, bf16[64,2048]{1,0:T(8,128)(2,1)S(1)}, u32[]{:S(2)}, u32[]{:S(2)}) collective-permute-start(bf16[64,2048]{1,0:T(8,128)(2,1)S(1)} %fusion), channel_id=1, source_target_pairs={{16,0},{32,16},{48,32},{64,48},{80,64},{96,80},{112,96},{0,112},{1... | collective-permute-start | bytes 786440 | tf_op jit(solution)/shard_map/ppermute | solution.py:495
  113.7 8.7 %collective-permute-done.25.returned = bf16[64,2048]{1,0:T(8,128)(2,1)S(1)} collective-permute-done((bf16[64,2048]{1,0:T(8,128)(2,1)S(1)}, bf16[64,2048]{1,0:T(8,128)(2,1)S(1)}, u32[]{:S(2)}, u32[]{:S(2)}) %collective-permute-start.25) | collective-permute-done | bytes 262176 | tf_op jit(solution)/shard_map/ppermute | solution.py:495
  123.2 2.0 %join.1 = bf16[2,64,2048]{2,1,0:T(8,128)(2,1)} custom-call(s32[7]{0:T(128)} %stack.67.meta, bf16[8,72,512]{2,1,0:T(8,128)(2,1)} %copy-done, bf16[64,2048]{1,0:T(8,128)(2,1)} %copy-done.7), custom_call_target="tpu_custom_call" | custom-call | flops 1000000 | bytes 1300000 | tf_op jit(solution)/shard_map/join/pallas_call | solution.py:390
  126.0 1.9 %spread.1 = (bf16[64,2048]{1,0:T(8,128)(2,1)}, bf16[64,2048]{1,0:T(8,128)(2,1)}) custom-call(bf16[8,64,512]{2,1,0:T(8,128)(2,1)} %copy-done.1), custom_call_target="tpu_custom_call" | custom-call | flops 1000000 | bytes 1000000 | tf_op jit(solution)/shard_map/spread/pallas_call | solution.py:313
  (103 shorter events, 25.5 us)
Async XLA Ops:
  1.7 15.5 %collective-permute-start = (bf16[64,2048]{1,0:T(8,128)(2,1)S(1)}, bf16[64,2048]{1,0:T(8,128)(2,1)S(1)}, u32[]{:S(2)}, u32[]{:S(2)}) collective-permute-start(bf16[64,2048]{1,0:T(8,128)(2,1)S(1)} %slice_bitcast_fusion.2), channel_id=1, source_target_pairs={{0,16},{16,32},{32,48},{48,64},{64,80},{80,96},{96,112},{112,0},{1... | collective-permute-start | bytes 786440 | tf_op jit(solution)/shard_map/ppermute | solution.py:441
  7.5 7.9 %collective-permute-start.5 = (bf16[64,1024]{1,0:T(8,128)(2,1)}, bf16[64,1024]{1,0:T(8,128)(2,1)S(1)}, u32[]{:S(2)}, u32[]{:S(2)}) collective-permute-start(bf16[64,1024]{1,0:T(8,128)(2,1)} %get-tuple-element.23), channel_id=1, source_target_pairs={{0,2},{2,4},{4,6},{6,0},{1,3},{3,5},{5,7},{7,1},{8,10},{10,12},{12... | collective-permute-start | bytes 393224 | tf_op jit(solution)/shard_map/ppermute | solution.py:452
  9.2 17.6 %collective-permute-start.15 = (bf16[64,1280]{1,0:T(8,128)(2,1)}, bf16[64,1280]{1,0:T(8,128)(2,1)S(1)}, u32[]{:S(2)}, u32[]{:S(2)}) collective-permute-start(bf16[64,1280]{1,0:T(8,128)(2,1)} %get-tuple-element.27), channel_id=1, source_target_pairs={{0,2},{2,4},{4,6},{6,0},{1,3},{3,5},{5,7},{7,1},{8,10},{10,12},{12... | collective-permute-start | bytes 491528 | tf_op jit(solution)/shard_map/ppermute | solution.py:449
  10.8 19.3 %collective-permute-start.16 = (bf16[64,1280]{1,0:T(8,128)(2,1)}, bf16[64,1280]{1,0:T(8,128)(2,1)S(1)}, u32[]{:S(2)}, u32[]{:S(2)}) collective-permute-start(bf16[64,1280]{1,0:T(8,128)(2,1)} %get-tuple-element.28), channel_id=1, source_target_pairs={{2,0},{4,2},{6,4},{0,6},{3,1},{5,3},{7,5},{1,7},{10,8},{12,10},{14... | collective-permute-start | bytes 491528 | tf_op jit(solution)/shard_map/ppermute | solution.py:450
  12.4 21.3 %collective-permute-start.17 = (bf16[64,1280]{1,0:T(8,128)(2,1)}, bf16[64,1280]{1,0:T(8,128)(2,1)S(1)}, u32[]{:S(2)}, u32[]{:S(2)}) collective-permute-start(bf16[64,1280]{1,0:T(8,128)(2,1)} %get-tuple-element.29), channel_id=1, source_target_pairs={{0,4},{2,6},{4,0},{6,2},{1,5},{3,7},{5,1},{7,3},{8,12},{10,14},{12... | collective-permute-start | bytes 491528 | tf_op jit(solution)/shard_map/ppermute | solution.py:451
  15.4 9.1 %collective-permute-start.6 = (bf16[64,1024]{1,0:T(8,128)(2,1)}, bf16[64,1024]{1,0:T(8,128)(2,1)S(1)}, u32[]{:S(2)}, u32[]{:S(2)}) collective-permute-start(bf16[64,1024]{1,0:T(8,128)(2,1)} %get-tuple-element.24), channel_id=1, source_target_pairs={{2,0},{4,2},{6,4},{0,6},{3,1},{5,3},{7,5},{1,7},{10,8},{12,10},{14... | collective-permute-start | bytes 393224 | tf_op jit(solution)/shard_map/ppermute | solution.py:453
  17.2 9.5 %collective-permute-start.7 = (bf16[64,1024]{1,0:T(8,128)(2,1)}, bf16[64,1024]{1,0:T(8,128)(2,1)S(1)}, u32[]{:S(2)}, u32[]{:S(2)}) collective-permute-start(bf16[64,1024]{1,0:T(8,128)(2,1)} %get-tuple-element.25), channel_id=1, source_target_pairs={{0,4},{2,6},{4,0},{6,2},{1,5},{3,7},{5,1},{7,3},{8,12},{10,14},{12... | collective-permute-start | bytes 393224 | tf_op jit(solution)/shard_map/ppermute | solution.py:454
  24.5 10.9 %collective-permute-start.11 = (bf16[64,2048]{1,0:T(8,128)(2,1)}, bf16[64,2048]{1,0:T(8,128)(2,1)S(1)}, u32[]{:S(2)}, u32[]{:S(2)}) collective-permute-start(bf16[64,2048]{1,0:T(8,128)(2,1)} %own.3), channel_id=1, source_target_pairs={{0,2},{2,4},{4,6},{6,0},{1,3},{3,5},{5,7},{7,1},{8,10},{10,12},{12... | collective-permute-start | bytes 786440 | tf_op jit(solution)/shard_map/ppermute | solution.py:442
  26.7 16.3 %collective-permute-start.1 = (bf16[2,64,2048]{2,1,0:T(8,128)(2,1)S(1)}, bf16[2,64,2048]{2,1,0:T(8,128)(2,1)S(1)}, u32[]{:S(2)}, u32[]{:S(2)}) collective-permute-start(bf16[2,64,2048]{2,1,0:T(8,128)(2,1)S(1)} %pad_maximum_fusion.1.a_own), channel_id=1, source_target_pairs={{0,2},{2,4},{4,6},{6,0},{1,3},{3,5},{5,7},{7,1},{8,10},{10,12},{12... | collective-permute-start | bytes 1572872 | tf_op jit(solution)/shard_map/ppermute | solution.py:472
  26.8 10.3 %collective-permute-start.12 = (bf16[64,2048]{1,0:T(8,128)(2,1)}, bf16[64,2048]{1,0:T(8,128)(2,1)S(1)}, u32[]{:S(2)}, u32[]{:S(2)}) collective-permute-start(bf16[64,2048]{1,0:T(8,128)(2,1)} %own.3), channel_id=1, source_target_pairs={{2,0},{4,2},{6,4},{0,6},{3,1},{5,3},{7,5},{1,7},{10,8},{12,10},{14... | collective-permute-start | bytes 786440 | tf_op jit(solution)/shard_map/ppermute | solution.py:443
  30.1 19.1 %collective-permute-start.8 = (bf16[4,64,1024]{2,1,0:T(8,128)(2,1)S(1)}, bf16[4,64,1024]{2,1,0:T(8,128)(2,1)}, u32[]{:S(2)}, u32[]{:S(2)}) collective-permute-start(bf16[4,64,1024]{2,1,0:T(8,128)(2,1)S(1)} %pad_maximum_fusion.2.p0), channel_id=1, source_target_pairs={{0,8},{8,0},{1,9},{9,1},{2,10},{10,2},{3,11},{11,3},{4,12},{12,4},... | collective-permute-start | bytes 1572872 | tf_op jit(solution)/shard_map/ppermute | solution.py:468
  33.9 16.6 %collective-permute-start.2 = (bf16[2,64,2048]{2,1,0:T(8,128)(2,1)S(1)}, bf16[2,64,2048]{2,1,0:T(8,128)(2,1)S(1)}, u32[]{:S(2)}, u32[]{:S(2)}) collective-permute-start(bf16[2,64,2048]{2,1,0:T(8,128)(2,1)S(1)} %pad_maximum_fusion.1.a_own), channel_id=1, source_target_pairs={{2,0},{4,2},{6,4},{0,6},{3,1},{5,3},{7,5},{1,7},{10,8},{12,10},{14... | collective-permute-start | bytes 1572872 | tf_op jit(solution)/shard_map/ppermute | solution.py:473
  35.4 29.5 %collective-permute-start.9 = (bf16[4,64,1024]{2,1,0:T(8,128)(2,1)S(1)}, bf16[4,64,1024]{2,1,0:T(8,128)(2,1)}, u32[]{:S(2)}, u32[]{:S(2)}) collective-permute-start(bf16[4,64,1024]{2,1,0:T(8,128)(2,1)S(1)} %pad_maximum_fusion.2.p0), channel_id=1, source_target_pairs={{0,1},{1,0},{2,3},{3,2},{4,5},{5,4},{6,7},{7,6},{8,9},{9,8},{10,11... | collective-permute-start | bytes 1572872 | tf_op jit(solution)/shard_map/ppermute | solution.py:469
  37.1 13.5 %collective-permute-start.18 = (bf16[5,64,512]{2,1,0:T(8,128)(2,1)S(1)}, bf16[5,64,512]{2,1,0:T(8,128)(2,1)}, u32[]{:S(2)}, u32[]{:S(2)}) collective-permute-start(bf16[5,64,512]{2,1,0:T(8,128)(2,1)S(1)} %pad_maximum_fusion.3.b0), channel_id=1, source_target_pairs={{0,8},{8,0},{1,9},{9,1},{2,10},{10,2},{3,11},{11,3},{4,12},{12,4},... | collective-permute-start | bytes 983048 | tf_op jit(solution)/shard_map/ppermute | solution.py:460
  50.4 14.6 %collective-permute-start.10 = (bf16[4,64,1024]{2,1,0:T(8,128)(2,1)}, bf16[4,64,1024]{2,1,0:T(8,128)(2,1)S(1)}, u32[]{:S(2)}, u32[]{:S(2)}) collective-permute-start(bf16[4,64,1024]{2,1,0:T(8,128)(2,1)} %collective-permute-done.8.p1), channel_id=1, source_target_pairs={{0,1},{1,0},{2,3},{3,2},{4,5},{5,4},{6,7},{7,6},{8,9},{9,8},{10,11... | collective-permute-start | bytes 1572872 | tf_op jit(solution)/shard_map/ppermute | solution.py:470
  50.6 8.6 %collective-permute-start.20 = (bf16[5,64,512]{2,1,0:T(8,128)(2,1)}, bf16[5,64,512]{2,1,0:T(8,128)(2,1)S(1)}, u32[]{:S(2)}, u32[]{:S(2)}) collective-permute-start(bf16[5,64,512]{2,1,0:T(8,128)(2,1)} %collective-permute-done.18.b1), channel_id=1, source_target_pairs={{0,1},{1,0},{2,3},{3,2},{4,5},{5,4},{6,7},{7,6},{8,9},{9,8},{10,11... | collective-permute-start | bytes 983048 | tf_op jit(solution)/shard_map/ppermute | solution.py:462
  55.1 9.9 %collective-permute-start.3 = (bf16[64,2048]{1,0:T(8,128)(2,1)S(1)}, bf16[64,2048]{1,0:T(8,128)(2,1)}, u32[]{:S(2)}, u32[]{:S(2)}) collective-permute-start(bf16[64,2048]{1,0:T(8,128)(2,1)S(1)} %slice_bitcast_fusion.1), channel_id=1, source_target_pairs={{0,2},{2,4},{4,6},{6,0},{1,3},{3,5},{5,7},{7,1},{8,10},{10,12},{12... | collective-permute-start | bytes 786440 | tf_op jit(solution)/shard_map/ppermute | solution.py:476
  55.1 9.9 %collective-permute-start.4 = (bf16[64,2048]{1,0:T(8,128)(2,1)S(1)}, bf16[64,2048]{1,0:T(8,128)(2,1)}, u32[]{:S(2)}, u32[]{:S(2)}) collective-permute-start(bf16[64,2048]{1,0:T(8,128)(2,1)S(1)} %slice_bitcast_fusion), channel_id=1, source_target_pairs={{2,0},{4,2},{6,4},{0,6},{3,1},{5,3},{7,5},{1,7},{10,8},{12,10},{14... | collective-permute-start | bytes 786440 | tf_op jit(solution)/shard_map/ppermute | solution.py:477
  75.2 16.1 %collective-permute-start.22 = (bf16[64,2304]{1,0:T(8,128)(2,1)}, bf16[64,2304]{1,0:T(8,128)(2,1)S(1)}, u32[]{:S(2)}, u32[]{:S(2)}) collective-permute-start(bf16[64,2304]{1,0:T(8,128)(2,1)} %get-tuple-element.36), channel_id=1, source_target_pairs={{2,0},{4,2},{6,4},{0,6},{3,1},{5,3},{7,5},{1,7},{10,8},{12,10},{14... | collective-permute-start | bytes 884744 | tf_op jit(solution)/shard_map/ppermute | solution.py:486
  77.4 20.8 %collective-permute-start.23 = (bf16[64,2304]{1,0:T(8,128)(2,1)}, bf16[64,2304]{1,0:T(8,128)(2,1)S(1)}, u32[]{:S(2)}, u32[]{:S(2)}) collective-permute-start(bf16[64,2304]{1,0:T(8,128)(2,1)} %get-tuple-element.37), channel_id=1, source_target_pairs={{0,2},{2,4},{4,6},{6,0},{1,3},{3,5},{5,7},{7,1},{8,10},{10,12},{12... | collective-permute-start | bytes 884744 | tf_op jit(solution)/shard_map/ppermute | solution.py:487
  77.4 20.8 %collective-permute-start.24 = (bf16[64,2304]{1,0:T(8,128)(2,1)}, bf16[64,2304]{1,0:T(8,128)(2,1)S(1)}, u32[]{:S(2)}, u32[]{:S(2)}) collective-permute-start(bf16[64,2304]{1,0:T(8,128)(2,1)} %get-tuple-element.38), channel_id=1, source_target_pairs={{0,4},{2,6},{4,0},{6,2},{1,5},{3,7},{5,1},{7,3},{8,12},{10,14},{12... | collective-permute-start | bytes 884744 | tf_op jit(solution)/shard_map/ppermute | solution.py:488
  81.2 22.3 %all-to-all-start = ((bf16[8,72,512]{2,1,0:T(8,128)(2,1)}), bf16[8,72,512]{2,1,0:T(8,128)(2,1)S(1)}, u32[]{:S(2)}, u32[]{:S(2)}) async-start(bf16[8,72,512]{2,1,0:T(8,128)(2,1)} %add_convert_fusion), calls=%async_computation | async-start | bytes 1179648 | tf_op jit(solution)/shard_map/all_to_all | solution.py:437
  106.1 19.1 %all-to-all-start.1 = ((bf16[8,64,512]{2,1,0:T(8,128)(2,1)}), bf16[8,64,512]{2,1,0:T(8,128)(2,1)S(1)}, u32[]{:S(2)}, u32[]{:S(2)}) async-start(bf16[8,64,512]{2,1,0:T(8,128)(2,1)} %finish.1), calls=%async_computation.1 | async-start | bytes 1048576 | tf_op jit(solution)/shard_map/all_to_all | solution.py:437
  109.6 12.9 %collective-permute-start.25 = (bf16[64,2048]{1,0:T(8,128)(2,1)S(1)}, bf16[64,2048]{1,0:T(8,128)(2,1)S(1)}, u32[]{:S(2)}, u32[]{:S(2)}) collective-permute-start(bf16[64,2048]{1,0:T(8,128)(2,1)S(1)} %fusion), channel_id=1, source_target_pairs={{16,0},{32,16},{48,32},{64,48},{80,64},{96,80},{112,96},{0,112},{1... | collective-permute-start | bytes 786440 | tf_op jit(solution)/shard_map/ppermute | solution.py:495
  (25 other events, 285.9 us)

commit v4 on v3

--- a/solution.py
+++ b/solution.py
@@ -9,7 +9,7 @@
 
 SITE = ("x", "zl")
 BOND = ("zh", "y", "c")
-VMEM_BYTES = 60 * 1024 * 1024
+VMEM_BYTES = 18 * 1024 * 1024
 F32 = jnp.float32
 BF16 = jnp.bfloat16
 
@@ -19,9 +19,10 @@
 
 
 def split_kernel(
-    meta, site, edge, proj, bulk, bulk_proj, bulk_left, w_0, w_1, w_2, w_3, b_0, b_1, b_2, b_3
+    site, edge, proj, bulk, bulk_proj, bulk_left, w_0, w_1, w_2, w_3, b_0, b_1, b_2, b_3
 ):
-    me, first, g = meta[2], meta[3], meta[4]
+    me = lax.axis_index("y")
+    g = 2 * lax.axis_index("x") + lax.axis_index("zl")
     quarter, width = 256, 1024
     column = lax.broadcasted_iota(jnp.int32, (width, 128), 1)
     source = (column // 8) * 64 + g * 8 + column % 8
@@ -39,12 +40,11 @@
             high = slice((2 + t) * quarter, (3 + t) * quarter)
             w_ref[:, low] = site[0, :, cols]
             b_ref[:, low] = bulk[:, cols]
-            w_ref[:, high] = jnp.where(first == 1, edge[:, cols], proj[0, :, cols])
+            w_ref[:, high] = jnp.where(g == 0, edge[:, cols], proj[0, :, cols])
             b_ref[:, high] = bulk_proj[:, cols]
 
 
-def split(meta, sites, edge, proj, bulk, bulk_proj, bulk_left):
-    smem = pl.BlockSpec(memory_space=pltpu.SMEM)
+def split(sites, edge, proj, bulk, bulk_proj, bulk_left):
     one = pl.BlockSpec((1, 64, 2048), lambda i: (0, 0, 0))
     flat = pl.BlockSpec((64, 2048), lambda i: (0, 0))
     return pl.pallas_call(
@@ -52,14 +52,14 @@
         grid=(1,),
         out_shape=(jax.ShapeDtypeStruct((64, 1024), BF16),) * 4
         + (jax.ShapeDtypeStruct((64, 1280), BF16),) * 4,
-        in_specs=[smem, one, flat, one, flat, flat, flat],
+        in_specs=[one, flat, one, flat, flat, flat],
         out_specs=(pl.BlockSpec((64, 1024), lambda i: (0, 0)),) * 4
         + (pl.BlockSpec((64, 1280), lambda i: (0, 0)),) * 4,
         cost_estimate=pl.CostEstimate(
             flops=40_000_000, bytes_accessed=3_000_000, transcendentals=0
         ),
         name="split",
-    )(meta, sites, edge, proj, bulk, bulk_proj, bulk_left)
+    )(sites, edge, proj, bulk, bulk_proj, bulk_left)
 
 
 def theta(h, base, x_of, y_part, raw, out):
@@ -290,6 +290,7 @@
         out_specs=pl.BlockSpec((8, 64, 512), lambda i: (0, 0, 0)),
         out_shape=jax.ShapeDtypeStruct((8, 64, 512), BF16),
         cost_estimate=pl.CostEstimate(flops=1_000_000, bytes_accessed=700_000, transcendentals=0),
+        compiler_params=pltpu.CompilerParams(vmem_limit_bytes=8 * 1024 * 1024),
         name="finish",
     )(left, got)
 
@@ -314,6 +315,7 @@
         spread_kernel,
         out_shape=(rows, rows),
         cost_estimate=pl.CostEstimate(flops=1_000_000, bytes_accessed=1_000_000, transcendentals=0),
+        compiler_params=pltpu.CompilerParams(vmem_limit_bytes=8 * 1024 * 1024),
         name="spread",
     )(ends)
 
@@ -393,6 +395,7 @@
         in_specs=[pl.BlockSpec(memory_space=pltpu.SMEM), vmem, vmem],
         out_specs=vmem,
         cost_estimate=pl.CostEstimate(flops=1_000_000, bytes_accessed=1_300_000, transcendentals=0),
+        compiler_params=pltpu.CompilerParams(vmem_limit_bytes=8 * 1024 * 1024),
         name="join",
     )(meta, got, returned)
 
@@ -444,7 +447,7 @@
 
     across = [(k, (k + 2) % ny) for k in range(ny)]
     w_0, w_1, w_2, w_3, b_0, b_1, b_2, b_3 = split(
-        meta, sites, edge_right, proj_right, bulk_first, bulk_right_proj, bulk_left_proj
+        sites, edge_right, proj_right, bulk_first, bulk_right_proj, bulk_left_proj
     )
     b_1 = lax.ppermute(b_1, "y", up)
     b_2 = lax.ppermute(b_2, "y", down)

time: 128 us -> 123 us (0.961)
  Pallas kernels: 22.4 us -> 17.5 us
  other arithmetic: 3.33 us -> 1.51 us
  local copies, waits for them, and re-layouts: 6.43 us -> 8.02 us
    ppermute x1, waiting for transfers between devices: 6.89 us -> 10.9 us  [half_step(): left_up = lax.ppermute(left_up, 'y', up)]
    ppermute x1, waiting for transfers between devices: 3.07 us -> 0.01 us  [half_step(): left_down = lax.ppermute(left_down, 'y', down)]
    pallas_call x2, Pallas kernels: 14.2 us -> 11.8 us  [call(): pl.pallas_call(kernel, out_shape=outs, in_specs=[smem, smem] + [anywhere]...]
    unnamed x42 -> x28, local copies, waits for them, and re-layouts: 3.88 us -> 5.18 us
  transfers between devices with their start and end apart: 28 -> 28, of which waited for: 11 -> 10; matrix products, arithmetic and copies ran while one was open for 4% -> 3% of each run, Pallas kernels for 7% -> 7%
where the time goes in v4:
time: 123 us
  starting transfers between devices  46.8 us (38%)
  waiting for transfers between devices  46.8 us (38%)
  Pallas kernels  17.5 us (14%)
  local copies, waits for them, and re-layouts  8.02 us (7%)
  between operations  2.19 us (2%)
  other arithmetic  1.51 us (1%)
    pallas_call x2, Pallas kernels, call(): pl.pallas_call(kernel, out_shape=outs, in_specs=[smem, smem] + [anywhere]...  11.8 us
    ppermute x1, waiting for transfers between devices, half_step(): left_up = lax.ppermute(left_up, 'y', up)  10.9 us
    all_to_all x2, starting transfers between devices, exchange(): return lax.all_to_all(v, axis, split_axis=0, concat_axis=0, tiled=True)  10.8 us
    ppermute x1, waiting for transfers between devices, half_step(): returned = lax.ppermute(left, SITE, back)  8.73 us
    ppermute x1, waiting for transfers between devices, half_step(): w_2 = lax.ppermute(w_2, 'y', down)  6.63 us
    all_to_all x2, waiting for transfers between devices, exchange(): return lax.all_to_all(v, axis, split_axis=0, concat_axis=0, tiled=True)  5.7 us
    ppermute x1, waiting for transfers between devices, half_step(): b_low = lax.ppermute(b_low, 'y', up)  5.45 us
    unnamed x28, local copies, waits for them, and re-layouts  5.18 us
  transfers between devices with their start and end apart: 28, of which 10 were waited for; matrix products, arithmetic and copies ran while one was open for 3% of the time, Pallas kernels for 7%

profile of v4, /device:TPU:0, one launch (start us, length us, event | category | flops | bytes accessed | tf_op | source)
XLA Modules:
  0.0 122.8 jit_solution(11093215226634205543)
XLA Ops:
  1.7 2.1 %collective-permute-start = (bf16[64,2048]{1,0:T(8,128)(2,1)S(1)}, bf16[64,2048]{1,0:T(8,128)(2,1)S(1)}, u32[]{:S(2)}, u32[]{:S(2)}) collective-permute-start(bf16[64,2048]{1,0:T(8,128)(2,1)S(1)} %slice_bitcast_fusion.2), channel_id=1, source_target_pairs={{0,16},{16,32},{32,48},{48,64},{64,80},{80,96},{96,112},{112,0},{1... | collective-permute-start | bytes 786440 | tf_op jit(solution)/shard_map/ppermute | solution.py:444
  3.8 2.6 %split.1 = (bf16[64,1024]{1,0:T(8,128)(2,1)}, bf16[64,1024]{1,0:T(8,128)(2,1)}, bf16[64,1024]{1,0:T(8,128)(2,1)}, bf16[64,1024]{1,0:T(8,128)(2,1)}, bf16[64,1280...) custom-call(bf16[2,64,2048]{2,1,0:T(8,128)(2,1)} %site.1, ...), custom_call_target="tpu_custom_call" | custom-call | flops 40000000 | bytes 3000000 | tf_op jit(solution)/shard_map/split/pallas_call | solution.py:50
  6.3 1.6 %collective-permute-start.5 = (bf16[64,1024]{1,0:T(8,128)(2,1)}, bf16[64,1024]{1,0:T(8,128)(2,1)S(1)}, u32[]{:S(2)}, u32[]{:S(2)}) collective-permute-start(bf16[64,1024]{1,0:T(8,128)(2,1)} %get-tuple-element.23), channel_id=1, source_target_pairs={{0,2},{2,4},{4,6},{6,0},{1,3},{3,5},{5,7},{7,1},{8,10},{10,12},{12... | collective-permute-start | bytes 393224 | tf_op jit(solution)/shard_map/ppermute | solution.py:455
  9.5 1.7 %collective-permute-start.16 = (bf16[64,1280]{1,0:T(8,128)(2,1)}, bf16[64,1280]{1,0:T(8,128)(2,1)S(1)}, u32[]{:S(2)}, u32[]{:S(2)}) collective-permute-start(bf16[64,1280]{1,0:T(8,128)(2,1)} %get-tuple-element.28), channel_id=1, source_target_pairs={{2,0},{4,2},{6,4},{0,6},{3,1},{5,3},{7,5},{1,7},{10,8},{12,10},{14... | collective-permute-start | bytes 491528 | tf_op jit(solution)/shard_map/ppermute | solution.py:453
  11.2 1.7 %collective-permute-start.17 = (bf16[64,1280]{1,0:T(8,128)(2,1)}, bf16[64,1280]{1,0:T(8,128)(2,1)S(1)}, u32[]{:S(2)}, u32[]{:S(2)}) collective-permute-start(bf16[64,1280]{1,0:T(8,128)(2,1)} %get-tuple-element.29), channel_id=1, source_target_pairs={{0,4},{2,6},{4,0},{6,2},{1,5},{3,7},{5,1},{7,3},{8,12},{10,14},{12... | collective-permute-start | bytes 491528 | tf_op jit(solution)/shard_map/ppermute | solution.py:454
  14.2 1.8 %collective-permute-start.6 = (bf16[64,1024]{1,0:T(8,128)(2,1)}, bf16[64,1024]{1,0:T(8,128)(2,1)S(1)}, u32[]{:S(2)}, u32[]{:S(2)}) collective-permute-start(bf16[64,1024]{1,0:T(8,128)(2,1)} %get-tuple-element.24), channel_id=1, source_target_pairs={{2,0},{4,2},{6,4},{0,6},{3,1},{5,3},{7,5},{1,7},{10,8},{12,10},{14... | collective-permute-start | bytes 393224 | tf_op jit(solution)/shard_map/ppermute | solution.py:456
  16.7 6.6 %collective-permute-done.6 = bf16[64,1024]{1,0:T(8,128)(2,1)S(1)} collective-permute-done((bf16[64,1024]{1,0:T(8,128)(2,1)}, bf16[64,1024]{1,0:T(8,128)(2,1)S(1)}, u32[]{:S(2)}, u32[]{:S(2)}) %collective-permute-start.6) | collective-permute-done | bytes 131104 | tf_op jit(solution)/shard_map/ppermute | solution.py:456
  23.3 2.2 %collective-permute-start.11 = (bf16[64,2048]{1,0:T(8,128)(2,1)}, bf16[64,2048]{1,0:T(8,128)(2,1)S(1)}, u32[]{:S(2)}, u32[]{:S(2)}) collective-permute-start(bf16[64,2048]{1,0:T(8,128)(2,1)} %own.3), channel_id=1, source_target_pairs={{0,2},{2,4},{4,6},{6,0},{1,3},{3,5},{5,7},{7,1},{8,10},{10,12},{12... | collective-permute-start | bytes 786440 | tf_op jit(solution)/shard_map/ppermute | solution.py:445
  25.6 3.3 %collective-permute-start.12 = (bf16[64,2048]{1,0:T(8,128)(2,1)}, bf16[64,2048]{1,0:T(8,128)(2,1)S(1)}, u32[]{:S(2)}, u32[]{:S(2)}) collective-permute-start(bf16[64,2048]{1,0:T(8,128)(2,1)} %own.3), channel_id=1, source_target_pairs={{2,0},{4,2},{6,4},{0,6},{3,1},{5,3},{7,5},{1,7},{10,8},{12,10},{14... | collective-permute-start | bytes 786440 | tf_op jit(solution)/shard_map/ppermute | solution.py:446
  28.9 3.6 %collective-permute-start.8 = (bf16[4,64,1024]{2,1,0:T(8,128)(2,1)S(1)}, bf16[4,64,1024]{2,1,0:T(8,128)(2,1)}, u32[]{:S(2)}, u32[]{:S(2)}) collective-permute-start(bf16[4,64,1024]{2,1,0:T(8,128)(2,1)S(1)} %pad_maximum_fusion.2.p0), channel_id=1, source_target_pairs={{0,8},{8,0},{1,9},{9,1},{2,10},{10,2},{3,11},{11,3},{4,12},{12,4},... | collective-permute-start | bytes 1572872 | tf_op jit(solution)/shard_map/ppermute | solution.py:471
  34.2 1.7 %collective-permute-done.12.after = bf16[64,2048]{1,0:T(8,128)(2,1)S(1)} collective-permute-done((bf16[64,2048]{1,0:T(8,128)(2,1)}, bf16[64,2048]{1,0:T(8,128)(2,1)S(1)}, u32[]{:S(2)}, u32[]{:S(2)}) %collective-permute-start.12) | collective-permute-done | bytes 262176 | tf_op jit(solution)/shard_map/ppermute | solution.py:446
  35.9 3.6 %collective-permute-start.18 = (bf16[5,64,512]{2,1,0:T(8,128)(2,1)S(1)}, bf16[5,64,512]{2,1,0:T(8,128)(2,1)}, u32[]{:S(2)}, u32[]{:S(2)}) collective-permute-start(bf16[5,64,512]{2,1,0:T(8,128)(2,1)S(1)} %pad_maximum_fusion.3.b0), channel_id=1, source_target_pairs={{0,8},{8,0},{1,9},{9,1},{2,10},{10,2},{3,11},{11,3},{4,12},{12,4},... | collective-permute-start | bytes 983048 | tf_op jit(solution)/shard_map/ppermute | solution.py:463
  39.5 2.3 %collective-permute-done.1.a_prev = bf16[2,64,2048]{2,1,0:T(8,128)(2,1)S(1)} collective-permute-done((bf16[2,64,2048]{2,1,0:T(8,128)(2,1)S(1)}, bf16[2,64,2048]{2,1,0:T(8,128)(2,1)S(1)}, u32[]{:S(2)}, u32[]{:S(2)}) %collective-permute-start.1) | collective-permute-done | bytes 524320 | tf_op jit(solution)/shard_map/ppermute | solution.py:475
  42.5 5.5 %collective-permute-done.13.far_low = bf16[64,1024]{1,0:T(8,128)(2,1)S(1)} collective-permute-done((bf16[64,1024]{1,0:T(8,128)(2,1)S(1)}, bf16[64,1024]{1,0:T(8,128)(2,1)S(1)}, u32[]{:S(2)}, u32[]{:S(2)}) %collective-permute-start.13) | collective-permute-done | bytes 131104 | tf_op jit(solution)/shard_map/ppermute | solution.py:468
  50.4 3.5 %collective-permute-done.14.far_high = bf16[64,1024]{1,0:T(8,128)(2,1)S(1)} collective-permute-done((bf16[64,1024]{1,0:T(8,128)(2,1)S(1)}, bf16[64,1024]{1,0:T(8,128)(2,1)S(1)}, u32[]{:S(2)}, u32[]{:S(2)}) %collective-permute-start.14) | collective-permute-done | bytes 131104 | tf_op jit(solution)/shard_map/ppermute | solution.py:469
  55.2 3.2 %collective-permute-start.4 = (bf16[64,2048]{1,0:T(8,128)(2,1)}, bf16[64,2048]{1,0:T(8,128)(2,1)}, u32[]{:S(2)}, u32[]{:S(2)}) collective-permute-start(bf16[64,2048]{1,0:T(8,128)(2,1)} %slice_bitcast_fusion), channel_id=1, source_target_pairs={{2,0},{4,2},{6,4},{0,6},{3,1},{5,3},{7,5},{1,7},{10,8},{12,10},{14... | collective-permute-start | bytes 786440 | tf_op jit(solution)/shard_map/ppermute | solution.py:480
  62.4 4.5 %shard_map.130 = (bf16[4,64,256]{2,1,0:T(8,128)(2,1)S(1)}, f32[8,8,512]{2,1,0:T(8,128)S(1)}, f32[8,8,512]{2,1,0:T(8,128)S(1)}) custom-call(s32[7]{0:T(128)S(1)} %stack.67.meta, f32[48]{0:T(128)S(1)} %pad_maximum_fusion.5.h, bf16[64,2048]{1,0:T(8,128)(2,1)} %own.3, bf16[64,2048]{1,0:T(8,128)(2,1)S(1)} %collective-permute-done.11.prev, ...), custom_call_target="tpu_custom_call" | custom-call | flops 1000000000 | bytes 10000000 | tf_op jit(solution)/shard_map/pallas_call | solution.py:259
  67.9 7.3 %shard_map.131 = (bf16[64,2304]{1,0:T(8,128)(2,1)S(1)}, bf16[64,2304]{1,0:T(8,128)(2,1)}, bf16[64,2304]{1,0:T(8,128)(2,1)}, bf16[64,2304]{1,0:T(8,128)(2,1)}, f3...) custom-call(s32[7]{0:T(128)S(1)} %stack.67.meta, f32[48]{0:T(128)S(1)} %pad_maximum_fusion.5.h, ...), custom_call_target="tpu_custom_call" | custom-call | flops 3000000000 | bytes 10000000 | tf_op jit(solution)/shard_map/pallas_call | solution.py:259
  79.2 7.3 %all-to-all-start = ((bf16[8,72,512]{2,1,0:T(8,128)(2,1)}), bf16[8,72,512]{2,1,0:T(8,128)(2,1)S(1)}, u32[]{:S(2)}, u32[]{:S(2)}) async-start(bf16[8,72,512]{2,1,0:T(8,128)(2,1)} %add_convert_fusion), calls=%async_computation | async-start | bytes 1179648 | tf_op jit(solution)/shard_map/all_to_all | solution.py:440
  86.5 10.9 %collective-permute-done.23 = bf16[64,2304]{1,0:T(8,128)(2,1)S(1)} collective-permute-done((bf16[64,2304]{1,0:T(8,128)(2,1)}, bf16[64,2304]{1,0:T(8,128)(2,1)S(1)}, u32[]{:S(2)}, u32[]{:S(2)}) %collective-permute-start.23) | collective-permute-done | bytes 294944 | tf_op jit(solution)/shard_map/ppermute | solution.py:490
  97.5 5.7 %all-to-all-done.got = bf16[8,72,512]{2,1,0:T(8,128)(2,1)S(1)} async-done(((bf16[8,72,512]{2,1,0:T(8,128)(2,1)}), bf16[8,72,512]{2,1,0:T(8,128)(2,1)S(1)}, u32[]{:S(2)}, u32[]{:S(2)}) %all-to-all-start) | async-done | bytes 589856 | tf_op jit(solution)/shard_map/all_to_all | solution.py:440
  104.1 3.5 %all-to-all-start.1 = ((bf16[8,64,512]{2,1,0:T(8,128)(2,1)}), bf16[8,64,512]{2,1,0:T(8,128)(2,1)S(1)}, u32[]{:S(2)}, u32[]{:S(2)}) async-start(bf16[8,64,512]{2,1,0:T(8,128)(2,1)} %finish.1), calls=%async_computation.1 | async-start | bytes 1048576 | tf_op jit(solution)/shard_map/all_to_all | solution.py:440
  107.6 4.1 %collective-permute-start.25 = (bf16[64,2048]{1,0:T(8,128)(2,1)S(1)}, bf16[64,2048]{1,0:T(8,128)(2,1)S(1)}, u32[]{:S(2)}, u32[]{:S(2)}) collective-permute-start(bf16[64,2048]{1,0:T(8,128)(2,1)S(1)} %fusion), channel_id=1, source_target_pairs={{16,0},{32,16},{48,32},{64,48},{80,64},{96,80},{112,96},{0,112},{1... | collective-permute-start | bytes 786440 | tf_op jit(solution)/shard_map/ppermute | solution.py:498
  111.8 8.7 %collective-permute-done.25.returned = bf16[64,2048]{1,0:T(8,128)(2,1)S(1)} collective-permute-done((bf16[64,2048]{1,0:T(8,128)(2,1)S(1)}, bf16[64,2048]{1,0:T(8,128)(2,1)S(1)}, u32[]{:S(2)}, u32[]{:S(2)}) %collective-permute-start.25) | collective-permute-done | bytes 262176 | tf_op jit(solution)/shard_map/ppermute | solution.py:498
  (89 shorter events, 21.7 us)
Async XLA Ops:
  1.7 14.3 %collective-permute-start = (bf16[64,2048]{1,0:T(8,128)(2,1)S(1)}, bf16[64,2048]{1,0:T(8,128)(2,1)S(1)}, u32[]{:S(2)}, u32[]{:S(2)}) collective-permute-start(bf16[64,2048]{1,0:T(8,128)(2,1)S(1)} %slice_bitcast_fusion.2), channel_id=1, source_target_pairs={{0,16},{16,32},{32,48},{48,64},{64,80},{80,96},{96,112},{112,0},{1... | collective-permute-start | bytes 786440 | tf_op jit(solution)/shard_map/ppermute | solution.py:444
  6.3 7.9 %collective-permute-start.5 = (bf16[64,1024]{1,0:T(8,128)(2,1)}, bf16[64,1024]{1,0:T(8,128)(2,1)S(1)}, u32[]{:S(2)}, u32[]{:S(2)}) collective-permute-start(bf16[64,1024]{1,0:T(8,128)(2,1)} %get-tuple-element.23), channel_id=1, source_target_pairs={{0,2},{2,4},{4,6},{6,0},{1,3},{3,5},{5,7},{7,1},{8,10},{10,12},{12... | collective-permute-start | bytes 393224 | tf_op jit(solution)/shard_map/ppermute | solution.py:455
  8.0 17.6 %collective-permute-start.15 = (bf16[64,1280]{1,0:T(8,128)(2,1)}, bf16[64,1280]{1,0:T(8,128)(2,1)S(1)}, u32[]{:S(2)}, u32[]{:S(2)}) collective-permute-start(bf16[64,1280]{1,0:T(8,128)(2,1)} %get-tuple-element.27), channel_id=1, source_target_pairs={{0,2},{2,4},{4,6},{6,0},{1,3},{3,5},{5,7},{7,1},{8,10},{10,12},{12... | collective-permute-start | bytes 491528 | tf_op jit(solution)/shard_map/ppermute | solution.py:452
  9.5 19.3 %collective-permute-start.16 = (bf16[64,1280]{1,0:T(8,128)(2,1)}, bf16[64,1280]{1,0:T(8,128)(2,1)S(1)}, u32[]{:S(2)}, u32[]{:S(2)}) collective-permute-start(bf16[64,1280]{1,0:T(8,128)(2,1)} %get-tuple-element.28), channel_id=1, source_target_pairs={{2,0},{4,2},{6,4},{0,6},{3,1},{5,3},{7,5},{1,7},{10,8},{12,10},{14... | collective-permute-start | bytes 491528 | tf_op jit(solution)/shard_map/ppermute | solution.py:453
  11.2 21.3 %collective-permute-start.17 = (bf16[64,1280]{1,0:T(8,128)(2,1)}, bf16[64,1280]{1,0:T(8,128)(2,1)S(1)}, u32[]{:S(2)}, u32[]{:S(2)}) collective-permute-start(bf16[64,1280]{1,0:T(8,128)(2,1)} %get-tuple-element.29), channel_id=1, source_target_pairs={{0,4},{2,6},{4,0},{6,2},{1,5},{3,7},{5,1},{7,3},{8,12},{10,14},{12... | collective-permute-start | bytes 491528 | tf_op jit(solution)/shard_map/ppermute | solution.py:454
  14.2 9.1 %collective-permute-start.6 = (bf16[64,1024]{1,0:T(8,128)(2,1)}, bf16[64,1024]{1,0:T(8,128)(2,1)S(1)}, u32[]{:S(2)}, u32[]{:S(2)}) collective-permute-start(bf16[64,1024]{1,0:T(8,128)(2,1)} %get-tuple-element.24), channel_id=1, source_target_pairs={{2,0},{4,2},{6,4},{0,6},{3,1},{5,3},{7,5},{1,7},{10,8},{12,10},{14... | collective-permute-start | bytes 393224 | tf_op jit(solution)/shard_map/ppermute | solution.py:456
  16.0 9.5 %collective-permute-start.7 = (bf16[64,1024]{1,0:T(8,128)(2,1)}, bf16[64,1024]{1,0:T(8,128)(2,1)S(1)}, u32[]{:S(2)}, u32[]{:S(2)}) collective-permute-start(bf16[64,1024]{1,0:T(8,128)(2,1)} %get-tuple-element.25), channel_id=1, source_target_pairs={{0,4},{2,6},{4,0},{6,2},{1,5},{3,7},{5,1},{7,3},{8,12},{10,14},{12... | collective-permute-start | bytes 393224 | tf_op jit(solution)/shard_map/ppermute | solution.py:457
  23.3 10.9 %collective-permute-start.11 = (bf16[64,2048]{1,0:T(8,128)(2,1)}, bf16[64,2048]{1,0:T(8,128)(2,1)S(1)}, u32[]{:S(2)}, u32[]{:S(2)}) collective-permute-start(bf16[64,2048]{1,0:T(8,128)(2,1)} %own.3), channel_id=1, source_target_pairs={{0,2},{2,4},{4,6},{6,0},{1,3},{3,5},{5,7},{7,1},{8,10},{10,12},{12... | collective-permute-start | bytes 786440 | tf_op jit(solution)/shard_map/ppermute | solution.py:445
  25.5 16.3 %collective-permute-start.1 = (bf16[2,64,2048]{2,1,0:T(8,128)(2,1)S(1)}, bf16[2,64,2048]{2,1,0:T(8,128)(2,1)S(1)}, u32[]{:S(2)}, u32[]{:S(2)}) collective-permute-start(bf16[2,64,2048]{2,1,0:T(8,128)(2,1)S(1)} %pad_maximum_fusion.1.a_own), channel_id=1, source_target_pairs={{0,2},{2,4},{4,6},{6,0},{1,3},{3,5},{5,7},{7,1},{8,10},{10,12},{12... | collective-permute-start | bytes 1572872 | tf_op jit(solution)/shard_map/ppermute | solution.py:475
  25.6 10.3 %collective-permute-start.12 = (bf16[64,2048]{1,0:T(8,128)(2,1)}, bf16[64,2048]{1,0:T(8,128)(2,1)S(1)}, u32[]{:S(2)}, u32[]{:S(2)}) collective-permute-start(bf16[64,2048]{1,0:T(8,128)(2,1)} %own.3), channel_id=1, source_target_pairs={{2,0},{4,2},{6,4},{0,6},{3,1},{5,3},{7,5},{1,7},{10,8},{12,10},{14... | collective-permute-start | bytes 786440 | tf_op jit(solution)/shard_map/ppermute | solution.py:446
  28.9 19.1 %collective-permute-start.8 = (bf16[4,64,1024]{2,1,0:T(8,128)(2,1)S(1)}, bf16[4,64,1024]{2,1,0:T(8,128)(2,1)}, u32[]{:S(2)}, u32[]{:S(2)}) collective-permute-start(bf16[4,64,1024]{2,1,0:T(8,128)(2,1)S(1)} %pad_maximum_fusion.2.p0), channel_id=1, source_target_pairs={{0,8},{8,0},{1,9},{9,1},{2,10},{10,2},{3,11},{11,3},{4,12},{12,4},... | collective-permute-start | bytes 1572872 | tf_op jit(solution)/shard_map/ppermute | solution.py:471
  32.6 16.5 %collective-permute-start.2 = (bf16[2,64,2048]{2,1,0:T(8,128)(2,1)S(1)}, bf16[2,64,2048]{2,1,0:T(8,128)(2,1)S(1)}, u32[]{:S(2)}, u32[]{:S(2)}) collective-permute-start(bf16[2,64,2048]{2,1,0:T(8,128)(2,1)S(1)} %pad_maximum_fusion.1.a_own), channel_id=1, source_target_pairs={{2,0},{4,2},{6,4},{0,6},{3,1},{5,3},{7,5},{1,7},{10,8},{12,10},{14... | collective-permute-start | bytes 1572872 | tf_op jit(solution)/shard_map/ppermute | solution.py:476
  34.2 32.7 %collective-permute-start.9 = (bf16[4,64,1024]{2,1,0:T(8,128)(2,1)S(1)}, bf16[4,64,1024]{2,1,0:T(8,128)(2,1)}, u32[]{:S(2)}, u32[]{:S(2)}) collective-permute-start(bf16[4,64,1024]{2,1,0:T(8,128)(2,1)S(1)} %pad_maximum_fusion.2.p0), channel_id=1, source_target_pairs={{0,1},{1,0},{2,3},{3,2},{4,5},{5,4},{6,7},{7,6},{8,9},{9,8},{10,11... | collective-permute-start | bytes 1572872 | tf_op jit(solution)/shard_map/ppermute | solution.py:472
  35.9 14.2 %collective-permute-start.18 = (bf16[5,64,512]{2,1,0:T(8,128)(2,1)S(1)}, bf16[5,64,512]{2,1,0:T(8,128)(2,1)}, u32[]{:S(2)}, u32[]{:S(2)}) collective-permute-start(bf16[5,64,512]{2,1,0:T(8,128)(2,1)S(1)} %pad_maximum_fusion.3.b0), channel_id=1, source_target_pairs={{0,8},{8,0},{1,9},{9,1},{2,10},{10,2},{3,11},{11,3},{4,12},{12,4},... | collective-permute-start | bytes 983048 | tf_op jit(solution)/shard_map/ppermute | solution.py:463
  49.1 17.8 %collective-permute-start.10 = (bf16[4,64,1024]{2,1,0:T(8,128)(2,1)}, bf16[4,64,1024]{2,1,0:T(8,128)(2,1)}, u32[]{:S(2)}, u32[]{:S(2)}) collective-permute-start(bf16[4,64,1024]{2,1,0:T(8,128)(2,1)} %collective-permute-done.8.p1), channel_id=1, source_target_pairs={{0,1},{1,0},{2,3},{3,2},{4,5},{5,4},{6,7},{7,6},{8,9},{9,8},{10,11... | collective-permute-start | bytes 1572872 | tf_op jit(solution)/shard_map/ppermute | solution.py:473
  50.1 9.5 %collective-permute-start.20 = (bf16[5,64,512]{2,1,0:T(8,128)(2,1)}, bf16[5,64,512]{2,1,0:T(8,128)(2,1)}, u32[]{:S(2)}, u32[]{:S(2)}) collective-permute-start(bf16[5,64,512]{2,1,0:T(8,128)(2,1)} %collective-permute-done.18.b1), channel_id=1, source_target_pairs={{0,1},{1,0},{2,3},{3,2},{4,5},{5,4},{6,7},{7,6},{8,9},{9,8},{10,11... | collective-permute-start | bytes 983048 | tf_op jit(solution)/shard_map/ppermute | solution.py:465
  54.5 12.4 %collective-permute-start.3 = (bf16[64,2048]{1,0:T(8,128)(2,1)}, bf16[64,2048]{1,0:T(8,128)(2,1)}, u32[]{:S(2)}, u32[]{:S(2)}) collective-permute-start(bf16[64,2048]{1,0:T(8,128)(2,1)} %slice_bitcast_fusion.1), channel_id=1, source_target_pairs={{0,2},{2,4},{4,6},{6,0},{1,3},{3,5},{5,7},{7,1},{8,10},{10,12},{12... | collective-permute-start | bytes 786440 | tf_op jit(solution)/shard_map/ppermute | solution.py:479
  55.2 11.7 %collective-permute-start.4 = (bf16[64,2048]{1,0:T(8,128)(2,1)}, bf16[64,2048]{1,0:T(8,128)(2,1)}, u32[]{:S(2)}, u32[]{:S(2)}) collective-permute-start(bf16[64,2048]{1,0:T(8,128)(2,1)} %slice_bitcast_fusion), channel_id=1, source_target_pairs={{2,0},{4,2},{6,4},{0,6},{3,1},{5,3},{7,5},{1,7},{10,8},{12,10},{14... | collective-permute-start | bytes 786440 | tf_op jit(solution)/shard_map/ppermute | solution.py:480
  75.4 11.2 %collective-permute-start.22 = (bf16[64,2304]{1,0:T(8,128)(2,1)}, bf16[64,2304]{1,0:T(8,128)(2,1)S(1)}, u32[]{:S(2)}, u32[]{:S(2)}) collective-permute-start(bf16[64,2304]{1,0:T(8,128)(2,1)} %get-tuple-element.36), channel_id=1, source_target_pairs={{2,0},{4,2},{6,4},{0,6},{3,1},{5,3},{7,5},{1,7},{10,8},{12,10},{14... | collective-permute-start | bytes 884744 | tf_op jit(solution)/shard_map/ppermute | solution.py:489
  76.6 20.8 %collective-permute-start.23 = (bf16[64,2304]{1,0:T(8,128)(2,1)}, bf16[64,2304]{1,0:T(8,128)(2,1)S(1)}, u32[]{:S(2)}, u32[]{:S(2)}) collective-permute-start(bf16[64,2304]{1,0:T(8,128)(2,1)} %get-tuple-element.37), channel_id=1, source_target_pairs={{0,2},{2,4},{4,6},{6,0},{1,3},{3,5},{5,7},{7,1},{8,10},{10,12},{12... | collective-permute-start | bytes 884744 | tf_op jit(solution)/shard_map/ppermute | solution.py:490
  77.5 19.9 %collective-permute-start.24 = (bf16[64,2304]{1,0:T(8,128)(2,1)}, bf16[64,2304]{1,0:T(8,128)(2,1)S(1)}, u32[]{:S(2)}, u32[]{:S(2)}) collective-permute-start(bf16[64,2304]{1,0:T(8,128)(2,1)} %get-tuple-element.38), channel_id=1, source_target_pairs={{0,4},{2,6},{4,0},{6,2},{1,5},{3,7},{5,1},{7,3},{8,12},{10,14},{12... | collective-permute-start | bytes 884744 | tf_op jit(solution)/shard_map/ppermute | solution.py:491
  79.2 24.1 %all-to-all-start = ((bf16[8,72,512]{2,1,0:T(8,128)(2,1)}), bf16[8,72,512]{2,1,0:T(8,128)(2,1)S(1)}, u32[]{:S(2)}, u32[]{:S(2)}) async-start(bf16[8,72,512]{2,1,0:T(8,128)(2,1)} %add_convert_fusion), calls=%async_computation | async-start | bytes 1179648 | tf_op jit(solution)/shard_map/all_to_all | solution.py:440
  104.1 17.8 %all-to-all-start.1 = ((bf16[8,64,512]{2,1,0:T(8,128)(2,1)}), bf16[8,64,512]{2,1,0:T(8,128)(2,1)S(1)}, u32[]{:S(2)}, u32[]{:S(2)}) async-start(bf16[8,64,512]{2,1,0:T(8,128)(2,1)} %finish.1), calls=%async_computation.1 | async-start | bytes 1048576 | tf_op jit(solution)/shard_map/all_to_all | solution.py:440
  107.6 12.9 %collective-permute-start.25 = (bf16[64,2048]{1,0:T(8,128)(2,1)S(1)}, bf16[64,2048]{1,0:T(8,128)(2,1)S(1)}, u32[]{:S(2)}, u32[]{:S(2)}) collective-permute-start(bf16[64,2048]{1,0:T(8,128)(2,1)S(1)} %fusion), channel_id=1, source_target_pairs={{16,0},{32,16},{48,32},{64,48},{80,64},{96,80},{112,96},{0,112},{1... | collective-permute-start | bytes 786440 | tf_op jit(solution)/shard_map/ppermute | solution.py:498
  (18 other events, 174.4 us)

commit v5 on v4

--- a/solution.py
+++ b/solution.py
@@ -140,8 +140,8 @@
 
 def window_kernel(
     meta, h, a_own, a_prev, a_after, x_far, l_far, p0, p1, p2, p3, own, prev, after, far_low, far_high,
-    b0, b1, b2, b3, bulk_left, bulk_keep, bulk_send, left_0, left_1, left_2, left_3, keep_out, send_out,
-    xs, ls, xb, ys, yb, raw, th, tmp, left, keep_rows, send_rows, sem, sem_y, sem_r, sem_b, sem_out,
+    b0, b1, b2, b3, bulk_left, bulk_keep, bulk_send, left_0, left_1, left_2, left_3, keep_rows, send_rows,
+    xs, ls, xb, ys, yb, raw, th, tmp, sem, sem_y, sem_r, sem_b,
 ):
     c, zh, me, first = meta[0], meta[1], meta[2], meta[3]
     ny, block, width, cols = 4, 64, 1024, 512
@@ -165,10 +165,10 @@
     ]
     late.append(pltpu.make_async_copy(bulk_keep, keep_rows.at[:, block : block + 8, :], sem.at[13]))
     late.append(pltpu.make_async_copy(bulk_send, send_rows.at[:, block : block + 8, :], sem.at[14]))
-    for n in range(ny):
+    for n, ref in enumerate((left_0, left_1, left_2, left_3)):
         proj.append(
             pltpu.make_async_copy(
-                bulk_left.at[n], left.at[rows[n], 2 * width : 2 * width + 256], sem.at[15 + n]
+                bulk_left.at[n], ref.at[:, 2 * width : 2 * width + 256], sem.at[15 + n]
             )
         )
     for copy in early:
@@ -205,21 +205,17 @@
     for copy in proj:
         copy.wait()
 
-    def left_chunk(n, _):
-        k_at = pl.multiple_of(n * 256, 256)
+    def left_chunk(m, _):
+        k_at = pl.multiple_of(m * 256, 256)
         r_part = ys[pl.ds(k_at, 256), cols : 2 * cols]
         for s in range(2):
-            lanes = pl.ds(pl.multiple_of(s * width + n * 256, 256), 256)
-            left[:, lanes] = dot(th[s], r_part, ((1,), (1,))).astype(BF16)
+            lanes = pl.ds(pl.multiple_of(s * width + m * 256, 256), 256)
+            part = dot(th[s], r_part, ((1,), (1,))).astype(BF16)
+            for n, ref in enumerate((left_0, left_1, left_2, left_3)):
+                ref[:, lanes] = part[n * block : (n + 1) * block]
         return 0
 
     lax.fori_loop(0, 4, left_chunk, 0, unroll=True)
-    outs = [
-        pltpu.make_async_copy(left.at[rows[n], :], ref, sem_out.at[n])
-        for n, ref in enumerate((left_0, left_1, left_2, left_3))
-    ]
-    for copy in outs:
-        copy.start()
 
     @pl.when(first == 1)
     def _():
@@ -245,12 +241,6 @@
         return 0
 
     lax.fori_loop(0, 4, right_chunk, 0, unroll=True)
-    outs.append(pltpu.make_async_copy(send_rows, send_out, sem_out.at[4]))
-    outs.append(pltpu.make_async_copy(keep_rows, keep_out, sem_out.at[5]))
-    for copy in outs[4:]:
-        copy.start()
-    for copy in outs:
-        copy.wait()
 
 
 def call(kernel, outs, out_space, scratch, flops, meta, h, *arrays):
@@ -350,7 +340,7 @@
     return call(
         window_kernel,
         (rows, rows, rows, rows, sums, sums),
-        pltpu.HBM,
+        pltpu.VMEM,
         [
             pltpu.VMEM((256, 2048), BF16),
             pltpu.VMEM((256, 2048), BF16),
@@ -360,14 +350,10 @@
             pltpu.VMEM((2, 256, 512), F32),
             pltpu.VMEM((2, 256, 512), BF16),
             pltpu.VMEM((256, 512), F32),
-            pltpu.VMEM((256, 2304), BF16),
-            pltpu.VMEM((8, 72, 512), F32),
-            pltpu.VMEM((8, 72, 512), F32),
             pltpu.SemaphoreType.DMA((19,)),
             pltpu.SemaphoreType.DMA((16,)),
             pltpu.SemaphoreType.DMA((16,)),
             pltpu.SemaphoreType.DMA((16,)),
-            pltpu.SemaphoreType.DMA((6,)),
         ],
         3_000_000_000,
         meta,

time: 123 us -> 123 us (level)
  no operation moved by 1% of the time
where the time goes in v5:
time: 123 us; the launch traced here: 122 us
  starting transfers between devices  46.8 us (38%)
  waiting for transfers between devices  46.8 us (38%)
  Pallas kernels  17 us (14%)
  local copies, waits for them, and re-layouts  8.02 us (7%)
  between operations  2.19 us (2%)
  other arithmetic  1.51 us (1%)
    pallas_call x2, Pallas kernels, call(): pl.pallas_call(kernel, out_shape=outs, in_specs=[smem, smem] + [anywhere]...  11.3 us
    ppermute x1, waiting for transfers between devices, half_step(): left_up = lax.ppermute(left_up, 'y', up)  10.9 us
    all_to_all x2, starting transfers between devices, exchange(): return lax.all_to_all(v, axis, split_axis=0, concat_axis=0, tiled=True)  10.8 us
    ppermute x1, waiting for transfers between devices, half_step(): returned = lax.ppermute(left, SITE, back)  8.73 us
    ppermute x1, waiting for transfers between devices, half_step(): w_2 = lax.ppermute(w_2, 'y', down)  6.63 us
    all_to_all x2, waiting for transfers between devices, exchange(): return lax.all_to_all(v, axis, split_axis=0, concat_axis=0, tiled=True)  5.7 us
    ppermute x1, waiting for transfers between devices, half_step(): b_low = lax.ppermute(b_low, 'y', up)  5.45 us
    unnamed x28, local copies, waits for them, and re-layouts  5.18 us
  transfers between devices with their start and end apart: 28, of which 10 were waited for; matrix products, arithmetic and copies ran while one was open for 3% of the time, Pallas kernels for 7%

profile of v5, /device:TPU:0, one launch (start us, length us, event | category | flops | bytes accessed | tf_op | source)
XLA Modules:
  0.0 122.3 jit_solution(17206062272504937917)
XLA Ops:
  1.7 2.1 %collective-permute-start = (bf16[64,2048]{1,0:T(8,128)(2,1)S(1)}, bf16[64,2048]{1,0:T(8,128)(2,1)S(1)}, u32[]{:S(2)}, u32[]{:S(2)}) collective-permute-start(bf16[64,2048]{1,0:T(8,128)(2,1)S(1)} %slice_bitcast_fusion.2), channel_id=1, source_target_pairs={{0,16},{16,32},{32,48},{48,64},{64,80},{80,96},{96,112},{112,0},{1... | collective-permute-start | bytes 786440 | tf_op jit(solution)/shard_map/ppermute | solution.py:430
  3.8 2.6 %split.1 = (bf16[64,1024]{1,0:T(8,128)(2,1)}, bf16[64,1024]{1,0:T(8,128)(2,1)}, bf16[64,1024]{1,0:T(8,128)(2,1)}, bf16[64,1024]{1,0:T(8,128)(2,1)}, bf16[64,1280...) custom-call(bf16[2,64,2048]{2,1,0:T(8,128)(2,1)} %site.1, ...), custom_call_target="tpu_custom_call" | custom-call | flops 40000000 | bytes 3000000 | tf_op jit(solution)/shard_map/split/pallas_call | solution.py:50
  6.3 1.6 %collective-permute-start.5 = (bf16[64,1024]{1,0:T(8,128)(2,1)}, bf16[64,1024]{1,0:T(8,128)(2,1)S(1)}, u32[]{:S(2)}, u32[]{:S(2)}) collective-permute-start(bf16[64,1024]{1,0:T(8,128)(2,1)} %get-tuple-element.23), channel_id=1, source_target_pairs={{0,2},{2,4},{4,6},{6,0},{1,3},{3,5},{5,7},{7,1},{8,10},{10,12},{12... | collective-permute-start | bytes 393224 | tf_op jit(solution)/shard_map/ppermute | solution.py:441
  9.5 1.7 %collective-permute-start.16 = (bf16[64,1280]{1,0:T(8,128)(2,1)}, bf16[64,1280]{1,0:T(8,128)(2,1)S(1)}, u32[]{:S(2)}, u32[]{:S(2)}) collective-permute-start(bf16[64,1280]{1,0:T(8,128)(2,1)} %get-tuple-element.28), channel_id=1, source_target_pairs={{2,0},{4,2},{6,4},{0,6},{3,1},{5,3},{7,5},{1,7},{10,8},{12,10},{14... | collective-permute-start | bytes 491528 | tf_op jit(solution)/shard_map/ppermute | solution.py:439
  11.2 1.7 %collective-permute-start.17 = (bf16[64,1280]{1,0:T(8,128)(2,1)}, bf16[64,1280]{1,0:T(8,128)(2,1)S(1)}, u32[]{:S(2)}, u32[]{:S(2)}) collective-permute-start(bf16[64,1280]{1,0:T(8,128)(2,1)} %get-tuple-element.29), channel_id=1, source_target_pairs={{0,4},{2,6},{4,0},{6,2},{1,5},{3,7},{5,1},{7,3},{8,12},{10,14},{12... | collective-permute-start | bytes 491528 | tf_op jit(solution)/shard_map/ppermute | solution.py:440
  14.2 1.8 %collective-permute-start.6 = (bf16[64,1024]{1,0:T(8,128)(2,1)}, bf16[64,1024]{1,0:T(8,128)(2,1)S(1)}, u32[]{:S(2)}, u32[]{:S(2)}) collective-permute-start(bf16[64,1024]{1,0:T(8,128)(2,1)} %get-tuple-element.24), channel_id=1, source_target_pairs={{2,0},{4,2},{6,4},{0,6},{3,1},{5,3},{7,5},{1,7},{10,8},{12,10},{14... | collective-permute-start | bytes 393224 | tf_op jit(solution)/shard_map/ppermute | solution.py:442
  16.7 6.6 %collective-permute-done.6 = bf16[64,1024]{1,0:T(8,128)(2,1)S(1)} collective-permute-done((bf16[64,1024]{1,0:T(8,128)(2,1)}, bf16[64,1024]{1,0:T(8,128)(2,1)S(1)}, u32[]{:S(2)}, u32[]{:S(2)}) %collective-permute-start.6) | collective-permute-done | bytes 131104 | tf_op jit(solution)/shard_map/ppermute | solution.py:442
  23.3 2.2 %collective-permute-start.11 = (bf16[64,2048]{1,0:T(8,128)(2,1)}, bf16[64,2048]{1,0:T(8,128)(2,1)S(1)}, u32[]{:S(2)}, u32[]{:S(2)}) collective-permute-start(bf16[64,2048]{1,0:T(8,128)(2,1)} %own.3), channel_id=1, source_target_pairs={{0,2},{2,4},{4,6},{6,0},{1,3},{3,5},{5,7},{7,1},{8,10},{10,12},{12... | collective-permute-start | bytes 786440 | tf_op jit(solution)/shard_map/ppermute | solution.py:431
  25.6 3.3 %collective-permute-start.12 = (bf16[64,2048]{1,0:T(8,128)(2,1)}, bf16[64,2048]{1,0:T(8,128)(2,1)S(1)}, u32[]{:S(2)}, u32[]{:S(2)}) collective-permute-start(bf16[64,2048]{1,0:T(8,128)(2,1)} %own.3), channel_id=1, source_target_pairs={{2,0},{4,2},{6,4},{0,6},{3,1},{5,3},{7,5},{1,7},{10,8},{12,10},{14... | collective-permute-start | bytes 786440 | tf_op jit(solution)/shard_map/ppermute | solution.py:432
  28.9 3.6 %collective-permute-start.8 = (bf16[4,64,1024]{2,1,0:T(8,128)(2,1)S(1)}, bf16[4,64,1024]{2,1,0:T(8,128)(2,1)}, u32[]{:S(2)}, u32[]{:S(2)}) collective-permute-start(bf16[4,64,1024]{2,1,0:T(8,128)(2,1)S(1)} %pad_maximum_fusion.2.p0), channel_id=1, source_target_pairs={{0,8},{8,0},{1,9},{9,1},{2,10},{10,2},{3,11},{11,3},{4,12},{12,4},... | collective-permute-start | bytes 1572872 | tf_op jit(solution)/shard_map/ppermute | solution.py:457
  34.2 1.7 %collective-permute-done.12.after = bf16[64,2048]{1,0:T(8,128)(2,1)S(1)} collective-permute-done((bf16[64,2048]{1,0:T(8,128)(2,1)}, bf16[64,2048]{1,0:T(8,128)(2,1)S(1)}, u32[]{:S(2)}, u32[]{:S(2)}) %collective-permute-start.12) | collective-permute-done | bytes 262176 | tf_op jit(solution)/shard_map/ppermute | solution.py:432
  35.9 3.6 %collective-permute-start.18 = (bf16[5,64,512]{2,1,0:T(8,128)(2,1)S(1)}, bf16[5,64,512]{2,1,0:T(8,128)(2,1)}, u32[]{:S(2)}, u32[]{:S(2)}) collective-permute-start(bf16[5,64,512]{2,1,0:T(8,128)(2,1)S(1)} %pad_maximum_fusion.3.b0), channel_id=1, source_target_pairs={{0,8},{8,0},{1,9},{9,1},{2,10},{10,2},{3,11},{11,3},{4,12},{12,4},... | collective-permute-start | bytes 983048 | tf_op jit(solution)/shard_map/ppermute | solution.py:449
  39.5 2.3 %collective-permute-done.1.a_prev = bf16[2,64,2048]{2,1,0:T(8,128)(2,1)S(1)} collective-permute-done((bf16[2,64,2048]{2,1,0:T(8,128)(2,1)S(1)}, bf16[2,64,2048]{2,1,0:T(8,128)(2,1)S(1)}, u32[]{:S(2)}, u32[]{:S(2)}) %collective-permute-start.1) | collective-permute-done | bytes 524320 | tf_op jit(solution)/shard_map/ppermute | solution.py:461
  42.5 5.5 %collective-permute-done.13.far_low = bf16[64,1024]{1,0:T(8,128)(2,1)S(1)} collective-permute-done((bf16[64,1024]{1,0:T(8,128)(2,1)S(1)}, bf16[64,1024]{1,0:T(8,128)(2,1)S(1)}, u32[]{:S(2)}, u32[]{:S(2)}) %collective-permute-start.13) | collective-permute-done | bytes 131104 | tf_op jit(solution)/shard_map/ppermute | solution.py:454
  50.4 3.5 %collective-permute-done.14.far_high = bf16[64,1024]{1,0:T(8,128)(2,1)S(1)} collective-permute-done((bf16[64,1024]{1,0:T(8,128)(2,1)S(1)}, bf16[64,1024]{1,0:T(8,128)(2,1)S(1)}, u32[]{:S(2)}, u32[]{:S(2)}) %collective-permute-start.14) | collective-permute-done | bytes 131104 | tf_op jit(solution)/shard_map/ppermute | solution.py:455
  55.2 3.2 %collective-permute-start.4 = (bf16[64,2048]{1,0:T(8,128)(2,1)}, bf16[64,2048]{1,0:T(8,128)(2,1)}, u32[]{:S(2)}, u32[]{:S(2)}) collective-permute-start(bf16[64,2048]{1,0:T(8,128)(2,1)} %slice_bitcast_fusion), channel_id=1, source_target_pairs={{2,0},{4,2},{6,4},{0,6},{3,1},{5,3},{7,5},{1,7},{10,8},{12,10},{14... | collective-permute-start | bytes 786440 | tf_op jit(solution)/shard_map/ppermute | solution.py:466
  62.4 4.5 %shard_map.130 = (bf16[4,64,256]{2,1,0:T(8,128)(2,1)S(1)}, f32[8,8,512]{2,1,0:T(8,128)S(1)}, f32[8,8,512]{2,1,0:T(8,128)S(1)}) custom-call(s32[7]{0:T(128)S(1)} %stack.67.meta, f32[48]{0:T(128)S(1)} %pad_maximum_fusion.5.h, bf16[64,2048]{1,0:T(8,128)(2,1)} %own.3, bf16[64,2048]{1,0:T(8,128)(2,1)S(1)} %collective-permute-done.11.prev, ...), custom_call_target="tpu_custom_call" | custom-call | flops 1000000000 | bytes 10000000 | tf_op jit(solution)/shard_map/pallas_call | solution.py:249
  67.9 6.8 %shard_map.131 = (bf16[64,2304]{1,0:T(8,128)(2,1)S(1)}, bf16[64,2304]{1,0:T(8,128)(2,1)}, bf16[64,2304]{1,0:T(8,128)(2,1)}, bf16[64,2304]{1,0:T(8,128)(2,1)}, f3...) custom-call(s32[7]{0:T(128)S(1)} %stack.67.meta, f32[48]{0:T(128)S(1)} %pad_maximum_fusion.5.h, ...), custom_call_target="tpu_custom_call" | custom-call | flops 3000000000 | bytes 10000000 | tf_op jit(solution)/shard_map/pallas_call | solution.py:249
  78.6 7.3 %all-to-all-start = ((bf16[8,72,512]{2,1,0:T(8,128)(2,1)}), bf16[8,72,512]{2,1,0:T(8,128)(2,1)S(1)}, u32[]{:S(2)}, u32[]{:S(2)}) async-start(bf16[8,72,512]{2,1,0:T(8,128)(2,1)} %add_convert_fusion), calls=%async_computation | async-start | bytes 1179648 | tf_op jit(solution)/shard_map/all_to_all | solution.py:426
  86.0 10.9 %collective-permute-done.23 = bf16[64,2304]{1,0:T(8,128)(2,1)S(1)} collective-permute-done((bf16[64,2304]{1,0:T(8,128)(2,1)}, bf16[64,2304]{1,0:T(8,128)(2,1)S(1)}, u32[]{:S(2)}, u32[]{:S(2)}) %collective-permute-start.23) | collective-permute-done | bytes 294944 | tf_op jit(solution)/shard_map/ppermute | solution.py:476
  97.0 5.7 %all-to-all-done.got = bf16[8,72,512]{2,1,0:T(8,128)(2,1)S(1)} async-done(((bf16[8,72,512]{2,1,0:T(8,128)(2,1)}), bf16[8,72,512]{2,1,0:T(8,128)(2,1)S(1)}, u32[]{:S(2)}, u32[]{:S(2)}) %all-to-all-start) | async-done | bytes 589856 | tf_op jit(solution)/shard_map/all_to_all | solution.py:426
  103.5 3.5 %all-to-all-start.1 = ((bf16[8,64,512]{2,1,0:T(8,128)(2,1)}), bf16[8,64,512]{2,1,0:T(8,128)(2,1)S(1)}, u32[]{:S(2)}, u32[]{:S(2)}) async-start(bf16[8,64,512]{2,1,0:T(8,128)(2,1)} %finish.1), calls=%async_computation.1 | async-start | bytes 1048576 | tf_op jit(solution)/shard_map/all_to_all | solution.py:426
  107.1 4.1 %collective-permute-start.25 = (bf16[64,2048]{1,0:T(8,128)(2,1)S(1)}, bf16[64,2048]{1,0:T(8,128)(2,1)S(1)}, u32[]{:S(2)}, u32[]{:S(2)}) collective-permute-start(bf16[64,2048]{1,0:T(8,128)(2,1)S(1)} %fusion), channel_id=1, source_target_pairs={{16,0},{32,16},{48,32},{64,48},{80,64},{96,80},{112,96},{0,112},{1... | collective-permute-start | bytes 786440 | tf_op jit(solution)/shard_map/ppermute | solution.py:484
  111.2 8.7 %collective-permute-done.25.returned = bf16[64,2048]{1,0:T(8,128)(2,1)S(1)} collective-permute-done((bf16[64,2048]{1,0:T(8,128)(2,1)S(1)}, bf16[64,2048]{1,0:T(8,128)(2,1)S(1)}, u32[]{:S(2)}, u32[]{:S(2)}) %collective-permute-start.25) | collective-permute-done | bytes 262176 | tf_op jit(solution)/shard_map/ppermute | solution.py:484
  (89 shorter events, 21.7 us)
Async XLA Ops:
  1.7 14.3 %collective-permute-start = (bf16[64,2048]{1,0:T(8,128)(2,1)S(1)}, bf16[64,2048]{1,0:T(8,128)(2,1)S(1)}, u32[]{:S(2)}, u32[]{:S(2)}) collective-permute-start(bf16[64,2048]{1,0:T(8,128)(2,1)S(1)} %slice_bitcast_fusion.2), channel_id=1, source_target_pairs={{0,16},{16,32},{32,48},{48,64},{64,80},{80,96},{96,112},{112,0},{1... | collective-permute-start | bytes 786440 | tf_op jit(solution)/shard_map/ppermute | solution.py:430
  6.3 7.9 %collective-permute-start.5 = (bf16[64,1024]{1,0:T(8,128)(2,1)}, bf16[64,1024]{1,0:T(8,128)(2,1)S(1)}, u32[]{:S(2)}, u32[]{:S(2)}) collective-permute-start(bf16[64,1024]{1,0:T(8,128)(2,1)} %get-tuple-element.23), channel_id=1, source_target_pairs={{0,2},{2,4},{4,6},{6,0},{1,3},{3,5},{5,7},{7,1},{8,10},{10,12},{12... | collective-permute-start | bytes 393224 | tf_op jit(solution)/shard_map/ppermute | solution.py:441
  8.0 17.6 %collective-permute-start.15 = (bf16[64,1280]{1,0:T(8,128)(2,1)}, bf16[64,1280]{1,0:T(8,128)(2,1)S(1)}, u32[]{:S(2)}, u32[]{:S(2)}) collective-permute-start(bf16[64,1280]{1,0:T(8,128)(2,1)} %get-tuple-element.27), channel_id=1, source_target_pairs={{0,2},{2,4},{4,6},{6,0},{1,3},{3,5},{5,7},{7,1},{8,10},{10,12},{12... | collective-permute-start | bytes 491528 | tf_op jit(solution)/shard_map/ppermute | solution.py:438
  9.5 19.3 %collective-permute-start.16 = (bf16[64,1280]{1,0:T(8,128)(2,1)}, bf16[64,1280]{1,0:T(8,128)(2,1)S(1)}, u32[]{:S(2)}, u32[]{:S(2)}) collective-permute-start(bf16[64,1280]{1,0:T(8,128)(2,1)} %get-tuple-element.28), channel_id=1, source_target_pairs={{2,0},{4,2},{6,4},{0,6},{3,1},{5,3},{7,5},{1,7},{10,8},{12,10},{14... | collective-permute-start | bytes 491528 | tf_op jit(solution)/shard_map/ppermute | solution.py:439
  11.2 21.3 %collective-permute-start.17 = (bf16[64,1280]{1,0:T(8,128)(2,1)}, bf16[64,1280]{1,0:T(8,128)(2,1)S(1)}, u32[]{:S(2)}, u32[]{:S(2)}) collective-permute-start(bf16[64,1280]{1,0:T(8,128)(2,1)} %get-tuple-element.29), channel_id=1, source_target_pairs={{0,4},{2,6},{4,0},{6,2},{1,5},{3,7},{5,1},{7,3},{8,12},{10,14},{12... | collective-permute-start | bytes 491528 | tf_op jit(solution)/shard_map/ppermute | solution.py:440
  14.2 9.1 %collective-permute-start.6 = (bf16[64,1024]{1,0:T(8,128)(2,1)}, bf16[64,1024]{1,0:T(8,128)(2,1)S(1)}, u32[]{:S(2)}, u32[]{:S(2)}) collective-permute-start(bf16[64,1024]{1,0:T(8,128)(2,1)} %get-tuple-element.24), channel_id=1, source_target_pairs={{2,0},{4,2},{6,4},{0,6},{3,1},{5,3},{7,5},{1,7},{10,8},{12,10},{14... | collective-permute-start | bytes 393224 | tf_op jit(solution)/shard_map/ppermute | solution.py:442
  16.0 9.5 %collective-permute-start.7 = (bf16[64,1024]{1,0:T(8,128)(2,1)}, bf16[64,1024]{1,0:T(8,128)(2,1)S(1)}, u32[]{:S(2)}, u32[]{:S(2)}) collective-permute-start(bf16[64,1024]{1,0:T(8,128)(2,1)} %get-tuple-element.25), channel_id=1, source_target_pairs={{0,4},{2,6},{4,0},{6,2},{1,5},{3,7},{5,1},{7,3},{8,12},{10,14},{12... | collective-permute-start | bytes 393224 | tf_op jit(solution)/shard_map/ppermute | solution.py:443
  23.3 10.9 %collective-permute-start.11 = (bf16[64,2048]{1,0:T(8,128)(2,1)}, bf16[64,2048]{1,0:T(8,128)(2,1)S(1)}, u32[]{:S(2)}, u32[]{:S(2)}) collective-permute-start(bf16[64,2048]{1,0:T(8,128)(2,1)} %own.3), channel_id=1, source_target_pairs={{0,2},{2,4},{4,6},{6,0},{1,3},{3,5},{5,7},{7,1},{8,10},{10,12},{12... | collective-permute-start | bytes 786440 | tf_op jit(solution)/shard_map/ppermute | solution.py:431
  25.5 16.3 %collective-permute-start.1 = (bf16[2,64,2048]{2,1,0:T(8,128)(2,1)S(1)}, bf16[2,64,2048]{2,1,0:T(8,128)(2,1)S(1)}, u32[]{:S(2)}, u32[]{:S(2)}) collective-permute-start(bf16[2,64,2048]{2,1,0:T(8,128)(2,1)S(1)} %pad_maximum_fusion.1.a_own), channel_id=1, source_target_pairs={{0,2},{2,4},{4,6},{6,0},{1,3},{3,5},{5,7},{7,1},{8,10},{10,12},{12... | collective-permute-start | bytes 1572872 | tf_op jit(solution)/shard_map/ppermute | solution.py:461
  25.6 10.3 %collective-permute-start.12 = (bf16[64,2048]{1,0:T(8,128)(2,1)}, bf16[64,2048]{1,0:T(8,128)(2,1)S(1)}, u32[]{:S(2)}, u32[]{:S(2)}) collective-permute-start(bf16[64,2048]{1,0:T(8,128)(2,1)} %own.3), channel_id=1, source_target_pairs={{2,0},{4,2},{6,4},{0,6},{3,1},{5,3},{7,5},{1,7},{10,8},{12,10},{14... | collective-permute-start | bytes 786440 | tf_op jit(solution)/shard_map/ppermute | solution.py:432
  28.9 19.1 %collective-permute-start.8 = (bf16[4,64,1024]{2,1,0:T(8,128)(2,1)S(1)}, bf16[4,64,1024]{2,1,0:T(8,128)(2,1)}, u32[]{:S(2)}, u32[]{:S(2)}) collective-permute-start(bf16[4,64,1024]{2,1,0:T(8,128)(2,1)S(1)} %pad_maximum_fusion.2.p0), channel_id=1, source_target_pairs={{0,8},{8,0},{1,9},{9,1},{2,10},{10,2},{3,11},{11,3},{4,12},{12,4},... | collective-permute-start | bytes 1572872 | tf_op jit(solution)/shard_map/ppermute | solution.py:457
  32.6 16.5 %collective-permute-start.2 = (bf16[2,64,2048]{2,1,0:T(8,128)(2,1)S(1)}, bf16[2,64,2048]{2,1,0:T(8,128)(2,1)S(1)}, u32[]{:S(2)}, u32[]{:S(2)}) collective-permute-start(bf16[2,64,2048]{2,1,0:T(8,128)(2,1)S(1)} %pad_maximum_fusion.1.a_own), channel_id=1, source_target_pairs={{2,0},{4,2},{6,4},{0,6},{3,1},{5,3},{7,5},{1,7},{10,8},{12,10},{14... | collective-permute-start | bytes 1572872 | tf_op jit(solution)/shard_map/ppermute | solution.py:462
  34.2 32.7 %collective-permute-start.9 = (bf16[4,64,1024]{2,1,0:T(8,128)(2,1)S(1)}, bf16[4,64,1024]{2,1,0:T(8,128)(2,1)}, u32[]{:S(2)}, u32[]{:S(2)}) collective-permute-start(bf16[4,64,1024]{2,1,0:T(8,128)(2,1)S(1)} %pad_maximum_fusion.2.p0), channel_id=1, source_target_pairs={{0,1},{1,0},{2,3},{3,2},{4,5},{5,4},{6,7},{7,6},{8,9},{9,8},{10,11... | collective-permute-start | bytes 1572872 | tf_op jit(solution)/shard_map/ppermute | solution.py:458
  35.9 14.2 %collective-permute-start.18 = (bf16[5,64,512]{2,1,0:T(8,128)(2,1)S(1)}, bf16[5,64,512]{2,1,0:T(8,128)(2,1)}, u32[]{:S(2)}, u32[]{:S(2)}) collective-permute-start(bf16[5,64,512]{2,1,0:T(8,128)(2,1)S(1)} %pad_maximum_fusion.3.b0), channel_id=1, source_target_pairs={{0,8},{8,0},{1,9},{9,1},{2,10},{10,2},{3,11},{11,3},{4,12},{12,4},... | collective-permute-start | bytes 983048 | tf_op jit(solution)/shard_map/ppermute | solution.py:449
  49.1 17.8 %collective-permute-start.10 = (bf16[4,64,1024]{2,1,0:T(8,128)(2,1)}, bf16[4,64,1024]{2,1,0:T(8,128)(2,1)}, u32[]{:S(2)}, u32[]{:S(2)}) collective-permute-start(bf16[4,64,1024]{2,1,0:T(8,128)(2,1)} %collective-permute-done.8.p1), channel_id=1, source_target_pairs={{0,1},{1,0},{2,3},{3,2},{4,5},{5,4},{6,7},{7,6},{8,9},{9,8},{10,11... | collective-permute-start | bytes 1572872 | tf_op jit(solution)/shard_map/ppermute | solution.py:459
  50.1 9.5 %collective-permute-start.20 = (bf16[5,64,512]{2,1,0:T(8,128)(2,1)}, bf16[5,64,512]{2,1,0:T(8,128)(2,1)}, u32[]{:S(2)}, u32[]{:S(2)}) collective-permute-start(bf16[5,64,512]{2,1,0:T(8,128)(2,1)} %collective-permute-done.18.b1), channel_id=1, source_target_pairs={{0,1},{1,0},{2,3},{3,2},{4,5},{5,4},{6,7},{7,6},{8,9},{9,8},{10,11... | collective-permute-start | bytes 983048 | tf_op jit(solution)/shard_map/ppermute | solution.py:451
  54.5 12.4 %collective-permute-start.3 = (bf16[64,2048]{1,0:T(8,128)(2,1)}, bf16[64,2048]{1,0:T(8,128)(2,1)}, u32[]{:S(2)}, u32[]{:S(2)}) collective-permute-start(bf16[64,2048]{1,0:T(8,128)(2,1)} %slice_bitcast_fusion.1), channel_id=1, source_target_pairs={{0,2},{2,4},{4,6},{6,0},{1,3},{3,5},{5,7},{7,1},{8,10},{10,12},{12... | collective-permute-start | bytes 786440 | tf_op jit(solution)/shard_map/ppermute | solution.py:465
  55.2 11.7 %collective-permute-start.4 = (bf16[64,2048]{1,0:T(8,128)(2,1)}, bf16[64,2048]{1,0:T(8,128)(2,1)}, u32[]{:S(2)}, u32[]{:S(2)}) collective-permute-start(bf16[64,2048]{1,0:T(8,128)(2,1)} %slice_bitcast_fusion), channel_id=1, source_target_pairs={{2,0},{4,2},{6,4},{0,6},{3,1},{5,3},{7,5},{1,7},{10,8},{12,10},{14... | collective-permute-start | bytes 786440 | tf_op jit(solution)/shard_map/ppermute | solution.py:466
  74.8 11.2 %collective-permute-start.22 = (bf16[64,2304]{1,0:T(8,128)(2,1)}, bf16[64,2304]{1,0:T(8,128)(2,1)S(1)}, u32[]{:S(2)}, u32[]{:S(2)}) collective-permute-start(bf16[64,2304]{1,0:T(8,128)(2,1)} %get-tuple-element.36), channel_id=1, source_target_pairs={{2,0},{4,2},{6,4},{0,6},{3,1},{5,3},{7,5},{1,7},{10,8},{12,10},{14... | collective-permute-start | bytes 884744 | tf_op jit(solution)/shard_map/ppermute | solution.py:475
  76.1 20.8 %collective-permute-start.23 = (bf16[64,2304]{1,0:T(8,128)(2,1)}, bf16[64,2304]{1,0:T(8,128)(2,1)S(1)}, u32[]{:S(2)}, u32[]{:S(2)}) collective-permute-start(bf16[64,2304]{1,0:T(8,128)(2,1)} %get-tuple-element.37), channel_id=1, source_target_pairs={{0,2},{2,4},{4,6},{6,0},{1,3},{3,5},{5,7},{7,1},{8,10},{10,12},{12... | collective-permute-start | bytes 884744 | tf_op jit(solution)/shard_map/ppermute | solution.py:476
  76.9 19.9 %collective-permute-start.24 = (bf16[64,2304]{1,0:T(8,128)(2,1)}, bf16[64,2304]{1,0:T(8,128)(2,1)S(1)}, u32[]{:S(2)}, u32[]{:S(2)}) collective-permute-start(bf16[64,2304]{1,0:T(8,128)(2,1)} %get-tuple-element.38), channel_id=1, source_target_pairs={{0,4},{2,6},{4,0},{6,2},{1,5},{3,7},{5,1},{7,3},{8,12},{10,14},{12... | collective-permute-start | bytes 884744 | tf_op jit(solution)/shard_map/ppermute | solution.py:477
  78.6 24.1 %all-to-all-start = ((bf16[8,72,512]{2,1,0:T(8,128)(2,1)}), bf16[8,72,512]{2,1,0:T(8,128)(2,1)S(1)}, u32[]{:S(2)}, u32[]{:S(2)}) async-start(bf16[8,72,512]{2,1,0:T(8,128)(2,1)} %add_convert_fusion), calls=%async_computation | async-start | bytes 1179648 | tf_op jit(solution)/shard_map/all_to_all | solution.py:426
  103.5 17.8 %all-to-all-start.1 = ((bf16[8,64,512]{2,1,0:T(8,128)(2,1)}), bf16[8,64,512]{2,1,0:T(8,128)(2,1)S(1)}, u32[]{:S(2)}, u32[]{:S(2)}) async-start(bf16[8,64,512]{2,1,0:T(8,128)(2,1)} %finish.1), calls=%async_computation.1 | async-start | bytes 1048576 | tf_op jit(solution)/shard_map/all_to_all | solution.py:426
  107.1 12.9 %collective-permute-start.25 = (bf16[64,2048]{1,0:T(8,128)(2,1)S(1)}, bf16[64,2048]{1,0:T(8,128)(2,1)S(1)}, u32[]{:S(2)}, u32[]{:S(2)}) collective-permute-start(bf16[64,2048]{1,0:T(8,128)(2,1)S(1)} %fusion), channel_id=1, source_target_pairs={{16,0},{32,16},{48,32},{64,48},{80,64},{96,80},{112,96},{0,112},{1... | collective-permute-start | bytes 786440 | tf_op jit(solution)/shard_map/ppermute | solution.py:484
  (18 other events, 174.4 us)
